TPU v7x, 32 devices: a whole 2x2x4 slice. The times are simulated.
32 devices in a mesh: shift: 2 (over y), space: 4 (over z), orb: 2 (over x), grid: 2 (over core).
Axes of the slice: x: 2, y: 2, z: 4, core: 2. Of those that a mesh axis runs over, the one named last changes fastest.
Arguments:
- support: bfloat16 [128, 9, 15, 256], P(('shift', 'space', 'orb'), None, None, 'grid'), parts along dimension 0, may hold values from -0.75 to 0.75
- anchor: int32 [128], P(('shift', 'space', 'orb')), parts along dimension 0, may hold values from 0 to 63, as said below
- kernel: float32 [512, 9, 9], P(('shift', 'space', 'orb')), parts along dimension 0, may hold values from -2.1 to 2.1
- pair_owner: int32 [512], P(('shift', 'space', 'orb')), parts along dimension 0, may hold values from 0 to 63, as said below
- pair_partner: int32 [512], P(('shift', 'space', 'orb')), parts along dimension 0, may hold values from 0 to 63, as said below
- pair_live: int32 [512], P(('shift', 'space', 'orb')), parts along dimension 0, may hold values 0 or 1
- v_ext: float32 [128, 256], P(('shift', 'space'), 'grid'), parts along dimension 0, may hold values from -6 to 6
Outputs:
- density: float32 [128, 256], P(('shift', 'space'), 'grid'), parts along dimension 0
- hamiltonian: float32 [512, 9, 9], P(('shift', 'space', 'orb')), parts along dimension 0
There are 2 independent parts, one for each index of `shift`. A program takes and returns all parts, laid end to end along the dimension named above; each array names one. Nothing has to cross between parts.
Inputs may be any that keep to these rules, and one draw needn't show every extreme that they name: Atom a lies in spatial domain a // 16, and its box starts at a plane of that domain: anchor[a] // 16 = a // 16. The owner of slot p is one of the 8 atoms of block p // 32: pair_owner[p] // 8 = p // 32. `pair_partner`: the partner of a slot lies in its owner's spatial domain or in one of the two adjacent domains, counted periodically, and its box shares at least one plane with the owner's box: |gap| <= 14.
All inputs are finite; a program needn't handle non-finite values. No bound on the sum of `pair_live` on one device may be relied on, other than what follows from the above.
Results may differ from a plain program's by a relative error of at most 0.0028.
Values may be sent and summed in bfloat16 or wider, within the bound.
No kernel may reach another device: no remote copies, remote signals or barrier semaphores. Data moves between devices by JAX's collectives and lax.ppermute only.
A program may use at most 64 MiB of HBM per device.

v0:
```python
import jax
import jax.numpy as jnp
from jax import lax
from jax.sharding import PartitionSpec as P


def shifted(value, axis, steps):
    count = lax.axis_size(axis)
    pairs = [(source, (source + steps) % count) for source in range(count)]
    return lax.ppermute(value, axis, pairs)


def shift_planes(rows, plane_gap, box_depth):
    index = jnp.arange(box_depth, dtype=jnp.int32)[None, :] + plane_gap[:, None]
    inside = (index >= 0) & (index < box_depth)
    picked = jnp.take_along_axis(rows, jnp.clip(index, 0, box_depth - 1)[:, None, :, None], axis=2)
    return jnp.where(inside[:, None, :, None], picked, jnp.zeros_like(picked))


def respond(field):
    return field / jnp.sqrt(1.0 + field * field)


def on_device(support, anchor, kernel, pair_owner, pair_partner, pair_live, v_ext):
    per_device, functions, box_depth, points = support.shape
    pair_count = kernel.shape[0]
    slab_rows = v_ext.shape[0]
    orb_count = lax.axis_size("orb")
    space_count = lax.axis_size("space")
    per_domain = per_device * orb_count
    total_planes = slab_rows * space_count
    domain = lax.axis_index("space")
    orb_index = lax.axis_index("orb")
    own_block = domain * orb_count + orb_index
    below_support, below_anchor = shifted((support, anchor), "space", 1)
    above_support, above_anchor = shifted((support, anchor), "space", -1)
    lower_support, domain_support, upper_support, lower_anchor, domain_anchor, upper_anchor = (
        lax.all_gather(below_support, "orb", axis=0, tiled=True),
        lax.all_gather(support, "orb", axis=0, tiled=True),
        lax.all_gather(above_support, "orb", axis=0, tiled=True),
        lax.all_gather(below_anchor, "orb", axis=0, tiled=True),
        lax.all_gather(anchor, "orb", axis=0, tiled=True),
        lax.all_gather(above_anchor, "orb", axis=0, tiled=True),
    )
    window_support = jnp.concatenate([lower_support, domain_support, upper_support], axis=0)
    window_anchor = jnp.concatenate([lower_anchor, domain_anchor, upper_anchor], axis=0)
    partner_domain = pair_partner // per_domain
    relative = (partner_domain - domain + 1 + space_count) % space_count
    window_index = relative * per_domain + pair_partner % per_domain
    owner_local = pair_owner - own_block * per_device
    plane_gap = (
        (anchor[owner_local] - window_anchor[window_index] + total_planes // 2) % total_planes
        - total_planes // 2
    ).astype(jnp.int32)
    alive = pair_live.astype(jnp.float32)
    block_count = pair_count // pair_count
    index_blocks = window_index.reshape(block_count, pair_count)
    gap_blocks = plane_gap.reshape(block_count, pair_count)
    owner_blocks = owner_local.reshape(block_count, pair_count)
    kernel_blocks = (kernel * alive[:, None, None]).reshape(
        block_count, pair_count, functions, functions
    )
    atom_ids = jnp.arange(per_device, dtype=jnp.int32)

    def aux_step(total, items):
        rows_index, gaps, kern, owners = items
        moved = shift_planes(window_support[rows_index], gaps, box_depth)
        terms = jnp.einsum(
            "pst,ptjq->psjq", kern, moved.astype(jnp.float32), precision=lax.Precision.HIGHEST
        )
        table = (owners[None, :] == atom_ids[:, None]).astype(jnp.float32)
        return (
            total + jnp.einsum("ap,psjq->asjq", table, terms, precision=lax.Precision.HIGHEST),
            None,
        )

    start_aux = jnp.zeros((per_device, functions, box_depth, points), jnp.float32)
    aux, _ = lax.scan(aux_step, start_aux, (index_blocks, gap_blocks, kernel_blocks, owner_blocks))
    deposit_terms = jnp.sum(support.astype(jnp.float32) * aux, axis=1)
    offset = anchor - domain * slab_rows
    local_plane = offset[:, None] + jnp.arange(box_depth, dtype=jnp.int32)[None, :]
    placing = (
        jnp.arange(2 * slab_rows, dtype=jnp.int32)[:, None, None] == local_plane[None, :, :]
    ).astype(jnp.float32)
    deposit = jnp.einsum("zaj,ajq->zq", placing, deposit_terms, precision=lax.Precision.HIGHEST)
    summed = lax.psum(deposit, "orb")
    incoming = shifted(summed[slab_rows:], "space", 1)
    density = summed[:slab_rows] + incoming
    potential = v_ext + respond(density)
    next_potential = shifted(potential, "space", -1)
    both_slabs = jnp.concatenate([potential, next_potential], axis=0)
    box_potential = jnp.einsum("zaj,zq->ajq", placing, both_slabs, precision=lax.Precision.HIGHEST)
    weighted = (support.astype(jnp.float32) * box_potential[:, None, :, :]).astype(jnp.bfloat16)

    def ham_block(items):
        rows_index, gaps, owners = items
        moved = shift_planes(window_support[rows_index], gaps, box_depth)
        owner_rows = weighted[owners]
        return jnp.einsum("psjq,ptjq->pst", owner_rows, moved, preferred_element_type=jnp.float32)

    partial_blocks = lax.map(ham_block, (index_blocks, gap_blocks, owner_blocks)).reshape(
        pair_count, functions, functions
    )
    hamiltonian = lax.psum(partial_blocks, "grid") * alive[:, None, None]
    return (density, hamiltonian)


def solution(mesh):
    placed = (
        P(("shift", "space", "orb"), None, None, "grid"),
        P(("shift", "space", "orb")),
        P(("shift", "space", "orb"), None, None),
        P(("shift", "space", "orb")),
        P(("shift", "space", "orb")),
        P(("shift", "space", "orb")),
        P(("shift", "space"), "grid"),
    )
    return jax.shard_map(
        on_device,
        mesh=mesh,
        in_specs=placed,
        out_specs=(P(("shift", "space"), "grid"), P(("shift", "space", "orb"), None, None)),
        check_vma=False,
    )
```

profile of v0, /device:TPU:0, one launch (start us, length us, event | category | flops | bytes accessed | tf_op | source)
XLA Modules:
  0.0 81.6 jit_solution(5677399734707426305)
XLA Ops:
  0.6 0.0 copy-start.5
  0.7 3.1 %collective-permute-start = (s32[8]{0:T(128)}, s32[8]{0:T(128)S(1)}, u32[]{:S(2)}, u32[]{:S(2)}) collective-permute-start(s32[8]{0:T(128)} %param.10), channel_id=1, source_target_pairs={{0,4},{4,8},{8,12},{12,0},{1,5},{5,9},{9,13},{13,1},{2,6},{6,10},{... | collective-permute-start | bytes 104 | tf_op jit(solution)/shard_map/ppermute | solution.py:10
  3.8 2.1 %collective-permute-start.1 = (s32[8]{0:T(128)}, s32[8]{0:T(128)S(1)}, u32[]{:S(2)}, u32[]{:S(2)}) collective-permute-start(s32[8]{0:T(128)} %param.10), channel_id=1, source_target_pairs={{0,12},{4,0},{8,4},{12,8},{1,13},{5,1},{9,5},{13,9},{2,14},{6,2},{... | collective-permute-start | bytes 104 | tf_op jit(solution)/shard_map/ppermute | solution.py:10
  5.9 3.8 %collective-permute-start.3 = (bf16[8,9,15,128]{3,0,2,1:T(8,128)(2,1)}, bf16[8,9,15,128]{3,0,2,1:T(8,128)(2,1)S(1)}, u32[]{:S(2)}, u32[]{:S(2)}) collective-permute-start(bf16[8,9,15,128]{3,0,2,1:T(8,128)(2,1)} %param.9), channel_id=1, source_target_pairs={{0,12},{4,0},{8,4},{12,8},{1,13},{5,1},{9,5},{13,9},{2,14},{6,2},{... | collective-permute-start | bytes 829448 | tf_op jit(solution)/shard_map/ppermute | solution.py:10
  9.7 8.4 %all_gather.22 = bf16[16,9,15,128]{3,0,2,1:T(8,128)(2,1)S(1)} all-gather(bf16[8,9,15,128]{3,0,2,1:T(8,128)(2,1)} %param.9), channel_id=1, replica_groups=mesh['shift'=2,'space'=4,'orb'=2,'grid'=2] {'orb'}, dimensions={0}, use_global_device_ids=true | all-gather | bytes 829440 | tf_op jit(solution)/shard_map/all_gather | solution.py:39
  18.1 0.7 compare_select_fusion.1
  18.8 0.7 compare_select_fusion.2
  19.5 1.4 %gather_fusion = s32[32]{0:T(128)S(1)} fusion(s32[8]{0:T(128)} %param.10, s32[1024]{0:T(1024)S(1)} %pad_clamp_fusion.1), kind=kCustom, calls=%fused_computation.1 | custom fusion | bytes 384 | tf_op jit(solution)/shard_map/gather | solution.py:52
  20.8 0.2 copy.38
  21.0 0.2 copy.36
  21.2 0.1 iota_add_fusion.1
  21.3 0.6 dynamic-slice.4
  22.6 0.2 dynamic-update-slice.1
  22.8 0.2 dynamic-update-slice
  23.1 0.2 dynamic-update-slice.2
  23.3 4.3 %all-reduce.3 = (s32[16]{0:T(128)S(1)}, s32[16]{0:T(128)S(1)}, s32[16]{0:T(128)S(1)}) all-reduce(s32[16]{0:T(128)S(1)} %dynamic-update-slice.2, s32[16]{0:T(128)S(1)} %dynamic-update-slice.1, s32[16]{0:T(128)S(1)} %dynamic-update-slice), channel_id=1, replica_groups=mesh['shift'=2,'space'=4,'orb'=2,'grid'=2] {'orb'}, use_global_device_ids=true, to_apply=%add.2 | all-reduce | flops 48 | bytes 384
  27.5 0.1 pad_add_fusion
  27.6 0.7 gather_fusion.1
  28.3 0.1 bitcast_or_fusion
  28.4 0.1 fusion.32
  28.5 0.1 reshape.174
  28.6 0.1 fusion.33
  28.7 8.0 %all_gather.21 = bf16[16,9,15,128]{3,0,2,1:T(8,128)(2,1)S(1)} all-gather(bf16[8,9,15,128]{3,0,2,1:T(8,128)(2,1)S(1)} %collective-permute-done.2), channel_id=1, replica_groups=mesh['shift'=2,'space'=4,'orb'=2,'grid'=2] {'orb'}, dimensions={0}, use_global_device_ids=true | all-gather | bytes 829440 | tf_op jit(solution)/shard_map/all_gather | solution.py:38
  36.7 0.2 copy.37
  36.8 7.2 %all_gather.23 = bf16[16,9,15,128]{3,0,2,1:T(8,128)(2,1)S(1)} all-gather(bf16[8,9,15,128]{3,0,2,1:T(8,128)(2,1)S(1)} %collective-permute-done.3), channel_id=1, replica_groups=mesh['shift'=2,'space'=4,'orb'=2,'grid'=2] {'orb'}, dimensions={0}, use_global_device_ids=true | all-gather | bytes 829440 | tf_op jit(solution)/shard_map/all_gather | solution.py:40
  44.0 0.2 copy.39
  44.2 0.3 pad_maximum_fusion
  44.5 0.8 gather_fusion.2
  45.3 1.8 %copy.40 = bf16[32,9,15,128]{3,1,2,0:T(8,128)(2,1)} copy(bf16[32,9,15,128]{3,2,1,0:T(8,128)(2,1)S(1)} %gather_fusion.2) | data formatting | bytes 2211840 | tf_op jit(solution)/shard_map/while/body/eval_jaxpr/gather | solution.py:67
  47.1 5.2 %gather_fusion.4 = bf16[480,9,128]{2,1,0:T(8,128)(2,1)S(1)} fusion(bf16[32,9,15,128]{3,1,2,0:T(8,128)(2,1)} %copy.40, s32[480]{0:T(512)S(1)} %reshape.174), kind=kCustom, calls=%fused_computation.clone | custom fusion | bytes 2215680 | tf_op jit(solution)/shard_map/while/body/eval_jaxpr/jit(take_along_axis)/gather | solution.py:16
  52.3 0.3 bitcast_select_fusion
  52.7 2.1 %fusion.4 = f32[32,9,15,128]{3,1,2,0:T(8,128)S(1)} fusion(bf16[32,9,15,128]{3,2,0,1:T(8,128)(2,1)S(1)} %bitcast_select_fusion, f32[32,9,9]{2,1,0:T(8,128)S(1)} %copy.36, f32[32]{0:T(128)S(1)} %convert_element_type.16), kind=kOutput, calls=%fused_computation.9 | convolution fusion | flops 59722272 | bytes 3328256 | tf_op jit(solution)/shard_map/while/body/eval_jaxpr/pst,ptjq->psjq/dot_general | solution.py:68
  54.8 1.5 %fusion.10 = f32[8,15,128]{2,0,1:T(8,128)S(1)} fusion(f32[32,9,15,128]{3,1,2,0:T(8,128)S(1)} %fusion.4, bf16[8,9,15,128]{3,0,2,1:T(8,128)(2,1)S(1)} %copy-done.1, s32[32]{0:T(128)S(1)} %get-tuple-element.62), kind=kOutput, calls=%fused_computation.14 | convolution fusion | flops 53483776 | bytes 2549888 | tf_op jit(solution)/shard_map/while/body/eval_jaxpr/ap,psjq->asjq/dot_general | solution.py:73
  56.3 0.3 convolution_bitcast_fusion
  56.6 8.3 %psum.14 = f32[32,128]{1,0:T(8,128)S(1)} all-reduce(f32[32,128]{1,0:T(8,128)S(1)} %convolution_bitcast_fusion), channel_id=1, replica_groups=mesh['shift'=2,'space'=4,'orb'=2,'grid'=2] {'orb'}, use_global_device_ids=true, to_apply=%region_1.3 | all-reduce | flops 4096 | bytes 32768 | tf_op jit(solution)/shard_map/psum | solution.py:86
  64.9 0.0 collective-permute-start.4
  64.9 5.4 %collective-permute-done.4 = f32[16,128]{1,0:T(8,128)S(1)} collective-permute-done((f32[16,128]{1,0:T(8,128)S(1)}, f32[16,128]{1,0:T(8,128)S(1)}, u32[]{:S(2)}, u32[]{:S(2)}) %collective-permute-start.4) | collective-permute-done | bytes 8224 | tf_op jit(solution)/shard_map/ppermute | solution.py:10
  70.4 0.6 multiply_add_fusion
  71.0 0.1 iota_compare_fusion
  71.1 3.6 %collective-permute-done.5 = f32[16,128]{1,0:T(8,128)S(1)} collective-permute-done((f32[16,128]{1,0:T(8,128)S(1)}, f32[16,128]{1,0:T(8,128)S(1)}, u32[]{:S(2)}, u32[]{:S(2)}) %collective-permute-start.5) | collective-permute-done | bytes 8224 | tf_op jit(solution)/shard_map/ppermute | solution.py:10
  74.6 0.2 fusion.23
  74.8 0.1 fusion.18
  74.9 0.1 copy.46
  75.0 0.8 gather_fusion.3
  75.7 1.0 %fusion.13 = f32[32,9,9]{2,1,0:T(8,128)S(1)} fusion(bf16[32,9,15,128]{3,2,0,1:T(8,128)(2,1)S(1)} %bitcast_select_fusion, bf16[32,9,15,128]{3,2,1,0:T(8,128)(2,1)S(1)} %gather_fusion.3), kind=kOutput, calls=%fused_computation.17 | convolution fusion | flops 9953280 | bytes 2222208 | tf_op jit(solution)/shard_map/while/body/eval_jaxpr/psjq,ptjq->pst/dot_general | solution.py:99
  76.7 4.0 %psum.15 = f32[32,9,9]{2,1,0:T(8,128)S(1)} all-reduce(f32[32,9,9]{2,1,0:T(8,128)S(1)} %fusion.13), channel_id=1, replica_groups=mesh['shift'=2,'space'=4,'orb'=2,'grid'=2] {'grid'}, use_global_device_ids=true, to_apply=%region_2.4 | all-reduce | flops 2592 | bytes 20736 | tf_op jit(solution)/shard_map/psum | solution.py:104
  80.7 0.1 broadcast_multiply_fusion
  80.8 0.8 copy.49
  (26 shorter events, 0.1 us)
Async XLA Ops:
  0.6 20.7 %copy-start.5 = (u32[32]{0:T(128)S(1)}, u32[32]{0:T(128)}, u32[]{:S(2)}) copy-start(u32[32]{0:T(128)} %constant.154) | copy-start | bytes 388
  0.6 20.6 %copy-start = (s32[8]{0:T(128)S(1)}, s32[8]{0:T(128)}, u32[]{:S(2)}) copy-start(s32[8]{0:T(128)} %param.10) | copy-start | bytes 100
  0.7 20.3 %copy-start.4 = (s32[32]{0:T(128)S(1)}, s32[32]{0:T(128)}, u32[]{:S(2)}) copy-start(s32[32]{0:T(128)} %param.14) | copy-start | bytes 388
  0.7 20.4 %copy-start.2 = (f32[32,9,9]{0,2,1:T(8,128)S(1)}, f32[32,9,9]{0,2,1:T(8,128)}, u32[]{:S(2)}) copy-start(f32[32,9,9]{0,2,1:T(8,128)} %param.11) | copy-start | bytes 31108
  0.7 22.1 %collective-permute-start = (s32[8]{0:T(128)}, s32[8]{0:T(128)S(1)}, u32[]{:S(2)}, u32[]{:S(2)}) collective-permute-start(s32[8]{0:T(128)} %param.10), channel_id=1, source_target_pairs={{0,4},{4,8},{8,12},{12,0},{1,5},{5,9},{9,13},{13,1},{2,6},{6,10},{... | collective-permute-start | bytes 104 | tf_op jit(solution)/shard_map/ppermute | solution.py:10
  3.8 19.3 %collective-permute-start.1 = (s32[8]{0:T(128)}, s32[8]{0:T(128)S(1)}, u32[]{:S(2)}, u32[]{:S(2)}) collective-permute-start(s32[8]{0:T(128)} %param.10), channel_id=1, source_target_pairs={{0,12},{4,0},{8,4},{12,8},{1,13},{5,1},{9,5},{13,9},{2,14},{6,2},{... | collective-permute-start | bytes 104 | tf_op jit(solution)/shard_map/ppermute | solution.py:10
  5.9 22.8 %collective-permute-start.2 = (bf16[8,9,15,128]{3,0,2,1:T(8,128)(2,1)}, bf16[8,9,15,128]{3,0,2,1:T(8,128)(2,1)S(1)}, u32[]{:S(2)}, u32[]{:S(2)}) collective-permute-start(bf16[8,9,15,128]{3,0,2,1:T(8,128)(2,1)} %param.9), channel_id=1, source_target_pairs={{0,4},{4,8},{8,12},{12,0},{1,5},{5,9},{9,13},{13,1},{2,6},{6,10},{... | collective-permute-start | bytes 829448 | tf_op jit(solution)/shard_map/ppermute | solution.py:10
  5.9 30.9 %collective-permute-start.3 = (bf16[8,9,15,128]{3,0,2,1:T(8,128)(2,1)}, bf16[8,9,15,128]{3,0,2,1:T(8,128)(2,1)S(1)}, u32[]{:S(2)}, u32[]{:S(2)}) collective-permute-start(bf16[8,9,15,128]{3,0,2,1:T(8,128)(2,1)} %param.9), channel_id=1, source_target_pairs={{0,12},{4,0},{8,4},{12,8},{1,13},{5,1},{9,5},{13,9},{2,14},{6,2},{... | collective-permute-start | bytes 829448 | tf_op jit(solution)/shard_map/ppermute | solution.py:10
  52.7 2.1 %copy-start.1 = (bf16[8,9,15,128]{3,0,2,1:T(8,128)(2,1)S(1)}, bf16[8,9,15,128]{3,0,2,1:T(8,128)(2,1)}, u32[]{:S(2)}) copy-start(bf16[8,9,15,128]{3,0,2,1:T(8,128)(2,1)} %param.9) | copy-start | bytes 829444
  54.7 15.6 %copy-start.3 = (f32[16,128]{1,0:T(8,128)S(1)}, f32[16,128]{1,0:T(8,128)}, u32[]{:S(2)}) copy-start(f32[16,128]{1,0:T(8,128)} %param.15) | copy-start | bytes 24580
  64.9 5.5 %collective-permute-start.4 = (f32[16,128]{1,0:T(8,128)S(1)}, f32[16,128]{1,0:T(8,128)S(1)}, u32[]{:S(2)}, u32[]{:S(2)}) collective-permute-start(f32[16,128]{1,0:T(8,128)S(1)} %slice.19), channel_id=1, source_target_pairs={{0,4},{4,8},{8,12},{12,0},{1,5},{5,9},{9,13},{13,1},{2,6},{6,10},{... | collective-permute-start | bytes 24584 | tf_op jit(solution)/shard_map/ppermute | solution.py:10
  71.0 3.7 %collective-permute-start.5 = (f32[16,128]{1,0:T(8,128)S(1)}, f32[16,128]{1,0:T(8,128)S(1)}, u32[]{:S(2)}, u32[]{:S(2)}) collective-permute-start(f32[16,128]{1,0:T(8,128)S(1)} %get-tuple-element.52), channel_id=1, source_target_pairs={{0,12},{4,0},{8,4},{12,8},{1,13},{5,1},{9,5},{13,9},{2,14},{6,2},{... | collective-permute-start | bytes 24584 | tf_op jit(solution)/shard_map/ppermute | solution.py:10
where the time goes:
time: 81.9 us; the launch traced here: 81.6 us
  blocking collectives  40.2 us (49%)
  local copies, waits for them, and re-layouts  13.5 us (16%)
  starting transfers between devices  9.06 us (11%)
  waiting for transfers between devices  9 us (11%)
  matrix products  5.05 us (6%)
  other arithmetic  3.28 us (4%)
  between operations  1.57 us (2%)
    ppermute x6, starting transfers between devices, shifted(): return lax.ppermute(value, axis, pairs)  9.06 us
    ppermute x6, waiting for transfers between devices, shifted(): return lax.ppermute(value, axis, pairs)  9 us
    all_gather x1, blocking collectives, on_device(): lax.all_gather(support, 'orb', axis=0, tiled=True)  8.41 us
    psum x1, blocking collectives, on_device(): summed = lax.psum(deposit, 'orb')  8.3 us
    all_gather x1, blocking collectives, on_device(): lax.all_gather(below_support, 'orb', axis=0, tiled=True)  7.96 us
    all_gather x1, blocking collectives, on_device(): lax.all_gather(above_support, 'orb', axis=0, tiled=True)  7.22 us
    gather x2, local copies, waits for them, and re-layouts, shift_planes(): jnp.take_along_axis(rows, jnp.clip(index, 0, box_depth - 1)[:, None, :, N...  5.32 us
    unnamed x1, blocking collectives  4.25 us
  transfers between devices with their start and end apart: 6, of which 2 were waited for; matrix products, arithmetic and copies ran while one was open for 7% of the time, Pallas kernels for 0%

commit v1 on v0

v1 whole, which is shorter than its diff:
```python
import functools

import jax
import jax.numpy as jnp
from jax import lax
from jax.experimental import pallas as pl
from jax.experimental.pallas import tpu as pltpu
from jax.sharding import PartitionSpec as P

LANES = 128
F32 = jnp.float32
BF16 = jnp.bfloat16


def moved_by(value, axes, steps):
    sizes = [lax.axis_size(axis) for axis in axes]
    pairs = []
    total = 1
    for size in sizes:
        total *= size
    for source in range(total):
        rest, place = source, []
        for size in reversed(sizes):
            place.insert(0, rest % size)
            rest //= size
        target = 0
        for size, here, step in zip(sizes, place, steps):
            target = target * size + (here + step) % size
        pairs.append((source, target))
    return lax.ppermute(value, axes if len(axes) > 1 else axes[0], pairs)


def round_up(count, unit):
    return (count + unit - 1) // unit * unit


def pack_kernel(dims, orb_ref, anchor_ref, x_ref, k_ref, owner_ref, live_ref, code_ref, *rest):
    atoms, functions, depth, points, slab, ways, reach, pairs = dims
    own_refs, next_refs = rest[:ways], rest[ways : 2 * ways]
    pair_ref, k_pad, row_pad = rest[2 * ways :]
    planes = slab // ways
    boxes = -(-depth // ways)
    orb = orb_ref[0]
    atom = lax.broadcasted_iota(jnp.int32, (atoms, points), 0)
    offset = jnp.zeros((atoms, points), jnp.int32)
    for a in range(atoms):
        offset = jnp.where(atom == a, lax.rem(anchor_ref[a], slab), offset)
    zero = jnp.zeros((atoms, points), F32)
    masks = []
    for k in range(ways):
        residue = lax.rem(orb + k, ways)
        start = offset - residue
        shift = jnp.zeros((atoms, points), jnp.int32)
        for low in range(slab // ways):
            shift = shift + (start > low * ways).astype(jnp.int32)
        phase = shift * ways - start
        bits, size = [], 1
        while size <= -(-(slab - 1) // ways):
            bits.append((size, (shift & size) != 0))
            size *= 2
        masks.append(([phase == e for e in range(ways)], bits))
    for s in range(functions):
        tiles = [x_ref[s, j].astype(F32) for j in range(depth)]
        for k in range(ways):
            phases, bits = masks[k]
            line = []
            for m in range(boxes):
                pick = zero
                for e in range(ways):
                    j = m * ways + e
                    pick = jnp.where(phases[e], tiles[j] if j < depth else zero, pick)
                line.append(pick)
            for size, mask in bits:
                length = min(len(line) + size, planes + reach)
                line = [
                    jnp.where(
                        mask,
                        line[h - size] if h >= size else zero,
                        line[h] if h < len(line) else zero,
                    )
                    for h in range(length)
                ]
            line = line + [zero] * (planes + reach - len(line))
            rows = pl.ds(s * atoms, atoms)
            for h in range(planes):
                own_refs[k][h, rows, :] = line[h].astype(BF16)
            for h in range(reach):
                next_refs[k][h, rows, :] = line[planes + h].astype(BF16)
    per = LANES // pairs
    groups = -(-functions // per)
    k_pad[...] = jnp.zeros_like(k_pad)
    k_pad[:, :functions, :pairs] = k_ref[...]
    pair_ref[...] = jnp.zeros_like(pair_ref)
    for s in range(functions):
        for g in range(groups):
            row = jnp.zeros((1, LANES), F32)
            for i in range(per):
                t = g * per + i
                if t < functions:
                    piece = k_pad[s, t : t + 1, :]
                    row = row + (pltpu.roll(piece, i * pairs, 1) if i else piece)
            pair_ref[s : s + 1, g * LANES : (g + 1) * LANES] = row
    row_pad[...] = jnp.zeros_like(row_pad)
    row_pad[0:1, :pairs] = owner_ref[...].astype(F32)
    row_pad[1:2, :pairs] = live_ref[...].astype(F32)
    row_pad[2:3, :pairs] = code_ref[...].astype(F32)
    index = row_pad[...]
    wide = index
    for i in range(1, per):
        wide = wide + pltpu.roll(index, i * pairs, 1)
    for g in range(groups):
        pair_ref[functions : functions + 3, g * LANES : (g + 1) * LANES] = wide[0:3]


def main_kernel(dims, orb_ref, v_ref, *rest):
    atoms, functions, depth, points, slab, ways, reach, pairs = dims
    planes = slab // ways
    sources = 2 * ways
    source_refs = rest[:sources]
    pair_refs = rest[sources : 2 * sources]
    own_out, low_out, f_ref, w_ref, d_ref, rt_ref, own_ref, h_ref = rest[2 * sources :]
    block = functions * atoms
    rows = sources * block
    padded = f_ref.shape[0]
    lanes = pair_refs[0].shape[1]
    orb = orb_ref[0]
    per_domain = atoms * ways
    for c in range(sources):
        count = source_refs[c].shape[0]
        for h in range(planes):
            place = (pl.ds(c * block, block), pl.ds(h * points, points))
            if h < count:
                f_ref[place] = source_refs[c][h]
            else:
                f_ref[place] = jnp.zeros((block, points), BF16)
    if padded > rows:
        f_ref[rows:, :] = jnp.zeros((padded - rows, planes * points), BF16)
    row_id = lax.broadcasted_iota(jnp.int32, (padded, lanes), 0)
    atom_id = lax.broadcasted_iota(jnp.int32, (atoms, lanes), 0)
    lane_id = lax.broadcasted_iota(jnp.int32, (1, lanes), 1)
    function_id = jnp.zeros((1, lanes), jnp.int32)
    for t in range(1, lanes // pairs):
        function_id = function_id + (lane_id >= t * pairs).astype(jnp.int32)
    for c in range(sources):
        info = pair_refs[c]
        owner = info[functions : functions + 1, :].astype(jnp.int32)
        live = info[functions + 1 : functions + 2, :]
        code = info[functions + 2 : functions + 3, :].astype(jnp.int32)
        domain = (code >= per_domain).astype(jnp.int32) + (code >= 2 * per_domain).astype(jnp.int32)
        inside = code - domain * per_domain
        orb_of = jnp.zeros((1, lanes), jnp.int32)
        for i in range(1, ways):
            orb_of = orb_of + (inside >= i * atoms).astype(jnp.int32)
        local = inside - orb_of * atoms
        slot = orb - orb_of
        slot = jnp.where(slot < 0, slot + ways, slot)
        if c < ways:
            slot = slot + jnp.where(domain == 0, ways, 0)
            valid = domain <= 1
        else:
            slot = slot + jnp.where(domain == 1, ways, 0)
            valid = domain >= 1
        valid = valid & (lane_id < functions * pairs)
        target = jnp.where(valid, slot * block + function_id * atoms + local, -1)
        table = jnp.where(row_id == target, 1.0, 0.0).astype(BF16)
        rt_ref[c] = table
        own = jnp.where(atom_id == owner, live, 0.0)
        own_ref[c] = own
        left = jnp.concatenate([info[s : s + 1, :] * own for s in range(functions)], axis=0)
        high = left.astype(BF16)
        low = (left - high.astype(F32)).astype(BF16)
        contract = (((1,), (1,)), ((), ()))
        part = lax.dot_general(high, table, contract, preferred_element_type=F32)
        part = part + lax.dot_general(low, table, contract, preferred_element_type=F32)
        high = part.astype(BF16)
        low = (part - high.astype(F32)).astype(BF16)
        d_ref[c * block : (c + 1) * block, :padded] = high
        d_ref[c * block : (c + 1) * block, padded:] = low
    f_all = f_ref[...]
    doubled = jnp.concatenate([f_all, f_all], axis=0)
    aux = jnp.dot(d_ref[...], doubled, preferred_element_type=F32)
    density = jnp.sum(aux * f_ref[:rows, :].astype(F32), axis=0, keepdims=True)
    v_ext = jnp.concatenate([v_ref[pl.ds(h * ways + orb, 1), :] for h in range(planes)], axis=1)
    potential = v_ext + density / jnp.sqrt(1.0 + density * density)
    w_ref[...] = (f_ref[:rows, :].astype(F32) * potential).astype(BF16)
    blocks = lax.dot_general(
        w_ref[...], f_all, (((1,), (1,)), ((), ())), preferred_element_type=F32
    )
    h_ref[...] = blocks
    own_out[...] = jnp.zeros_like(own_out)
    low_out[...] = jnp.zeros_like(low_out)
    for c in range(sources):
        part = h_ref[c * block : (c + 1) * block, :]
        high = part.astype(BF16)
        low = (part - high.astype(F32)).astype(BF16)
        table = rt_ref[c]
        spread = jnp.dot(high, table, preferred_element_type=F32)
        spread = spread + jnp.dot(low, table, preferred_element_type=F32)
        own = own_ref[c]
        picked = jnp.concatenate(
            [
                jnp.sum(spread[s * atoms : (s + 1) * atoms] * own, axis=0, keepdims=True)
                for s in range(functions)
            ],
            axis=0,
        )
        if c < ways:
            own_out[c, :functions, :] = picked
            for h in range(planes):
                own_out[c, 16 + h : 17 + h, :points] = density[:, h * points : (h + 1) * points]
        else:
            low_out[c - ways, :functions, :] = picked


def final_kernel(dims, orb_ref, mine_ref, other_ref, *rest):
    atoms, functions, depth, points, slab, ways, reach, pairs = dims
    planes = slab // ways
    message_refs = rest[:ways]
    density_ref, out_ref, pad_ref = rest[ways:]
    orb = orb_ref[0]
    for k in range(ways):
        residue = lax.rem(orb + k, ways)
        for h in range(planes):
            density_ref[pl.ds(h * ways + residue, 1), :] = message_refs[k][16 + h : 17 + h, :points]
    total = mine_ref[...] + other_ref[...]
    per = LANES // pairs
    for t in range(functions):
        g, i = t // per, t % per
        piece = total[:, g * LANES : (g + 1) * LANES]
        if i:
            piece = pltpu.roll(piece, LANES - i * pairs, 1)
        pad_ref[...] = piece
        for s in range(functions):
            out_ref[s, t : t + 1, :] = pad_ref[s : s + 1, :pairs]


def on_device(support, anchor, kernel, pair_owner, pair_partner, pair_live, v_ext):
    atoms, functions, depth, points = support.shape
    pairs = kernel.shape[0]
    slab = v_ext.shape[0]
    ways = lax.axis_size("orb")
    space = lax.axis_size("space")
    per_domain = atoms * ways
    planes = slab // ways
    reach = min((depth - 2) // ways + 1, planes)
    dims = (atoms, functions, depth, points, slab, ways, reach, pairs)
    domain = lax.axis_index("space")
    orb = lax.axis_index("orb")
    orb_row = jnp.reshape(orb, (1,)).astype(jnp.int32)
    block = functions * atoms
    lanes = round_up(functions * pairs, LANES)
    smem = pl.BlockSpec(memory_space=pltpu.SMEM)
    vmem = pl.BlockSpec(memory_space=pltpu.VMEM)

    relative = (pair_partner // per_domain - domain + 1 + space) % space
    code = (relative * per_domain + pair_partner % per_domain).reshape(1, pairs)
    owner = (pair_owner % atoms).reshape(1, pairs)
    live = pair_live.reshape(1, pairs)

    packed = pl.pallas_call(
        functools.partial(pack_kernel, dims),
        out_shape=[jax.ShapeDtypeStruct((planes, block, points), BF16)] * ways
        + [jax.ShapeDtypeStruct((reach, block, points), BF16)] * ways
        + [jax.ShapeDtypeStruct((16, lanes), F32)],
        in_specs=[smem, smem] + [vmem] * 5,
        out_specs=[vmem] * (2 * ways + 1),
        scratch_shapes=[pltpu.VMEM((functions, 16, LANES), F32), pltpu.VMEM((8, LANES), F32)],
        name="pack",
    )(
        orb_row,
        anchor,
        support.transpose(1, 2, 0, 3),
        kernel.transpose(1, 2, 0),
        owner,
        live,
        code,
    )
    own, onward, pair_rows = packed[:ways], packed[ways : 2 * ways], packed[2 * ways]
    sources, pair_sources = [own[0]], [pair_rows]
    for k in range(1, ways):
        sources.append(moved_by(own[k], ("orb",), (k,)))
        pair_sources.append(moved_by(pair_rows, ("orb",), (k,)))
    for k in range(ways):
        sources.append(moved_by(onward[k], ("space", "orb"), (1, k)))
        pair_sources.append(moved_by(pair_rows, ("space", "orb"), (1, k)))

    rows = 2 * ways * block
    padded = round_up(rows, LANES)
    own_part, low_part = pl.pallas_call(
        functools.partial(main_kernel, dims),
        out_shape=[
            jax.ShapeDtypeStruct((ways, 16 + round_up(planes, 8), lanes), F32),
            jax.ShapeDtypeStruct((ways, 16, lanes), F32),
        ],
        in_specs=[smem] + [vmem] * (1 + 4 * ways),
        out_specs=[vmem] * 2,
        scratch_shapes=[
            pltpu.VMEM((padded, planes * points), BF16),
            pltpu.VMEM((rows, planes * points), BF16),
            pltpu.VMEM((rows, 2 * padded), BF16),
            pltpu.VMEM((2 * ways, padded, lanes), BF16),
            pltpu.VMEM((2 * ways, atoms, lanes), F32),
            pltpu.VMEM((rows, padded), F32),
        ],
        name="main",
    )(orb_row, v_ext, *sources, *pair_sources)

    from_above = moved_by(low_part, ("space",), (-1,))
    total = own_part + jnp.pad(from_above, ((0, 0), (0, own_part.shape[1] - 16), (0, 0)))
    messages = [total[0]]
    mine = total[0, :16]
    for k in range(1, ways):
        message = moved_by(total[k], ("orb",), (-k,))
        messages.append(message)
        mine = mine + message[:16]
    other = mine
    shares = lax.axis_size("grid")
    other = moved_by(mine, ("grid",), (1,))
    for k in range(2, shares):
        other = other + moved_by(mine, ("grid",), (k,))
    density, blocks = pl.pallas_call(
        functools.partial(final_kernel, dims),
        out_shape=[
            jax.ShapeDtypeStruct((slab, points), F32),
            jax.ShapeDtypeStruct((functions, functions, pairs), F32),
        ],
        in_specs=[smem] + [vmem] * (2 + ways),
        out_specs=[vmem] * 2,
        scratch_shapes=[pltpu.VMEM((16, LANES), F32)],
        name="final",
    )(orb_row, mine, other, *messages)
    return (density, blocks.transpose(2, 0, 1))


def solution(mesh):
    placed = (
        P(("shift", "space", "orb"), None, None, "grid"),
        P(("shift", "space", "orb")),
        P(("shift", "space", "orb"), None, None),
        P(("shift", "space", "orb")),
        P(("shift", "space", "orb")),
        P(("shift", "space", "orb")),
        P(("shift", "space"), "grid"),
    )
    return jax.shard_map(
        on_device,
        mesh=mesh,
        in_specs=placed,
        out_specs=(P(("shift", "space"), "grid"), P(("shift", "space", "orb"), None, None)),
        check_vma=False,
    )
```

time: 81.9 us -> 40.1 us (0.49)
  blocking collectives: 40.2 us -> 0 us
  local copies, waits for them, and re-layouts: 13.5 us -> 3.21 us
  Pallas kernels: 0 us -> 7.84 us
  starting transfers between devices: 9.06 us -> 14.5 us
  matrix products: 5.05 us -> 0 us
  waiting for transfers between devices: 9 us -> 12 us
  other arithmetic: 3.28 us -> 1.43 us
  between operations: 1.57 us -> 0.71 us
    all_gather x3 -> x0, blocking collectives: 23.6 us -> none  [the longest x1 8.41 us: on_device(): lax.all_gather(support, 'orb', axis=0, tiled=True)]
    psum x2 -> x0, blocking collectives: 12.3 us -> none  [the longest x1 8.3 us: on_device(): summed = lax.psum(deposit, 'orb')]
    gather x7 -> x0, local copies, waits for them, and re-layouts: 10.7 us -> none  [the longest x2 5.32 us: shift_planes(): jnp.take_along_axis(rows, jnp.clip(index, 0, box_depth - 1)[:, None, :, N...]
    pallas_call x0 -> x3, Pallas kernels: none -> 7.84 us  [the longest x1 4.22 us: on_device(): pl.pallas_call(functools.partial(main_kernel, dims), out_shape=[jax.Shape...]
    ppermute x6 -> x9, starting transfers between devices: 9.06 us -> 14.5 us  [moved_by(): return lax.ppermute(value, axes if len(axes) > 1 else axes[0], pairs)]
    dot_general x5 -> x0, matrix products: 5.05 us -> none  [the longest x1 2.06 us: aux_step(): jnp.einsum('pst,ptjq->psjq', kern, moved.astype(jnp.float32), precision=l...]
    unnamed x1 -> x0, blocking collectives: 4.25 us -> none
    ppermute x6 -> x9, waiting for transfers between devices: 9 us -> 12 us  [moved_by(): return lax.ppermute(value, axes if len(axes) > 1 else axes[0], pairs)]
  transfers between devices with their start and end apart: 6 -> 9, of which waited for: 2 -> 5; matrix products, arithmetic and copies ran while one was open for 7% -> 0% of each run, Pallas kernels for 0% -> 0%
where the time goes in v1:
time: 40.1 us; the launch traced here: 39.8 us
  starting transfers between devices  14.5 us (36%)
  waiting for transfers between devices  12 us (30%)
  Pallas kernels  7.84 us (20%)
  local copies, waits for them, and re-layouts  3.21 us (8%)
  other arithmetic  1.43 us (4%)
  between operations  0.71 us (2%)
    ppermute x9, starting transfers between devices, moved_by(): return lax.ppermute(value, axes if len(axes) > 1 else axes[0], pairs)  14.5 us
    ppermute x9, waiting for transfers between devices, moved_by(): return lax.ppermute(value, axes if len(axes) > 1 else axes[0], pairs)  12 us
    pallas_call x1, Pallas kernels, on_device(): pl.pallas_call(functools.partial(main_kernel, dims), out_shape=[jax.Shape...  4.22 us
    unnamed x22, local copies, waits for them, and re-layouts  2.58 us
    pallas_call x1, Pallas kernels, on_device(): pl.pallas_call(functools.partial(pack_kernel, dims), out_shape=[jax.Shape...  2.03 us
    pallas_call x1, Pallas kernels, on_device(): pl.pallas_call(functools.partial(final_kernel, dims), out_shape=[jax.Shap...  1.59 us
    add x1, other arithmetic, on_device(): own_part + jnp.pad(from_above, ((0, 0), (0, own_part.shape[1] - 16), (0,...  0.89 us
  transfers between devices with their start and end apart: 9, of which 5 were waited for; matrix products, arithmetic and copies ran while one was open for 0% of the time, Pallas kernels for 0%

profile of v1, /device:TPU:0, one launch (start us, length us, event | category | flops | bytes accessed | tf_op | source)
XLA Modules:
  0.0 39.8 jit_solution(15064334609489025137)
XLA Ops:
  0.6 0.0 copy-start.9
  0.6 0.0 copy-start.10
  0.7 0.6 %copy-done.9 = s32[32]{0:T(128)S(1)} copy-done((s32[32]{0:T(128)S(1)}, s32[32]{0:T(128)}, u32[]{:S(2)}) %copy-start.9) | copy-done | bytes 152
  1.3 0.0 copy-done.10
  1.3 0.5 %fusion.1 = (s32[1,32]{1,0:T(1,128)}, s32[1,32]{1,0:T(1,128)}) fusion(s32[32]{0:T(128)S(1)} %copy-done.9, s32[]{:T(128)S(6)} %axis_index.28, s32[32]{0:T(128)S(1)} %copy-done.10), kind=kLoop, calls=%fused_computation.17 | loop fusion | flops 1440 | bytes 516 | tf_op jit(solution)/shard_map/reshape | solution.py:257
  1.8 2.0 %pack.1 = (bf16[8,72,128]{2,1,0:T(8,128)(2,1)}, bf16[8,72,128]{2,1,0:T(8,128)(2,1)}, bf16[7,72,128]{2,1,0:T(8,128)(2,1)}, bf16[7,72,128]{2,1,0:T(8,128)(2,1)}, f32[16,384]{1,0:T(8,128)}) custom-call(s32[1]{0:T(128)} %bitcast.orb_ref, s32[8]{0:T(128)} %anchor_ref.1, bf16[9,15,8,128]{3,2,1,0:T(8,128)(2,1)} %bitcast.17, f32[9,9,32]{2,1,0:T(8,128)} %bitcast.18, ...), custom_call_target="tpu_custom_call" | custom-call | tf_op jit(solution)/shard_map/pack/pallas_call | solution.py:260
  3.9 3.0 %collective-permute-start = (bf16[8,72,128]{2,1,0:T(8,128)(2,1)}, bf16[8,72,128]{2,1,0:T(8,128)(2,1)S(1)}, u32[]{:S(2)}, u32[]{:S(2)}) collective-permute-start(bf16[8,72,128]{2,1,0:T(8,128)(2,1)} %get-tuple-element.12), channel_id=1, source_target_pairs={{0,2},{2,0},{1,3},{3,1},{4,6},{6,4},{5,7},{7,5},{8,10},{10,8},{9,1... | collective-permute-start | bytes 442376 | tf_op jit(solution)/shard_map/ppermute | solution.py:30
  6.8 1.6 %collective-permute-start.1 = (bf16[7,72,128]{2,1,0:T(8,128)(2,1)}, bf16[7,72,128]{2,1,0:T(8,128)(2,1)S(1)}, u32[]{:S(2)}, u32[]{:S(2)}) collective-permute-start(bf16[7,72,128]{2,1,0:T(8,128)(2,1)} %get-tuple-element.13), channel_id=1, source_target_pairs={{0,4},{2,6},{4,8},{6,10},{8,12},{10,14},{12,0},{14,2},{1,5},{3,7},... | collective-permute-start | bytes 387080 | tf_op jit(solution)/shard_map/ppermute | solution.py:30
  8.4 1.5 %collective-permute-start.2 = (bf16[7,72,128]{2,1,0:T(8,128)(2,1)}, bf16[7,72,128]{2,1,0:T(8,128)(2,1)S(1)}, u32[]{:S(2)}, u32[]{:S(2)}) collective-permute-start(bf16[7,72,128]{2,1,0:T(8,128)(2,1)} %get-tuple-element.14), channel_id=1, source_target_pairs={{0,6},{2,4},{4,10},{6,8},{8,14},{10,12},{12,2},{14,0},{1,7},{3,5},... | collective-permute-start | bytes 387080 | tf_op jit(solution)/shard_map/ppermute | solution.py:30
  10.0 1.5 %collective-permute-start.3 = (f32[16,384]{1,0:T(8,128)}, f32[16,384]{1,0:T(8,128)S(1)}, u32[]{:S(2)}, u32[]{:S(2)}) collective-permute-start(f32[16,384]{1,0:T(8,128)} %get-tuple-element.15.rest_4_), channel_id=1, source_target_pairs={{0,2},{2,0},{1,3},{3,1},{4,6},{6,4},{5,7},{7,5},{8,10},{10,8},{9,1... | collective-permute-start | bytes 73736 | tf_op jit(solution)/shard_map/ppermute | solution.py:30
  11.5 1.6 %collective-permute-start.4 = (f32[16,384]{1,0:T(8,128)}, f32[16,384]{1,0:T(8,128)S(1)}, u32[]{:S(2)}, u32[]{:S(2)}) collective-permute-start(f32[16,384]{1,0:T(8,128)} %get-tuple-element.15.rest_4_), channel_id=1, source_target_pairs={{0,4},{2,6},{4,8},{6,10},{8,12},{10,14},{12,0},{14,2},{1,5},{3,7},... | collective-permute-start | bytes 73736 | tf_op jit(solution)/shard_map/ppermute | solution.py:30
  13.0 1.2 %collective-permute-done.3.rest_5_ = f32[16,384]{1,0:T(8,128)S(1)} collective-permute-done((f32[16,384]{1,0:T(8,128)}, f32[16,384]{1,0:T(8,128)S(1)}, u32[]{:S(2)}, u32[]{:S(2)}) %collective-permute-start.3) | collective-permute-done | bytes 24608 | tf_op jit(solution)/shard_map/ppermute | solution.py:30
  14.3 0.0 copy-start.5
  14.3 3.4 %collective-permute-start.5 = (f32[16,384]{1,0:T(8,128)}, f32[16,384]{1,0:T(8,128)S(1)}, u32[]{:S(2)}, u32[]{:S(2)}) collective-permute-start(f32[16,384]{1,0:T(8,128)} %get-tuple-element.15.rest_4_), channel_id=1, source_target_pairs={{0,6},{2,4},{4,10},{6,8},{8,14},{10,12},{12,2},{14,0},{1,7},{3,5},... | collective-permute-start | bytes 73736 | tf_op jit(solution)/shard_map/ppermute | solution.py:30
  17.7 0.0 collective-permute-done.4.rest_6_
  17.7 0.0 copy-start.6
  17.7 3.3 %collective-permute-done.5.rest_7_ = f32[16,384]{1,0:T(8,128)S(1)} collective-permute-done((f32[16,384]{1,0:T(8,128)}, f32[16,384]{1,0:T(8,128)S(1)}, u32[]{:S(2)}, u32[]{:S(2)}) %collective-permute-start.5) | collective-permute-done | bytes 24608 | tf_op jit(solution)/shard_map/ppermute | solution.py:30
  21.0 0.0 copy-start.7
  21.0 0.0 collective-permute-done.1.rest_2_
  21.0 0.0 copy-start.1
  21.0 0.0 collective-permute-done.2.rest_3_
  21.0 0.0 copy-start.2
  21.0 0.0 collective-permute-done.rest_1_
  21.0 0.0 copy-start
  21.0 0.0 copy-done.5
  21.0 0.0 copy-done.6
  21.1 0.5 %copy-done.7 = f32[16,384]{1,0:T(8,128)} copy-done((f32[16,384]{1,0:T(8,128)}, f32[16,384]{1,0:T(8,128)S(1)}, u32[]{:S(2)}) %copy-start.7) | copy-done | bytes 24600
  21.6 0.1 copy-done.1
  21.7 0.0 copy-done.2
  21.7 0.1 copy-done
  21.8 4.2 %main.1 = (f32[2,24,384]{2,1,0:T(8,128)}, f32[2,16,384]{2,1,0:T(8,128)}) custom-call(s32[1]{0:T(128)} %bitcast.orb_ref, f32[16,128]{1,0:T(8,128)} %v_ref.1, bf16[8,72,128]{2,1,0:T(8,128)(2,1)} %get-tuple-element.11.rest_0_, bf16[8,72,128]{2,1,0:T(8,128)(2,1)} %copy-done, bf16[7,72,128]{2,1,0:T(8,128)(2,1)} %copy-done.1, bf16[7,72,128]{2,1,0:T(8,128)(2,1)} %copy-done.2, ...), custom_call_target="tpu_custom_call" | custom-call | tf_op jit(solution)/shard_map/main/pallas_call | solution.py:289
  26.0 0.4 %collective-permute-start.6 = (f32[2,16,384]{2,1,0:T(8,128)}, f32[2,16,384]{2,1,0:T(8,128)S(1)}, u32[]{:S(2)}, u32[]{:S(2)}) collective-permute-start(f32[2,16,384]{2,1,0:T(8,128)} %get-tuple-element.17), channel_id=1, source_target_pairs={{0,12},{4,0},{8,4},{12,8},{1,13},{5,1},{9,5},{13,9},{2,14},{6,2},{... | collective-permute-start | bytes 147464 | tf_op jit(solution)/shard_map/ppermute | solution.py:30
  26.4 3.9 %collective-permute-done.6 = f32[2,16,384]{2,1,0:T(8,128)S(1)} collective-permute-done((f32[2,16,384]{2,1,0:T(8,128)}, f32[2,16,384]{2,1,0:T(8,128)S(1)}, u32[]{:S(2)}, u32[]{:S(2)}) %collective-permute-start.6) | collective-permute-done | bytes 49184 | tf_op jit(solution)/shard_map/ppermute | solution.py:30
  30.3 0.9 %pad_add_fusion = f32[2,24,384]{2,1,0:T(8,128)S(1)} fusion(f32[2,24,384]{2,1,0:T(8,128)} %get-tuple-element.16, f32[2,16,384]{2,1,0:T(8,128)S(1)} %collective-permute-done.6), kind=kLoop, calls=%fused_computation | loop fusion | flops 18432 | bytes 196608 | tf_op jit(solution)/shard_map/add | solution.py:309
  31.2 0.6 %slice_bitcast_fusion = (f32[24,384]{1,0:T(8,128)}, f32[24,384]{1,0:T(8,128)S(1)}) fusion(f32[2,24,384]{2,1,0:T(8,128)S(1)} %pad_add_fusion), kind=kLoop, calls=%fused_computation.1 | loop fusion | bytes 147456 | tf_op jit(solution)/shard_map/squeeze | solution.py:310
  31.8 1.5 %collective-permute-start.7 = (f32[24,384]{1,0:T(8,128)S(1)}, f32[24,384]{1,0:T(8,128)S(1)}, u32[]{:S(2)}, u32[]{:S(2)}) collective-permute-start(f32[24,384]{1,0:T(8,128)S(1)} %get-tuple-element.21), channel_id=1, source_target_pairs={{0,2},{2,0},{1,3},{3,1},{4,6},{6,4},{5,7},{7,5},{8,10},{10,8},{9,1... | collective-permute-start | bytes 110600 | tf_op jit(solution)/shard_map/ppermute | solution.py:30
  33.3 2.5 %collective-permute-done.7.rest_1_ = f32[24,384]{1,0:T(8,128)S(1)} collective-permute-done((f32[24,384]{1,0:T(8,128)S(1)}, f32[24,384]{1,0:T(8,128)S(1)}, u32[]{:S(2)}, u32[]{:S(2)}) %collective-permute-start.7) | collective-permute-done | bytes 36896 | tf_op jit(solution)/shard_map/ppermute | solution.py:30
  35.8 0.0 copy-start.3
  35.8 0.6 %copy-done.3 = f32[24,384]{1,0:T(8,128)} copy-done((f32[24,384]{1,0:T(8,128)}, f32[24,384]{1,0:T(8,128)S(1)}, u32[]{:S(2)}) %copy-start.3) | copy-done | bytes 36888
  36.4 0.0 copy-start.4
  36.4 0.0 collective-permute-start.8
  36.4 1.2 %collective-permute-done.8.other_ref = f32[16,384]{1,0:T(8,128)S(1)} collective-permute-done((f32[16,384]{1,0:T(8,128)S(1)}, f32[16,384]{1,0:T(8,128)S(1)}, u32[]{:S(2)}, u32[]{:S(2)}) %collective-permute-start.8) | collective-permute-done | bytes 24608 | tf_op jit(solution)/shard_map/ppermute | solution.py:30
  37.6 0.0 copy-start.8
  37.6 0.0 copy-done.4
  37.6 0.6 %copy-done.8 = f32[16,384]{1,0:T(8,128)} copy-done((f32[16,384]{1,0:T(8,128)}, f32[16,384]{1,0:T(8,128)S(1)}, u32[]{:S(2)}) %copy-start.8) | copy-done | bytes 24600
  38.2 1.6 %final.1 = (f32[16,128]{1,0:T(8,128)}, f32[9,9,32]{2,1,0:T(8,128)}) custom-call(s32[1]{0:T(128)} %bitcast.orb_ref, f32[16,384]{1,0:T(8,128)} %copy-done.4, f32[16,384]{1,0:T(8,128)} %copy-done.8, f32[24,384]{1,0:T(8,128)} %get-tuple-element.20.rest_0_, f32[24,384]{1,0:T(8,128)} %copy-done.3), custom_call_target="tpu_custom_call" | custom-call | tf_op jit(solution)/shard_map/final/pallas_call | solution.py:321
  (1 shorter events, 0.0 us)
Async XLA Ops:
  0.6 0.7 %copy-start.9 = (s32[32]{0:T(128)S(1)}, s32[32]{0:T(128)}, u32[]{:S(2)}) copy-start(s32[32]{0:T(128)} %param.10) | copy-start | bytes 388
  0.6 0.7 %copy-start.10 = (s32[32]{0:T(128)S(1)}, s32[32]{0:T(128)}, u32[]{:S(2)}) copy-start(s32[32]{0:T(128)} %param.11) | copy-start | bytes 388
  3.9 17.2 %collective-permute-start = (bf16[8,72,128]{2,1,0:T(8,128)(2,1)}, bf16[8,72,128]{2,1,0:T(8,128)(2,1)S(1)}, u32[]{:S(2)}, u32[]{:S(2)}) collective-permute-start(bf16[8,72,128]{2,1,0:T(8,128)(2,1)} %get-tuple-element.12), channel_id=1, source_target_pairs={{0,2},{2,0},{1,3},{3,1},{4,6},{6,4},{5,7},{7,5},{8,10},{10,8},{9,1... | collective-permute-start | bytes 442376 | tf_op jit(solution)/shard_map/ppermute | solution.py:30
  6.8 14.2 %collective-permute-start.1 = (bf16[7,72,128]{2,1,0:T(8,128)(2,1)}, bf16[7,72,128]{2,1,0:T(8,128)(2,1)S(1)}, u32[]{:S(2)}, u32[]{:S(2)}) collective-permute-start(bf16[7,72,128]{2,1,0:T(8,128)(2,1)} %get-tuple-element.13), channel_id=1, source_target_pairs={{0,4},{2,6},{4,8},{6,10},{8,12},{10,14},{12,0},{14,2},{1,5},{3,7},... | collective-permute-start | bytes 387080 | tf_op jit(solution)/shard_map/ppermute | solution.py:30
  8.4 12.6 %collective-permute-start.2 = (bf16[7,72,128]{2,1,0:T(8,128)(2,1)}, bf16[7,72,128]{2,1,0:T(8,128)(2,1)S(1)}, u32[]{:S(2)}, u32[]{:S(2)}) collective-permute-start(bf16[7,72,128]{2,1,0:T(8,128)(2,1)} %get-tuple-element.14), channel_id=1, source_target_pairs={{0,6},{2,4},{4,10},{6,8},{8,14},{10,12},{12,2},{14,0},{1,7},{3,5},... | collective-permute-start | bytes 387080 | tf_op jit(solution)/shard_map/ppermute | solution.py:30
  10.0 4.3 %collective-permute-start.3 = (f32[16,384]{1,0:T(8,128)}, f32[16,384]{1,0:T(8,128)S(1)}, u32[]{:S(2)}, u32[]{:S(2)}) collective-permute-start(f32[16,384]{1,0:T(8,128)} %get-tuple-element.15.rest_4_), channel_id=1, source_target_pairs={{0,2},{2,0},{1,3},{3,1},{4,6},{6,4},{5,7},{7,5},{8,10},{10,8},{9,1... | collective-permute-start | bytes 73736 | tf_op jit(solution)/shard_map/ppermute | solution.py:30
  11.5 6.2 %collective-permute-start.4 = (f32[16,384]{1,0:T(8,128)}, f32[16,384]{1,0:T(8,128)S(1)}, u32[]{:S(2)}, u32[]{:S(2)}) collective-permute-start(f32[16,384]{1,0:T(8,128)} %get-tuple-element.15.rest_4_), channel_id=1, source_target_pairs={{0,4},{2,6},{4,8},{6,10},{8,12},{10,14},{12,0},{14,2},{1,5},{3,7},... | collective-permute-start | bytes 73736 | tf_op jit(solution)/shard_map/ppermute | solution.py:30
  14.3 6.8 %copy-start.5 = (f32[16,384]{1,0:T(8,128)}, f32[16,384]{1,0:T(8,128)S(1)}, u32[]{:S(2)}) copy-start(f32[16,384]{1,0:T(8,128)S(1)} %collective-permute-done.3.rest_5_) | copy-start | bytes 73732
  14.3 6.7 %collective-permute-start.5 = (f32[16,384]{1,0:T(8,128)}, f32[16,384]{1,0:T(8,128)S(1)}, u32[]{:S(2)}, u32[]{:S(2)}) collective-permute-start(f32[16,384]{1,0:T(8,128)} %get-tuple-element.15.rest_4_), channel_id=1, source_target_pairs={{0,6},{2,4},{4,10},{6,8},{8,14},{10,12},{12,2},{14,0},{1,7},{3,5},... | collective-permute-start | bytes 73736 | tf_op jit(solution)/shard_map/ppermute | solution.py:30
  17.7 3.4 %copy-start.6 = (f32[16,384]{1,0:T(8,128)}, f32[16,384]{1,0:T(8,128)S(1)}, u32[]{:S(2)}) copy-start(f32[16,384]{1,0:T(8,128)S(1)} %collective-permute-done.4.rest_6_) | copy-start | bytes 73732
  21.0 0.6 %copy-start.7 = (f32[16,384]{1,0:T(8,128)}, f32[16,384]{1,0:T(8,128)S(1)}, u32[]{:S(2)}) copy-start(f32[16,384]{1,0:T(8,128)S(1)} %collective-permute-done.5.rest_7_) | copy-start | bytes 73732
  21.0 0.7 %copy-start.1 = (bf16[7,72,128]{2,1,0:T(8,128)(2,1)}, bf16[7,72,128]{2,1,0:T(8,128)(2,1)S(1)}, u32[]{:S(2)}) copy-start(bf16[7,72,128]{2,1,0:T(8,128)(2,1)S(1)} %collective-permute-done.1.rest_2_) | copy-start | bytes 387076
  21.0 0.7 %copy-start.2 = (bf16[7,72,128]{2,1,0:T(8,128)(2,1)}, bf16[7,72,128]{2,1,0:T(8,128)(2,1)S(1)}, u32[]{:S(2)}) copy-start(bf16[7,72,128]{2,1,0:T(8,128)(2,1)S(1)} %collective-permute-done.2.rest_3_) | copy-start | bytes 387076
  21.0 0.7 %copy-start = (bf16[8,72,128]{2,1,0:T(8,128)(2,1)}, bf16[8,72,128]{2,1,0:T(8,128)(2,1)S(1)}, u32[]{:S(2)}) copy-start(bf16[8,72,128]{2,1,0:T(8,128)(2,1)S(1)} %collective-permute-done.rest_1_) | copy-start | bytes 442372
  26.0 4.3 %collective-permute-start.6 = (f32[2,16,384]{2,1,0:T(8,128)}, f32[2,16,384]{2,1,0:T(8,128)S(1)}, u32[]{:S(2)}, u32[]{:S(2)}) collective-permute-start(f32[2,16,384]{2,1,0:T(8,128)} %get-tuple-element.17), channel_id=1, source_target_pairs={{0,12},{4,0},{8,4},{12,8},{1,13},{5,1},{9,5},{13,9},{2,14},{6,2},{... | collective-permute-start | bytes 147464 | tf_op jit(solution)/shard_map/ppermute | solution.py:30
  31.8 4.0 %collective-permute-start.7 = (f32[24,384]{1,0:T(8,128)S(1)}, f32[24,384]{1,0:T(8,128)S(1)}, u32[]{:S(2)}, u32[]{:S(2)}) collective-permute-start(f32[24,384]{1,0:T(8,128)S(1)} %get-tuple-element.21), channel_id=1, source_target_pairs={{0,2},{2,0},{1,3},{3,1},{4,6},{6,4},{5,7},{7,5},{8,10},{10,8},{9,1... | collective-permute-start | bytes 110600 | tf_op jit(solution)/shard_map/ppermute | solution.py:30
  35.8 0.6 %copy-start.3 = (f32[24,384]{1,0:T(8,128)}, f32[24,384]{1,0:T(8,128)S(1)}, u32[]{:S(2)}) copy-start(f32[24,384]{1,0:T(8,128)S(1)} %collective-permute-done.7.rest_1_) | copy-start | bytes 110596
  36.4 1.2 %copy-start.4 = (f32[16,384]{1,0:T(8,128)}, f32[16,384]{1,0:T(8,128)S(1)}, u32[]{:S(2)}) copy-start(f32[16,384]{1,0:T(8,128)S(1)} %slice_add_fusion.mine_ref) | copy-start | bytes 73732
  36.4 1.2 %collective-permute-start.8 = (f32[16,384]{1,0:T(8,128)S(1)}, f32[16,384]{1,0:T(8,128)S(1)}, u32[]{:S(2)}, u32[]{:S(2)}) collective-permute-start(f32[16,384]{1,0:T(8,128)S(1)} %slice_add_fusion.mine_ref), channel_id=1, source_target_pairs={{0,1},{1,0},{2,3},{3,2},{4,5},{5,4},{6,7},{7,6},{8,9},{9,8},{10,11... | collective-permute-start | bytes 73736 | tf_op jit(solution)/shard_map/ppermute | solution.py:30
  37.6 0.6 %copy-start.8 = (f32[16,384]{1,0:T(8,128)}, f32[16,384]{1,0:T(8,128)S(1)}, u32[]{:S(2)}) copy-start(f32[16,384]{1,0:T(8,128)S(1)} %collective-permute-done.8.other_ref) | copy-start | bytes 73732

commit v2 on v1

v2 whole, which is shorter than its diff:
```python
import functools

import jax
import jax.numpy as jnp
from jax import lax
from jax.experimental import pallas as pl
from jax.experimental.pallas import tpu as pltpu
from jax.sharding import PartitionSpec as P


LANES = 128
F32 = jnp.float32
BF16 = jnp.bfloat16


def moved_by(value, axes, steps):
    sizes = [lax.axis_size(axis) for axis in axes]
    pairs = []
    total = 1
    for size in sizes:
        total *= size
    for source in range(total):
        rest, place = source, []
        for size in reversed(sizes):
            place.insert(0, rest % size)
            rest //= size
        target = 0
        for size, here, step in zip(sizes, place, steps):
            target = target * size + (here + step) % size
        pairs.append((source, target))
    return lax.ppermute(value, axes if len(axes) > 1 else axes[0], pairs)


def round_up(count, unit):
    return (count + unit - 1) // unit * unit


def fixed(value):
    return pltpu.with_memory_space_constraint(value, pltpu.HBM)


def pack_kernel(dims, orb_ref, domain_ref, *rest):
    atoms, functions, depth, points, slab, ways, reach, pairs, space = dims
    given, rest = rest[:6], rest[6:]
    own_refs, next_refs = rest[:ways], rest[ways : 2 * ways]
    k_pad, row_pad, *held, x_sem, sems = rest[2 * ways :]
    anchor_ref, x_ref, k_ref, owner_ref, partner_ref, live_ref = held
    copies = [
        pltpu.make_async_copy(given[i], held[i], sems.at[i]) for i in range(6) if i != 1
    ]
    x_copies = [
        pltpu.make_async_copy(given[1].at[s], x_ref.at[s], x_sem.at[s]) for s in range(functions)
    ]
    copies[0].start()
    for copy in x_copies:
        copy.start()
    for copy in copies[1:]:
        copy.start()
    copies[0].wait()
    planes = slab // ways
    boxes = -(-depth // ways)
    orb, domain = orb_ref[0], domain_ref[0]
    atom = lax.broadcasted_iota(jnp.int32, (atoms, points), 0)
    offset = jnp.zeros((atoms, points), jnp.int32)
    for a in range(atoms):
        offset = jnp.where(atom == a, lax.rem(anchor_ref[a], slab), offset)
    zero = jnp.zeros((atoms, points), F32)
    masks = []
    for k in range(ways):
        residue = lax.rem(orb + k, ways)
        start = offset - residue
        shift = jnp.zeros((atoms, points), jnp.int32)
        for low in range(slab // ways):
            shift = shift + (start > low * ways).astype(jnp.int32)
        phase = shift * ways - start
        bits, size = [], 1
        while size <= -(-(slab - 1) // ways):
            bits.append((size, (shift & size) != 0))
            size *= 2
        masks.append(([phase == e for e in range(ways)], bits))
    for s in range(functions):
        x_copies[s].wait()
        tiles = [x_ref[s, j].astype(F32) for j in range(depth)]
        for k in range(ways):
            phases, bits = masks[k]
            line = []
            for m in range(boxes):
                pick = zero
                for e in range(ways):
                    j = m * ways + e
                    pick = jnp.where(phases[e], tiles[j] if j < depth else zero, pick)
                line.append(pick)
            for size, mask in bits:
                length = min(len(line) + size, planes + reach)
                line = [
                    jnp.where(
                        mask,
                        line[h - size] if h >= size else zero,
                        line[h] if h < len(line) else zero,
                    )
                    for h in range(length)
                ]
            line = line + [zero] * (planes + reach - len(line))
            rows = pl.ds(s * atoms, atoms)
            for h in range(planes):
                own_refs[k][h, rows, :] = line[h].astype(BF16)
            for h in range(reach):
                next_refs[k][h, rows, :] = line[planes + h].astype(BF16)
    per = LANES // pairs
    groups = -(-functions // per)
    for copy in copies[1:]:
        copy.wait()
    k_pad[...] = jnp.zeros_like(k_pad)
    k_pad[:, :functions, :pairs] = k_ref[...]
    row_pad[...] = jnp.zeros_like(row_pad)
    for s in range(functions):
        for g in range(groups):
            row = jnp.zeros((1, LANES), F32)
            for i in range(per):
                t = g * per + i
                if t < functions:
                    piece = k_pad[s, t : t + 1, :]
                    row = row + (pltpu.roll(piece, i * pairs, 1) if i else piece)
            row_pad[g * functions + s : g * functions + s + 1, :] = row
    per_domain = atoms * ways
    owner = owner_ref[...] - (domain * ways + orb) * atoms
    partner = partner_ref[...]
    home = jnp.floor((partner.astype(F32) + 0.5) * (1.0 / per_domain)).astype(jnp.int32)
    relative = home - domain + 1
    relative = jnp.where(relative < 0, relative + space, relative)
    relative = jnp.where(relative >= space, relative - space, relative)
    code = relative * per_domain + partner - home * per_domain
    base = groups * functions
    row_pad[base : base + 1, :pairs] = owner.astype(F32)
    row_pad[base + 1 : base + 2, :pairs] = live_ref[...].astype(F32)
    row_pad[base + 2 : base + 3, :pairs] = code.astype(F32)
    index = row_pad[base : base + 3, :]
    wide = index
    for i in range(1, per):
        wide = wide + pltpu.roll(index, i * pairs, 1)
    row_pad[base : base + 3, :] = wide
    info = row_pad[...]
    high = info.astype(BF16)
    low = (info - high.astype(F32)).astype(BF16)
    height = info.shape[0]
    for refs, last in ((own_refs, planes), (next_refs, reach)):
        for k in range(ways):
            refs[k][last, 0:height, :] = high
            refs[k][last, height : 2 * height, :] = low


def main_kernel(dims, orb_ref, v_ref, *rest):
    atoms, functions, _, points, slab, ways, _, pairs, _ = dims
    planes = slab // ways
    sources = 2 * ways
    source_refs = rest[:sources]
    own_out, low_out, f_ref, w_ref, d_ref, table_ref, own_ref, info_ref = rest[sources:]
    block = functions * atoms
    band = sources * atoms
    rows = functions * band
    padded = f_ref.shape[0]
    per = LANES // pairs
    groups = -(-functions // per)
    height = info_ref.shape[0] // 2
    spans, first = [], 0
    most = table_ref.shape[1] // band
    while first < functions:
        count = min(most, functions - first)
        spans.append((first, count, round_up(count * pairs, LANES)))
        first += count
    orb = orb_ref[0]
    per_domain = atoms * ways
    contract = (((1,), (1,)), ((), ()))
    for h in range(planes):
        for c in range(sources):
            last = source_refs[c].shape[0] - 1
            for s in range(functions):
                place = (pl.ds((s * sources + c) * atoms, atoms), pl.ds(h * points, points))
                if h < last:
                    f_ref[place] = source_refs[c][h, s * atoms : (s + 1) * atoms, :]
                else:
                    f_ref[place] = jnp.zeros((atoms, points), BF16)
    if padded > rows:
        f_ref[rows:, :] = jnp.zeros((padded - rows, planes * points), BF16)
    tail = rows // LANES * LANES
    if padded > tail:
        d_ref[:, tail:padded] = jnp.zeros((rows, padded - tail), BF16)
        d_ref[:, padded + tail :] = jnp.zeros((rows, padded - tail), BF16)
    size = table_ref.shape[1:]
    row_id = lax.broadcasted_iota(jnp.int32, size, 0)
    lane_id = lax.broadcasted_iota(jnp.int32, (1, size[1]), 1)
    function_id = jnp.zeros((1, size[1]), jnp.int32)
    for t in range(1, size[1] // pairs):
        function_id = function_id + (lane_id >= t * pairs).astype(jnp.int32)
    atom_id = lax.broadcasted_iota(jnp.int32, (atoms, LANES), 0)
    base = groups * functions
    for c in range(sources):
        last = source_refs[c].shape[0] - 1
        pair_high = source_refs[c][last, 0:height, :].astype(F32)
        pair_low = source_refs[c][last, height : 2 * height, :].astype(F32)
        owner = pair_high[base : base + 1, :].astype(jnp.int32)
        live = pair_high[base + 1 : base + 2, :]
        code = pair_high[base + 2 : base + 3, :].astype(jnp.int32)
        domain = (code >= per_domain).astype(jnp.int32) + (code >= 2 * per_domain).astype(jnp.int32)
        inside = code - domain * per_domain
        orb_of = jnp.zeros(code.shape, jnp.int32)
        for i in range(1, ways):
            orb_of = orb_of + (inside >= i * atoms).astype(jnp.int32)
        local = inside - orb_of * atoms
        slot = orb - orb_of
        slot = jnp.where(slot < 0, slot + ways, slot)
        if c < ways:
            slot = slot + jnp.where(domain == 0, ways, 0)
            valid = domain <= 1
        else:
            slot = slot + jnp.where(domain == 1, ways, 0)
            valid = domain >= 1
        inner = jnp.where(valid, slot * atoms + local, -padded * LANES)
        inner = jnp.concatenate([inner] * (size[1] // LANES), axis=1)
        target = inner + function_id * band
        table = jnp.where(row_id == target, 1.0, 0.0).astype(BF16)
        table_ref[c] = table
        own = jnp.where(atom_id == owner, live, 0.0)
        own_ref[c] = own
        for first, count, lanes in spans:
            parts = []
            for pair_rows in (pair_high, pair_low):
                for s in range(functions):
                    parts.append(
                        jnp.concatenate(
                            [
                                pair_rows[g * functions + s : g * functions + s + 1, :] * own
                                for g in range(first // per, first // per + lanes // LANES)
                            ],
                            axis=1,
                        )
                    )
            left = jnp.concatenate(parts, axis=0).astype(BF16)
            cols = count * band
            part = lax.dot_general(
                left, table_ref[c, :cols, :lanes], contract, preferred_element_type=F32
            )
            part = part[:block] + part[block:]
            high = part.astype(BF16)
            low = (part - high.astype(F32)).astype(BF16)
            for s in range(functions):
                place = pl.ds((s * sources + c) * atoms, atoms)
                d_ref[place, first * band : first * band + cols] = high[s * atoms : (s + 1) * atoms]
                d_ref[place, padded + first * band : padded + first * band + cols] = low[
                    s * atoms : (s + 1) * atoms
                ]
    f_all = f_ref[...]
    aux = jnp.dot(d_ref[...], jnp.concatenate([f_all, f_all], axis=0), preferred_element_type=F32)
    density = jnp.sum(aux * f_ref[:rows, :].astype(F32), axis=0, keepdims=True)
    v_ext = jnp.concatenate([v_ref[pl.ds(h * ways + orb, 1), :] for h in range(planes)], axis=1)
    potential = v_ext + density / jnp.sqrt(1.0 + density * density)
    w_ref[...] = (f_ref[:rows, :].astype(F32) * potential).astype(BF16)
    blocks = lax.dot_general(w_ref[...], f_ref[:rows, :], contract, preferred_element_type=F32)
    own_out[...] = jnp.zeros_like(own_out)
    low_out[...] = jnp.zeros_like(low_out)
    for c in range(sources):
        own = own_ref[c]
        mine = jnp.concatenate(
            [blocks[(s * sources + c) * atoms : (s * sources + c + 1) * atoms] for s in range(functions)],
            axis=0,
        )
        high = mine.astype(BF16)
        low = (mine - high.astype(F32)).astype(BF16)
        both = jnp.concatenate([high, low], axis=0)
        for first, count, lanes in spans:
            cols = count * band
            spread = jnp.dot(
                both[:, first * band : first * band + cols],
                table_ref[c, :cols, :lanes],
                preferred_element_type=F32,
            )
            spread = spread[:block] + spread[block:]
            owned = jnp.concatenate([own] * (lanes // LANES), axis=1)
            picked = jnp.concatenate(
                [
                    jnp.sum(spread[s * atoms : (s + 1) * atoms] * owned, axis=0, keepdims=True)
                    for s in range(functions)
                ],
                axis=0,
            )
            place = pl.ds(first * pairs, lanes)
            if c < ways:
                own_out[c, :functions, place] = picked
            else:
                low_out[c - ways, :functions, place] = picked
        if c < ways:
            for h in range(planes):
                own_out[c, 16 + h : 17 + h, :points] = density[:, h * points : (h + 1) * points]


def final_kernel(dims, orb_ref, mine_ref, other_ref, *rest):
    _, functions, _, points, slab, ways, _, pairs, _ = dims
    planes = slab // ways
    message_refs = rest[:ways]
    density_out, blocks_out, density_ref, blocks_ref, pad_ref, sems = rest[ways:]
    orb = orb_ref[0]
    for k in range(ways):
        residue = lax.rem(orb + k, ways)
        for h in range(planes):
            density_ref[pl.ds(h * ways + residue, 1), :] = message_refs[k][16 + h : 17 + h, :points]
    first = pltpu.make_async_copy(density_ref, density_out, sems.at[0])
    first.start()
    total = mine_ref[...] + other_ref[...]
    per = LANES // pairs
    for t in range(functions):
        g, i = t // per, t % per
        piece = total[:, g * LANES : (g + 1) * LANES]
        if i:
            piece = pltpu.roll(piece, LANES - i * pairs, 1)
        pad_ref[t] = piece
    for t in range(functions):
        for s in range(functions):
            blocks_ref[s, t : t + 1, :] = pad_ref[t, s : s + 1, :pairs]
    second = pltpu.make_async_copy(blocks_ref, blocks_out, sems.at[1])
    second.start()
    first.wait()
    second.wait()


def on_device(support, anchor, kernel, pair_owner, pair_partner, pair_live, v_ext):
    atoms, functions, depth, points = support.shape
    pairs = kernel.shape[0]
    slab = v_ext.shape[0]
    ways = lax.axis_size("orb")
    space = lax.axis_size("space")
    planes = slab // ways
    reach = min((depth - 2) // ways + 1, planes)
    dims = (atoms, functions, depth, points, slab, ways, reach, pairs, space)
    orb = jnp.reshape(lax.axis_index("orb"), (1,)).astype(jnp.int32)
    domain = jnp.reshape(lax.axis_index("space"), (1,)).astype(jnp.int32)
    block = functions * atoms
    band = 2 * ways * atoms
    per = LANES // pairs
    groups = -(-functions // per)
    lanes = groups * LANES
    height = round_up(groups * functions + 3, 16)
    smem = pl.BlockSpec(memory_space=pltpu.SMEM)
    vmem = pl.BlockSpec(memory_space=pltpu.VMEM)
    hbm = pl.BlockSpec(memory_space=pltpu.HBM)

    packed = pl.pallas_call(
        functools.partial(pack_kernel, dims),
        out_shape=[jax.ShapeDtypeStruct((planes + 1, block, points), BF16)] * ways
        + [jax.ShapeDtypeStruct((reach + 1, block, points), BF16)] * ways,
        in_specs=[smem, smem] + [hbm] * 6,
        out_specs=[vmem] * (2 * ways),
        scratch_shapes=[
            pltpu.VMEM((functions, 16, LANES), F32),
            pltpu.VMEM((height, LANES), F32),
            pltpu.SMEM((atoms,), jnp.int32),
            pltpu.VMEM((functions, depth, atoms, points), BF16),
            pltpu.VMEM((functions, functions, pairs), F32),
            pltpu.VMEM((1, pairs), jnp.int32),
            pltpu.VMEM((1, pairs), jnp.int32),
            pltpu.VMEM((1, pairs), jnp.int32),
            pltpu.SemaphoreType.DMA((functions,)),
            pltpu.SemaphoreType.DMA((6,)),
        ],
        compiler_params=pltpu.CompilerParams(vmem_limit_bytes=8 << 20),
        name="pack",
    )(
        orb,
        domain,
        fixed(anchor),
        fixed(support.transpose(1, 2, 0, 3)),
        fixed(kernel.transpose(1, 2, 0)),
        fixed(pair_owner.reshape(1, pairs)),
        fixed(pair_partner.reshape(1, pairs)),
        fixed(pair_live.reshape(1, pairs)),
    )
    own, onward = packed[:ways], packed[ways:]
    upper, peers = [], []
    for k in range(ways):
        upper.append(moved_by(onward[k], ("space", "orb"), (1, k)))
    for k in range(1, ways):
        peers.append(moved_by(own[k], ("orb",), (k,)))
    sources = [own[0]] + peers + upper

    rows = functions * band
    padded = round_up(rows, LANES)
    most = 256 // max(band, pairs)
    own_part, low_part = pl.pallas_call(
        functools.partial(main_kernel, dims),
        out_shape=[
            jax.ShapeDtypeStruct((ways, 16 + round_up(planes, 8), lanes), F32),
            jax.ShapeDtypeStruct((ways, 16, lanes), F32),
        ],
        in_specs=[smem] + [vmem] * (1 + 2 * ways),
        out_specs=[vmem] * 2,
        scratch_shapes=[
            pltpu.VMEM((padded, planes * points), BF16),
            pltpu.VMEM((rows, planes * points), BF16),
            pltpu.VMEM((rows, 2 * padded), BF16),
            pltpu.VMEM((2 * ways, most * band, round_up(most * pairs, LANES)), BF16),
            pltpu.VMEM((2 * ways, atoms, LANES), F32),
            pltpu.VMEM((2 * height, LANES), F32),
        ],
        compiler_params=pltpu.CompilerParams(vmem_limit_bytes=24 << 20),
        name="main",
    )(orb, v_ext, *sources)

    from_above = moved_by(low_part, ("space",), (-1,))
    total = own_part + jnp.pad(from_above, ((0, 0), (0, own_part.shape[1] - 16), (0, 0)))
    messages = [total[0]]
    mine = total[0, :16]
    for k in range(1, ways):
        message = moved_by(total[k], ("orb",), (-k,))
        messages.append(message)
        mine = mine + message[:16]
    shares = lax.axis_size("grid")
    other = moved_by(mine, ("grid",), (1,))
    for k in range(2, shares):
        other = other + moved_by(mine, ("grid",), (k,))
    density, blocks = pl.pallas_call(
        functools.partial(final_kernel, dims),
        out_shape=[
            jax.ShapeDtypeStruct((slab, points), F32),
            jax.ShapeDtypeStruct((functions, functions, pairs), F32),
        ],
        in_specs=[smem] + [vmem] * (2 + ways),
        out_specs=[hbm] * 2,
        scratch_shapes=[
            pltpu.VMEM((slab, points), F32),
            pltpu.VMEM((functions, functions, pairs), F32),
            pltpu.VMEM((functions, 16, LANES), F32),
            pltpu.SemaphoreType.DMA((2,)),
        ],
        compiler_params=pltpu.CompilerParams(vmem_limit_bytes=4 << 20),
        name="final",
    )(orb, mine, other, *messages)
    return (density, blocks.transpose(2, 0, 1))


def solution(mesh):
    placed = (
        P(("shift", "space", "orb"), None, None, "grid"),
        P(("shift", "space", "orb")),
        P(("shift", "space", "orb"), None, None),
        P(("shift", "space", "orb")),
        P(("shift", "space", "orb")),
        P(("shift", "space", "orb")),
        P(("shift", "space"), "grid"),
    )
    return jax.shard_map(
        on_device,
        mesh=mesh,
        in_specs=placed,
        out_specs=(P(("shift", "space"), "grid"), P(("shift", "space", "orb"), None, None)),
        check_vma=False,
    )
```

time: 40.1 us -> 27.3 us (0.68)
  starting transfers between devices: 14.5 us -> 9.51 us
  Pallas kernels: 7.84 us -> 3.72 us
  local copies, waits for them, and re-layouts: 3.21 us -> 0.01 us
  other arithmetic: 1.43 us -> 0.01 us
  waiting for transfers between devices: 12 us -> 13.2 us
    ppermute x9 -> x6, starting transfers between devices: 14.5 us -> 9.51 us  [moved_by(): return lax.ppermute(value, axes if len(axes) > 1 else axes[0], pairs)]
    pallas_call x1, Pallas kernels: 4.22 us -> 1.62 us  [on_device(): pl.pallas_call(functools.partial(main_kernel, dims), out_shape=[jax.Shape...]
    unnamed x22 -> x2, local copies, waits for them, and re-layouts: 2.58 us -> 0.01 us
    ppermute x9 -> x6, waiting for transfers between devices: 12 us -> 13.2 us  [moved_by(): return lax.ppermute(value, axes if len(axes) > 1 else axes[0], pairs)]
    add x1, other arithmetic: 0.89 us -> 0.01 us  [on_device(): own_part + jnp.pad(from_above, ((0, 0), (0, own_part.shape[1] - 16), (0,...]
    pallas_call x1, Pallas kernels: 1.59 us -> 0.73 us  [on_device(): pl.pallas_call(functools.partial(final_kernel, dims), out_shape=[jax.Shap...]
    pallas_call x1, Pallas kernels: 2.03 us -> 1.37 us  [on_device(): pl.pallas_call(functools.partial(pack_kernel, dims), out_shape=[jax.Shape...]
    squeeze x1, local copies, waits for them, and re-layouts: 0.63 us -> 0.01 us  [on_device(): messages = [total[0]]]
  transfers between devices with their start and end apart: 9 -> 6, of which waited for: 5 -> 5; matrix products, arithmetic and copies ran while one was open for 0% -> 0% of each run, Pallas kernels for 0% -> 0%
where the time goes in v2:
time: 27.3 us; the launch traced here: 27.1 us
  waiting for transfers between devices  13.2 us (48%)
  starting transfers between devices  9.51 us (35%)
  Pallas kernels  3.72 us (14%)
  between operations  0.68 us (2%)
    ppermute x6, waiting for transfers between devices, moved_by(): return lax.ppermute(value, axes if len(axes) > 1 else axes[0], pairs)  13.2 us
    ppermute x6, starting transfers between devices, moved_by(): return lax.ppermute(value, axes if len(axes) > 1 else axes[0], pairs)  9.51 us
    pallas_call x1, Pallas kernels, on_device(): pl.pallas_call(functools.partial(main_kernel, dims), out_shape=[jax.Shape...  1.62 us
    pallas_call x1, Pallas kernels, on_device(): pl.pallas_call(functools.partial(pack_kernel, dims), out_shape=[jax.Shape...  1.37 us
    pallas_call x1, Pallas kernels, on_device(): pl.pallas_call(functools.partial(final_kernel, dims), out_shape=[jax.Shap...  0.73 us
  transfers between devices with their start and end apart: 6, of which 5 were waited for; matrix products, arithmetic and copies ran while one was open for 0% of the time, Pallas kernels for 0%

profile of v2, /device:TPU:0, one launch (start us, length us, event | category | flops | bytes accessed | tf_op | source)
XLA Modules:
  0.0 27.1 jit_solution(5398341492931939004)
XLA Ops:
  0.6 0.0 copy-start
  0.6 1.4 %pack.1 = (bf16[9,72,128]{2,1,0:T(8,128)(2,1)S(1)}, bf16[9,72,128]{2,1,0:T(8,128)(2,1)S(1)}, bf16[8,72,128]{2,1,0:T(8,128)(2,1)S(1)}, bf16[8,72,128]{2,1,0:T(8,128)(2,1)S(1)}) custom-call(s32[1]{0:T(128)} %bitcast.orb_ref, s32[1]{0:T(128)} %bitcast.1.domain_ref, s32[8]{0:T(128)} %rest_0_.1, bf16[9,15,8,128]{3,2,1,0:T(8,128)(2,1)} %bitcast.16, ...), custom_call_target="tpu_custom_call" | custom-call | tf_op jit(solution)/shard_map/pack/pallas_call | solution.py:346
  2.0 3.0 %collective-permute-start = (bf16[9,72,128]{2,1,0:T(8,128)(2,1)S(1)}, bf16[9,72,128]{2,1,0:T(8,128)(2,1)S(1)}, u32[]{:S(2)}, u32[]{:S(2)}) collective-permute-start(bf16[9,72,128]{2,1,0:T(8,128)(2,1)S(1)} %get-tuple-element.11), channel_id=1, source_target_pairs={{0,2},{2,0},{1,3},{3,1},{4,6},{6,4},{5,7},{7,5},{8,10},{10,8},{9,1... | collective-permute-start | bytes 497672 | tf_op jit(solution)/shard_map/ppermute | solution.py:31
  5.1 1.6 %collective-permute-start.1 = (bf16[8,72,128]{2,1,0:T(8,128)(2,1)S(1)}, bf16[8,72,128]{2,1,0:T(8,128)(2,1)S(1)}, u32[]{:S(2)}, u32[]{:S(2)}) collective-permute-start(bf16[8,72,128]{2,1,0:T(8,128)(2,1)S(1)} %get-tuple-element.12), channel_id=1, source_target_pairs={{0,4},{2,6},{4,8},{6,10},{8,12},{10,14},{12,0},{14,2},{1,5},{3,7},... | collective-permute-start | bytes 442376 | tf_op jit(solution)/shard_map/ppermute | solution.py:31
  6.6 1.5 %collective-permute-start.2 = (bf16[8,72,128]{2,1,0:T(8,128)(2,1)S(1)}, bf16[8,72,128]{2,1,0:T(8,128)(2,1)S(1)}, u32[]{:S(2)}, u32[]{:S(2)}) collective-permute-start(bf16[8,72,128]{2,1,0:T(8,128)(2,1)S(1)} %get-tuple-element.13), channel_id=1, source_target_pairs={{0,6},{2,4},{4,10},{6,8},{8,14},{10,12},{12,2},{14,0},{1,7},{3,5},... | collective-permute-start | bytes 442376 | tf_op jit(solution)/shard_map/ppermute | solution.py:31
  8.2 5.4 %collective-permute-done.1.rest_2_ = bf16[8,72,128]{2,1,0:T(8,128)(2,1)S(1)} collective-permute-done((bf16[8,72,128]{2,1,0:T(8,128)(2,1)S(1)}, bf16[8,72,128]{2,1,0:T(8,128)(2,1)S(1)}, u32[]{:S(2)}, u32[]{:S(2)}) %collective-permute-start.1) | collective-permute-done | bytes 147488 | tf_op jit(solution)/shard_map/ppermute | solution.py:31
  13.6 1.8 %collective-permute-done.2.rest_3_ = bf16[8,72,128]{2,1,0:T(8,128)(2,1)S(1)} collective-permute-done((bf16[8,72,128]{2,1,0:T(8,128)(2,1)S(1)}, bf16[8,72,128]{2,1,0:T(8,128)(2,1)S(1)}, u32[]{:S(2)}, u32[]{:S(2)}) %collective-permute-start.2) | collective-permute-done | bytes 147488 | tf_op jit(solution)/shard_map/ppermute | solution.py:31
  15.4 0.0 collective-permute-done.rest_1_
  15.4 0.0 copy-done
  15.4 1.6 %main.1 = (f32[2,24,384]{2,1,0:T(8,128)S(1)}, f32[2,16,384]{2,1,0:T(8,128)S(1)}) custom-call(s32[1]{0:T(128)} %bitcast.orb_ref, f32[16,128]{1,0:T(8,128)S(1)} %copy-done, bf16[9,72,128]{2,1,0:T(8,128)(2,1)S(1)} %get-tuple-element.10.rest_0_, bf16[9,72,128]{2,1,0:T(8,128)(2,1)S(1)} %collective-permute-done.rest_1_, ...), custom_call_target="tpu_custom_call" | custom-call | tf_op jit(solution)/shard_map/main/pallas_call | solution.py:387
  17.0 1.8 %collective-permute-start.3 = (f32[2,16,384]{2,1,0:T(8,128)S(1)}, f32[2,16,384]{2,1,0:T(8,128)S(1)}, u32[]{:S(2)}, u32[]{:S(2)}) collective-permute-start(f32[2,16,384]{2,1,0:T(8,128)S(1)} %get-tuple-element.15), channel_id=1, source_target_pairs={{0,12},{4,0},{8,4},{12,8},{1,13},{5,1},{9,5},{13,9},{2,14},{6,2},{... | collective-permute-start | bytes 147464 | tf_op jit(solution)/shard_map/ppermute | solution.py:31
  18.8 2.3 %collective-permute-done.3 = f32[2,16,384]{2,1,0:T(8,128)S(1)} collective-permute-done((f32[2,16,384]{2,1,0:T(8,128)S(1)}, f32[2,16,384]{2,1,0:T(8,128)S(1)}, u32[]{:S(2)}, u32[]{:S(2)}) %collective-permute-start.3) | collective-permute-done | bytes 49184 | tf_op jit(solution)/shard_map/ppermute | solution.py:31
  21.2 1.6 %collective-permute-start.4 = (f32[24,384]{1,0:T(8,128)S(1)}, f32[24,384]{1,0:T(8,128)S(1)}, u32[]{:S(2)}, u32[]{:S(2)}) collective-permute-start(f32[24,384]{1,0:T(8,128)S(1)} %get-tuple-element.19), channel_id=1, source_target_pairs={{0,2},{2,0},{1,3},{3,1},{4,6},{6,4},{5,7},{7,5},{8,10},{10,8},{9,1... | collective-permute-start | bytes 110600 | tf_op jit(solution)/shard_map/ppermute | solution.py:31
  22.7 2.5 %collective-permute-done.4.rest_1_ = f32[24,384]{1,0:T(8,128)S(1)} collective-permute-done((f32[24,384]{1,0:T(8,128)S(1)}, f32[24,384]{1,0:T(8,128)S(1)}, u32[]{:S(2)}, u32[]{:S(2)}) %collective-permute-start.4) | collective-permute-done | bytes 36896 | tf_op jit(solution)/shard_map/ppermute | solution.py:31
  25.2 0.0 collective-permute-start.5
  25.2 1.2 %collective-permute-done.5.other_ref = f32[16,384]{1,0:T(8,128)S(1)} collective-permute-done((f32[16,384]{1,0:T(8,128)S(1)}, f32[16,384]{1,0:T(8,128)S(1)}, u32[]{:S(2)}, u32[]{:S(2)}) %collective-permute-start.5) | collective-permute-done | bytes 24608 | tf_op jit(solution)/shard_map/ppermute | solution.py:31
  26.4 0.7 %final.1 = (f32[16,128]{1,0:T(8,128)}, f32[9,9,32]{2,1,0:T(8,128)}) custom-call(s32[1]{0:T(128)} %bitcast.orb_ref, f32[16,384]{1,0:T(8,128)S(1)} %slice_add_fusion.mine_ref, f32[16,384]{1,0:T(8,128)S(1)} %collective-permute-done.5.other_ref, f32[24,384]{1,0:T(8,128)S(1)} %get-tuple-element.18.rest_0_, f32[24,384]{1,0:T(8,128)S(1)} %collective-permute-done.4.rest_1_), custom_call_target="tpu_custom_call" | custom-call | tf_op jit(solution)/shard_map/final/pallas_call | solution.py:419
  (3 shorter events, 0.0 us)
Async XLA Ops:
  0.6 14.7 %copy-start = (f32[16,128]{1,0:T(8,128)S(1)}, f32[16,128]{1,0:T(8,128)}, u32[]{:S(2)}) copy-start(f32[16,128]{1,0:T(8,128)} %v_ref.1) | copy-start | bytes 24580
  2.0 13.3 %collective-permute-start = (bf16[9,72,128]{2,1,0:T(8,128)(2,1)S(1)}, bf16[9,72,128]{2,1,0:T(8,128)(2,1)S(1)}, u32[]{:S(2)}, u32[]{:S(2)}) collective-permute-start(bf16[9,72,128]{2,1,0:T(8,128)(2,1)S(1)} %get-tuple-element.11), channel_id=1, source_target_pairs={{0,2},{2,0},{1,3},{3,1},{4,6},{6,4},{5,7},{7,5},{8,10},{10,8},{9,1... | collective-permute-start | bytes 497672 | tf_op jit(solution)/shard_map/ppermute | solution.py:31
  5.1 8.5 %collective-permute-start.1 = (bf16[8,72,128]{2,1,0:T(8,128)(2,1)S(1)}, bf16[8,72,128]{2,1,0:T(8,128)(2,1)S(1)}, u32[]{:S(2)}, u32[]{:S(2)}) collective-permute-start(bf16[8,72,128]{2,1,0:T(8,128)(2,1)S(1)} %get-tuple-element.12), channel_id=1, source_target_pairs={{0,4},{2,6},{4,8},{6,10},{8,12},{10,14},{12,0},{14,2},{1,5},{3,7},... | collective-permute-start | bytes 442376 | tf_op jit(solution)/shard_map/ppermute | solution.py:31
  6.6 8.7 %collective-permute-start.2 = (bf16[8,72,128]{2,1,0:T(8,128)(2,1)S(1)}, bf16[8,72,128]{2,1,0:T(8,128)(2,1)S(1)}, u32[]{:S(2)}, u32[]{:S(2)}) collective-permute-start(bf16[8,72,128]{2,1,0:T(8,128)(2,1)S(1)} %get-tuple-element.13), channel_id=1, source_target_pairs={{0,6},{2,4},{4,10},{6,8},{8,14},{10,12},{12,2},{14,0},{1,7},{3,5},... | collective-permute-start | bytes 442376 | tf_op jit(solution)/shard_map/ppermute | solution.py:31
  17.0 4.1 %collective-permute-start.3 = (f32[2,16,384]{2,1,0:T(8,128)S(1)}, f32[2,16,384]{2,1,0:T(8,128)S(1)}, u32[]{:S(2)}, u32[]{:S(2)}) collective-permute-start(f32[2,16,384]{2,1,0:T(8,128)S(1)} %get-tuple-element.15), channel_id=1, source_target_pairs={{0,12},{4,0},{8,4},{12,8},{1,13},{5,1},{9,5},{13,9},{2,14},{6,2},{... | collective-permute-start | bytes 147464 | tf_op jit(solution)/shard_map/ppermute | solution.py:31
  21.2 4.0 %collective-permute-start.4 = (f32[24,384]{1,0:T(8,128)S(1)}, f32[24,384]{1,0:T(8,128)S(1)}, u32[]{:S(2)}, u32[]{:S(2)}) collective-permute-start(f32[24,384]{1,0:T(8,128)S(1)} %get-tuple-element.19), channel_id=1, source_target_pairs={{0,2},{2,0},{1,3},{3,1},{4,6},{6,4},{5,7},{7,5},{8,10},{10,8},{9,1... | collective-permute-start | bytes 110600 | tf_op jit(solution)/shard_map/ppermute | solution.py:31
  25.2 1.2 %collective-permute-start.5 = (f32[16,384]{1,0:T(8,128)S(1)}, f32[16,384]{1,0:T(8,128)S(1)}, u32[]{:S(2)}, u32[]{:S(2)}) collective-permute-start(f32[16,384]{1,0:T(8,128)S(1)} %slice_add_fusion.mine_ref), channel_id=1, source_target_pairs={{0,1},{1,0},{2,3},{3,2},{4,5},{5,4},{6,7},{7,6},{8,9},{9,8},{10,11... | collective-permute-start | bytes 73736 | tf_op jit(solution)/shard_map/ppermute | solution.py:31

commit v3 on v2

--- a/solution.py
+++ b/solution.py
@@ -154,7 +154,8 @@
     planes = slab // ways
     sources = 2 * ways
     source_refs = rest[:sources]
-    own_out, low_out, f_ref, w_ref, d_ref, table_ref, own_ref, info_ref = rest[sources:]
+    own_outs, low_outs = rest[sources : sources + ways], rest[sources + ways : sources + 2 * ways]
+    f_ref, w_ref, d_ref, table_ref, own_ref, info_ref = rest[sources + 2 * ways :]
     block = functions * atoms
     band = sources * atoms
     rows = functions * band
@@ -256,8 +257,10 @@
     potential = v_ext + density / jnp.sqrt(1.0 + density * density)
     w_ref[...] = (f_ref[:rows, :].astype(F32) * potential).astype(BF16)
     blocks = lax.dot_general(w_ref[...], f_ref[:rows, :], contract, preferred_element_type=F32)
-    own_out[...] = jnp.zeros_like(own_out)
-    low_out[...] = jnp.zeros_like(low_out)
+    used = groups * functions
+    head = round_up(used, 8)
+    for out in (*own_outs, *low_outs):
+        out[used:, :] = jnp.zeros((out.shape[0] - used, LANES), F32)
     for c in range(sources):
         own = own_ref[c]
         mine = jnp.concatenate(
@@ -283,14 +286,15 @@
                 ],
                 axis=0,
             )
-            place = pl.ds(first * pairs, lanes)
-            if c < ways:
-                own_out[c, :functions, place] = picked
-            else:
-                low_out[c - ways, :functions, place] = picked
+            out = own_outs[c] if c < ways else low_outs[c - ways]
+            for i in range(lanes // LANES):
+                g = first // per + i
+                out[g * functions : (g + 1) * functions, :] = picked[:, i * LANES : (i + 1) * LANES]
         if c < ways:
             for h in range(planes):
-                own_out[c, 16 + h : 17 + h, :points] = density[:, h * points : (h + 1) * points]
+                own_outs[c][head + h : head + h + 1, :points] = density[
+                    :, h * points : (h + 1) * points
+                ]
 
 
 def final_kernel(dims, orb_ref, mine_ref, other_ref, *rest):
@@ -299,17 +303,21 @@
     message_refs = rest[:ways]
     density_out, blocks_out, density_ref, blocks_ref, pad_ref, sems = rest[ways:]
     orb = orb_ref[0]
+    per = LANES // pairs
+    groups = -(-functions // per)
+    head = round_up(groups * functions, 8)
     for k in range(ways):
         residue = lax.rem(orb + k, ways)
         for h in range(planes):
-            density_ref[pl.ds(h * ways + residue, 1), :] = message_refs[k][16 + h : 17 + h, :points]
+            density_ref[pl.ds(h * ways + residue, 1), :] = message_refs[k][
+                head + h : head + h + 1, :points
+            ]
     first = pltpu.make_async_copy(density_ref, density_out, sems.at[0])
     first.start()
     total = mine_ref[...] + other_ref[...]
-    per = LANES // pairs
     for t in range(functions):
         g, i = t // per, t % per
-        piece = total[:, g * LANES : (g + 1) * LANES]
+        piece = total[g * functions : (g + 1) * functions]
         if i:
             piece = pltpu.roll(piece, LANES - i * pairs, 1)
         pad_ref[t] = piece
@@ -337,7 +345,6 @@
     band = 2 * ways * atoms
     per = LANES // pairs
     groups = -(-functions // per)
-    lanes = groups * LANES
     height = round_up(groups * functions + 3, 16)
     smem = pl.BlockSpec(memory_space=pltpu.SMEM)
     vmem = pl.BlockSpec(memory_space=pltpu.VMEM)
@@ -384,14 +391,13 @@
     rows = functions * band
     padded = round_up(rows, LANES)
     most = 256 // max(band, pairs)
-    own_part, low_part = pl.pallas_call(
+    head = round_up(groups * functions, 8)
+    parts = pl.pallas_call(
         functools.partial(main_kernel, dims),
-        out_shape=[
-            jax.ShapeDtypeStruct((ways, 16 + round_up(planes, 8), lanes), F32),
-            jax.ShapeDtypeStruct((ways, 16, lanes), F32),
-        ],
+        out_shape=[jax.ShapeDtypeStruct((head + round_up(planes, 8), LANES), F32)] * ways
+        + [jax.ShapeDtypeStruct((head, LANES), F32)] * ways,
         in_specs=[smem] + [vmem] * (1 + 2 * ways),
-        out_specs=[vmem] * 2,
+        out_specs=[vmem] * (2 * ways),
         scratch_shapes=[
             pltpu.VMEM((padded, planes * points), BF16),
             pltpu.VMEM((rows, planes * points), BF16),
@@ -404,14 +410,17 @@
         name="main",
     )(orb, v_ext, *sources)
 
-    from_above = moved_by(low_part, ("space",), (-1,))
-    total = own_part + jnp.pad(from_above, ((0, 0), (0, own_part.shape[1] - 16), (0, 0)))
-    messages = [total[0]]
-    mine = total[0, :16]
+    own_parts, low_parts = parts[:ways], parts[ways:]
+    messages, arrived = [own_parts[0]], []
+    for k in range(ways):
+        arrived.append(moved_by(low_parts[k], ("space", "orb"), (-1, -k)))
     for k in range(1, ways):
-        message = moved_by(total[k], ("orb",), (-k,))
-        messages.append(message)
-        mine = mine + message[:16]
+        messages.append(moved_by(own_parts[k], ("orb",), (-k,)))
+    mine = arrived[0]
+    for part in arrived[1:]:
+        mine = mine + part
+    for message in messages:
+        mine = mine + message[:head]
     shares = lax.axis_size("grid")
     other = moved_by(mine, ("grid",), (1,))
     for k in range(2, shares):
@@ -427,7 +436,7 @@
         scratch_shapes=[
             pltpu.VMEM((slab, points), F32),
             pltpu.VMEM((functions, functions, pairs), F32),
-            pltpu.VMEM((functions, 16, LANES), F32),
+            pltpu.VMEM((functions, functions, LANES), F32),
             pltpu.SemaphoreType.DMA((2,)),
         ],
         compiler_params=pltpu.CompilerParams(vmem_limit_bytes=4 << 20),

time: 27.3 us -> 27.1 us (level)
  waiting for transfers between devices: 13.2 us -> 12.6 us
  starting transfers between devices: 9.51 us -> 9.96 us
    ppermute x6 -> x7, waiting for transfers between devices: 13.2 us -> 12.6 us  [moved_by(): return lax.ppermute(value, axes if len(axes) > 1 else axes[0], pairs)]
    ppermute x6 -> x7, starting transfers between devices: 9.51 us -> 9.96 us  [moved_by(): return lax.ppermute(value, axes if len(axes) > 1 else axes[0], pairs)]
  transfers between devices with their start and end apart: 6 -> 7, of which waited for: 5 -> 5; matrix products, arithmetic and copies ran while one was open for 0% -> 0% of each run, Pallas kernels for 0% -> 0%
where the time goes in v3:
time: 27.1 us; the launch traced here: 26.9 us
  waiting for transfers between devices  12.6 us (46%)
  starting transfers between devices  9.96 us (37%)
  Pallas kernels  3.72 us (14%)
  between operations  0.68 us (3%)
    ppermute x7, waiting for transfers between devices, moved_by(): return lax.ppermute(value, axes if len(axes) > 1 else axes[0], pairs)  12.6 us
    ppermute x7, starting transfers between devices, moved_by(): return lax.ppermute(value, axes if len(axes) > 1 else axes[0], pairs)  9.96 us
    pallas_call x1, Pallas kernels, on_device(): pl.pallas_call(functools.partial(main_kernel, dims), out_shape=[jax.Shape...  1.62 us
    pallas_call x1, Pallas kernels, on_device(): pl.pallas_call(functools.partial(pack_kernel, dims), out_shape=[jax.Shape...  1.37 us
    pallas_call x1, Pallas kernels, on_device(): pl.pallas_call(functools.partial(final_kernel, dims), out_shape=[jax.Shap...  0.73 us
  transfers between devices with their start and end apart: 7, of which 5 were waited for; matrix products, arithmetic and copies ran while one was open for 0% of the time, Pallas kernels for 0%

profile of v3, /device:TPU:0, one launch (start us, length us, event | category | flops | bytes accessed | tf_op | source)
XLA Modules:
  0.0 26.9 jit_solution(6972386893835069178)
XLA Ops:
  0.6 0.0 copy-start
  0.6 1.4 %pack.1 = (bf16[9,72,128]{2,1,0:T(8,128)(2,1)S(1)}, bf16[9,72,128]{2,1,0:T(8,128)(2,1)S(1)}, bf16[8,72,128]{2,1,0:T(8,128)(2,1)S(1)}, bf16[8,72,128]{2,1,0:T(8,128)(2,1)S(1)}) custom-call(s32[1]{0:T(128)} %bitcast.orb_ref, s32[1]{0:T(128)} %bitcast.1.domain_ref, s32[8]{0:T(128)} %rest_0_.1, bf16[9,15,8,128]{3,2,1,0:T(8,128)(2,1)} %bitcast.8, ...), custom_call_target="tpu_custom_call" | custom-call | tf_op jit(solution)/shard_map/pack/pallas_call | solution.py:353
  2.0 3.0 %collective-permute-start = (bf16[9,72,128]{2,1,0:T(8,128)(2,1)S(1)}, bf16[9,72,128]{2,1,0:T(8,128)(2,1)S(1)}, u32[]{:S(2)}, u32[]{:S(2)}) collective-permute-start(bf16[9,72,128]{2,1,0:T(8,128)(2,1)S(1)} %get-tuple-element.13), channel_id=1, source_target_pairs={{0,2},{2,0},{1,3},{3,1},{4,6},{6,4},{5,7},{7,5},{8,10},{10,8},{9,1... | collective-permute-start | bytes 497672 | tf_op jit(solution)/shard_map/ppermute | solution.py:31
  5.1 1.6 %collective-permute-start.1 = (bf16[8,72,128]{2,1,0:T(8,128)(2,1)S(1)}, bf16[8,72,128]{2,1,0:T(8,128)(2,1)S(1)}, u32[]{:S(2)}, u32[]{:S(2)}) collective-permute-start(bf16[8,72,128]{2,1,0:T(8,128)(2,1)S(1)} %get-tuple-element.14), channel_id=1, source_target_pairs={{0,4},{2,6},{4,8},{6,10},{8,12},{10,14},{12,0},{14,2},{1,5},{3,7},... | collective-permute-start | bytes 442376 | tf_op jit(solution)/shard_map/ppermute | solution.py:31
  6.6 1.5 %collective-permute-start.2 = (bf16[8,72,128]{2,1,0:T(8,128)(2,1)S(1)}, bf16[8,72,128]{2,1,0:T(8,128)(2,1)S(1)}, u32[]{:S(2)}, u32[]{:S(2)}) collective-permute-start(bf16[8,72,128]{2,1,0:T(8,128)(2,1)S(1)} %get-tuple-element.15), channel_id=1, source_target_pairs={{0,6},{2,4},{4,10},{6,8},{8,14},{10,12},{12,2},{14,0},{1,7},{3,5},... | collective-permute-start | bytes 442376 | tf_op jit(solution)/shard_map/ppermute | solution.py:31
  8.2 5.4 %collective-permute-done.1.rest_2_ = bf16[8,72,128]{2,1,0:T(8,128)(2,1)S(1)} collective-permute-done((bf16[8,72,128]{2,1,0:T(8,128)(2,1)S(1)}, bf16[8,72,128]{2,1,0:T(8,128)(2,1)S(1)}, u32[]{:S(2)}, u32[]{:S(2)}) %collective-permute-start.1) | collective-permute-done | bytes 147488 | tf_op jit(solution)/shard_map/ppermute | solution.py:31
  13.6 1.8 %collective-permute-done.2.rest_3_ = bf16[8,72,128]{2,1,0:T(8,128)(2,1)S(1)} collective-permute-done((bf16[8,72,128]{2,1,0:T(8,128)(2,1)S(1)}, bf16[8,72,128]{2,1,0:T(8,128)(2,1)S(1)}, u32[]{:S(2)}, u32[]{:S(2)}) %collective-permute-start.2) | collective-permute-done | bytes 147488 | tf_op jit(solution)/shard_map/ppermute | solution.py:31
  15.4 0.0 collective-permute-done.rest_1_
  15.4 0.0 copy-done
  15.4 1.6 %main.1 = (f32[40,128]{1,0:T(8,128)S(1)}, f32[40,128]{1,0:T(8,128)S(1)}, f32[32,128]{1,0:T(8,128)S(1)}, f32[32,128]{1,0:T(8,128)S(1)}) custom-call(s32[1]{0:T(128)} %bitcast.orb_ref, f32[16,128]{1,0:T(8,128)S(1)} %copy-done, bf16[9,72,128]{2,1,0:T(8,128)(2,1)S(1)} %get-tuple-element.12.rest_0_, bf16[9,72,128]{2,1,0:T(8,128)(2,1)S(1)} %collective-permute-done.rest_1_, ...), custom_call_target="tpu_custom_call" | custom-call | tf_op jit(solution)/shard_map/main/pallas_call | solution.py:395
  17.0 1.6 %collective-permute-start.5 = (f32[40,128]{1,0:T(8,128)S(1)}, f32[40,128]{1,0:T(8,128)S(1)}, u32[]{:S(2)}, u32[]{:S(2)}) collective-permute-start(f32[40,128]{1,0:T(8,128)S(1)} %get-tuple-element.19), channel_id=1, source_target_pairs={{0,2},{2,0},{1,3},{3,1},{4,6},{6,4},{5,7},{7,5},{8,10},{10,8},{9,1... | collective-permute-start | bytes 61448 | tf_op jit(solution)/shard_map/ppermute | solution.py:31
  18.5 1.7 %collective-permute-start.3 = (f32[32,128]{1,0:T(8,128)S(1)}, f32[32,128]{1,0:T(8,128)S(1)}, u32[]{:S(2)}, u32[]{:S(2)}) collective-permute-start(f32[32,128]{1,0:T(8,128)S(1)} %get-tuple-element.16), channel_id=1, source_target_pairs={{0,12},{2,14},{4,0},{6,2},{8,4},{10,6},{12,8},{14,10},{1,13},{3,15... | collective-permute-start | bytes 49160 | tf_op jit(solution)/shard_map/ppermute | solution.py:31
  20.3 0.4 %collective-permute-start.4 = (f32[32,128]{1,0:T(8,128)S(1)}, f32[32,128]{1,0:T(8,128)S(1)}, u32[]{:S(2)}, u32[]{:S(2)}) collective-permute-start(f32[32,128]{1,0:T(8,128)S(1)} %get-tuple-element.17), channel_id=1, source_target_pairs={{0,14},{2,12},{4,2},{6,0},{8,6},{10,4},{12,10},{14,8},{1,15},{3,13... | collective-permute-start | bytes 49160 | tf_op jit(solution)/shard_map/ppermute | solution.py:31
  20.7 1.6 %collective-permute-done.3 = f32[32,128]{1,0:T(8,128)S(1)} collective-permute-done((f32[32,128]{1,0:T(8,128)S(1)}, f32[32,128]{1,0:T(8,128)S(1)}, u32[]{:S(2)}, u32[]{:S(2)}) %collective-permute-start.3) | collective-permute-done | bytes 16416 | tf_op jit(solution)/shard_map/ppermute | solution.py:31
  22.3 2.6 %collective-permute-done.4 = f32[32,128]{1,0:T(8,128)S(1)} collective-permute-done((f32[32,128]{1,0:T(8,128)S(1)}, f32[32,128]{1,0:T(8,128)S(1)}, u32[]{:S(2)}, u32[]{:S(2)}) %collective-permute-start.4) | collective-permute-done | bytes 16416 | tf_op jit(solution)/shard_map/ppermute | solution.py:31
  24.9 0.0 collective-permute-done.5.rest_1_
  24.9 0.1 collective-permute-start.6
  25.0 1.2 %collective-permute-done.6.other_ref = f32[32,128]{1,0:T(8,128)S(1)} collective-permute-done((f32[32,128]{1,0:T(8,128)S(1)}, f32[32,128]{1,0:T(8,128)S(1)}, u32[]{:S(2)}, u32[]{:S(2)}) %collective-permute-start.6) | collective-permute-done | bytes 16416 | tf_op jit(solution)/shard_map/ppermute | solution.py:31
  26.2 0.7 %final.1 = (f32[16,128]{1,0:T(8,128)}, f32[9,9,32]{2,1,0:T(8,128)}) custom-call(s32[1]{0:T(128)} %bitcast.orb_ref, f32[32,128]{1,0:T(8,128)S(1)} %slice_add_fusion.mine_ref, f32[32,128]{1,0:T(8,128)S(1)} %collective-permute-done.6.other_ref, f32[40,128]{1,0:T(8,128)S(1)} %get-tuple-element.18.rest_0_, f32[40,128]{1,0:T(8,128)S(1)} %collective-permute-done.5.rest_1_), custom_call_target="tpu_custom_call" | custom-call | tf_op jit(solution)/shard_map/final/pallas_call | solution.py:428
  (1 shorter events, 0.0 us)
Async XLA Ops:
  0.6 14.7 %copy-start = (f32[16,128]{1,0:T(8,128)S(1)}, f32[16,128]{1,0:T(8,128)}, u32[]{:S(2)}) copy-start(f32[16,128]{1,0:T(8,128)} %v_ref.1) | copy-start | bytes 24580
  2.0 13.3 %collective-permute-start = (bf16[9,72,128]{2,1,0:T(8,128)(2,1)S(1)}, bf16[9,72,128]{2,1,0:T(8,128)(2,1)S(1)}, u32[]{:S(2)}, u32[]{:S(2)}) collective-permute-start(bf16[9,72,128]{2,1,0:T(8,128)(2,1)S(1)} %get-tuple-element.13), channel_id=1, source_target_pairs={{0,2},{2,0},{1,3},{3,1},{4,6},{6,4},{5,7},{7,5},{8,10},{10,8},{9,1... | collective-permute-start | bytes 497672 | tf_op jit(solution)/shard_map/ppermute | solution.py:31
  5.1 8.5 %collective-permute-start.1 = (bf16[8,72,128]{2,1,0:T(8,128)(2,1)S(1)}, bf16[8,72,128]{2,1,0:T(8,128)(2,1)S(1)}, u32[]{:S(2)}, u32[]{:S(2)}) collective-permute-start(bf16[8,72,128]{2,1,0:T(8,128)(2,1)S(1)} %get-tuple-element.14), channel_id=1, source_target_pairs={{0,4},{2,6},{4,8},{6,10},{8,12},{10,14},{12,0},{14,2},{1,5},{3,7},... | collective-permute-start | bytes 442376 | tf_op jit(solution)/shard_map/ppermute | solution.py:31
  6.6 8.7 %collective-permute-start.2 = (bf16[8,72,128]{2,1,0:T(8,128)(2,1)S(1)}, bf16[8,72,128]{2,1,0:T(8,128)(2,1)S(1)}, u32[]{:S(2)}, u32[]{:S(2)}) collective-permute-start(bf16[8,72,128]{2,1,0:T(8,128)(2,1)S(1)} %get-tuple-element.15), channel_id=1, source_target_pairs={{0,6},{2,4},{4,10},{6,8},{8,14},{10,12},{12,2},{14,0},{1,7},{3,5},... | collective-permute-start | bytes 442376 | tf_op jit(solution)/shard_map/ppermute | solution.py:31
  17.0 7.9 %collective-permute-start.5 = (f32[40,128]{1,0:T(8,128)S(1)}, f32[40,128]{1,0:T(8,128)S(1)}, u32[]{:S(2)}, u32[]{:S(2)}) collective-permute-start(f32[40,128]{1,0:T(8,128)S(1)} %get-tuple-element.19), channel_id=1, source_target_pairs={{0,2},{2,0},{1,3},{3,1},{4,6},{6,4},{5,7},{7,5},{8,10},{10,8},{9,1... | collective-permute-start | bytes 61448 | tf_op jit(solution)/shard_map/ppermute | solution.py:31
  18.5 3.7 %collective-permute-start.3 = (f32[32,128]{1,0:T(8,128)S(1)}, f32[32,128]{1,0:T(8,128)S(1)}, u32[]{:S(2)}, u32[]{:S(2)}) collective-permute-start(f32[32,128]{1,0:T(8,128)S(1)} %get-tuple-element.16), channel_id=1, source_target_pairs={{0,12},{2,14},{4,0},{6,2},{8,4},{10,6},{12,8},{14,10},{1,13},{3,15... | collective-permute-start | bytes 49160 | tf_op jit(solution)/shard_map/ppermute | solution.py:31
  20.3 4.6 %collective-permute-start.4 = (f32[32,128]{1,0:T(8,128)S(1)}, f32[32,128]{1,0:T(8,128)S(1)}, u32[]{:S(2)}, u32[]{:S(2)}) collective-permute-start(f32[32,128]{1,0:T(8,128)S(1)} %get-tuple-element.17), channel_id=1, source_target_pairs={{0,14},{2,12},{4,2},{6,0},{8,6},{10,4},{12,10},{14,8},{1,15},{3,13... | collective-permute-start | bytes 49160 | tf_op jit(solution)/shard_map/ppermute | solution.py:31
  24.9 1.2 %collective-permute-start.6 = (f32[32,128]{1,0:T(8,128)S(1)}, f32[32,128]{1,0:T(8,128)S(1)}, u32[]{:S(2)}, u32[]{:S(2)}) collective-permute-start(f32[32,128]{1,0:T(8,128)S(1)} %slice_add_fusion.mine_ref), channel_id=1, source_target_pairs={{0,1},{1,0},{2,3},{3,2},{4,5},{5,4},{6,7},{7,6},{8,9},{9,8},{10,11... | collective-permute-start | bytes 49160 | tf_op jit(solution)/shard_map/ppermute | solution.py:31

commit v4 on v3

v4 whole, which is shorter than its diff:
```python
import functools

import jax
import jax.numpy as jnp
from jax import lax
from jax.experimental import pallas as pl
from jax.experimental.pallas import tpu as pltpu
from jax.sharding import PartitionSpec as P


LANES = 128
F32 = jnp.float32
BF16 = jnp.bfloat16


def moved_by(value, axes, steps):
    sizes = [lax.axis_size(axis) for axis in axes]
    pairs = []
    total = 1
    for size in sizes:
        total *= size
    for source in range(total):
        rest, place = source, []
        for size in reversed(sizes):
            place.insert(0, rest % size)
            rest //= size
        target = 0
        for size, here, step in zip(sizes, place, steps):
            target = target * size + (here + step) % size
        pairs.append((source, target))
    return lax.ppermute(value, axes if len(axes) > 1 else axes[0], pairs)


def round_up(count, unit):
    return (count + unit - 1) // unit * unit


def fixed(value):
    return pltpu.with_memory_space_constraint(value, pltpu.HBM)


def pieces_of(functions, pairs):
    per = LANES // pairs
    full = functions // per * per
    places = {}
    for t in range(full):
        for s in range(functions):
            places[t, s] = (t // per * functions + s, t % per)
    count = full * functions
    for t in range(full, functions):
        for s in range(functions):
            places[t, s] = (count // per, count % per)
            count += 1
    for name in range(3):
        places[name] = (count // per, count % per)
        count += 1
    return places, round_up(-(-count // per), 8)


def plane_masks(atoms, points, slab, ways, repeat, anchor_ref, residues):
    rows = atoms * repeat
    row = lax.broadcasted_iota(jnp.int32, (rows, points), 0)
    offset = jnp.zeros((rows, points), jnp.int32)
    for a in range(atoms):
        here = row == a
        for i in range(1, repeat):
            here = here | (row == a + i * atoms)
        offset = jnp.where(here, lax.rem(anchor_ref[a], slab), offset)
    planes = slab // ways
    found = []
    for residue in residues:
        start = offset - residue
        shift = jnp.zeros((rows, points), jnp.int32)
        for low in range(planes):
            shift = shift + (start > low * ways).astype(jnp.int32)
        phase = (shift * ways - start).astype(F32).astype(BF16)
        bits, size = [], 1
        while size <= planes:
            if size % planes:
                bit = ((shift & size) != 0).astype(F32).astype(BF16)
                bits.append((size, bit > 0.5))
            size *= 2
        level = shift.astype(F32).astype(BF16)
        found.append(
            (
                [phase == float(e) for e in range(ways - 1)],
                bits,
                [level <= float(h) for h in range(planes)],
            )
        )
    return found


def pack_kernel(dims, *rest):
    atoms, functions, depth, points, slab, ways, reach, pairs, space = dims
    given, rest = rest[:6], rest[6:]
    own_refs, next_refs = rest[:ways], rest[ways : 2 * ways]
    k_pad, row_pad, *held, x_sem, sems = rest[2 * ways :]
    anchor_ref, x_ref, k_ref, owner_ref, partner_ref, live_ref = held
    block = functions * atoms
    copies = [
        pltpu.make_async_copy(given[i], held[i], sems.at[i]) for i in range(6) if i != 1
    ]
    x_copies = [
        pltpu.make_async_copy(
            given[1].at[s], x_ref.at[:, pl.ds(s * atoms, atoms), :], x_sem.at[s]
        )
        for s in range(functions)
    ]
    copies[0].start()
    for copy in x_copies:
        copy.start()
    for copy in copies[1:]:
        copy.start()
    k_pad[...] = jnp.zeros_like(k_pad)
    row_pad[...] = jnp.zeros_like(row_pad)
    planes = slab // ways
    orb, domain = lax.axis_index("orb"), lax.axis_index("space")
    copies[0].wait()
    residues = [lax.rem(orb + k, ways) for k in range(ways)]
    first = 0
    masks = {}
    while first < functions:
        repeat = min(2, functions - first)
        if repeat not in masks:
            masks[repeat] = plane_masks(atoms, points, slab, ways, repeat, anchor_ref, residues)
        for s in range(first, first + repeat):
            x_copies[s].wait()
        rows = atoms * repeat
        zero = jnp.zeros((rows, points), BF16)
        tiles = [x_ref[j, first * atoms : first * atoms + rows, :] for j in range(depth)]
        tiles = tiles + [zero] * (planes * ways - depth)
        for k in range(ways):
            phases, bits, levels = masks[repeat][k]
            line = []
            for m in range(planes):
                pick = tiles[m * ways + ways - 1]
                for e in reversed(range(ways - 1)):
                    pick = jnp.where(phases[e], tiles[m * ways + e], pick)
                line.append(pick)
            for size, mask in bits:
                line = [jnp.where(mask, line[(h - size) % planes], line[h]) for h in range(planes)]
            for h in range(planes):
                place = h * block + first * atoms
                own_refs[k][place : place + rows, :] = jnp.where(levels[h], line[h], zero)
                if h < reach:
                    next_refs[k][place : place + rows, :] = jnp.where(levels[h], zero, line[h])
        first += repeat
    for copy in copies[1:]:
        copy.wait()
    places, height = pieces_of(functions, pairs)
    k_pad[0:functions, :functions, :pairs] = k_ref[...]
    per_domain = atoms * ways
    owner = owner_ref[...] - (domain * ways + orb) * atoms
    partner = partner_ref[...]
    home = jnp.floor((partner.astype(F32) + 0.5) * (1.0 / per_domain)).astype(jnp.int32)
    relative = home - domain + 1
    relative = jnp.where(relative < 0, relative + space, relative)
    relative = jnp.where(relative >= space, relative - space, relative)
    code = relative * per_domain + partner - home * per_domain
    k_pad[functions, 0:1, :pairs] = owner.astype(F32)
    k_pad[functions, 1:2, :pairs] = live_ref[...].astype(F32)
    k_pad[functions, 2:3, :pairs] = code.astype(F32)
    lines = {}
    for name, (row, column) in places.items():
        if isinstance(name, tuple):
            piece = k_pad[name[1], name[0] : name[0] + 1, :]
        else:
            piece = k_pad[functions, name : name + 1, :]
        piece = pltpu.roll(piece, column * pairs, 1) if column else piece
        lines[row] = lines[row] + piece if row in lines else piece
    for row, line in lines.items():
        row_pad[row : row + 1, :] = line
    info = row_pad[...]
    high = info.astype(BF16)
    low = (info - high.astype(F32)).astype(BF16)
    for refs, last in ((own_refs, planes), (next_refs, reach)):
        for k in range(ways):
            refs[k][last * block : last * block + height, :] = high
            refs[k][last * block + height : last * block + 2 * height, :] = low


def spans_of(functions, pairs, band):
    most = 256 // max(band, pairs)
    spans, first = [], 0
    while first < functions:
        count = min(most, functions - first)
        spans.append((first, count, round_up(count * pairs, LANES)))
        first += count
    return spans, (most * band, round_up(most * pairs, LANES))


def lined(rows, place, pairs):
    row, column = place
    line = rows[row : row + 1, :]
    return pltpu.roll(line, LANES - column * pairs, 1) if column else line


def fill_source(dims, c, source_ref, f_ref, d_ref, table_ref, own_ref):
    atoms, functions, _, points, slab, ways, _, pairs, _ = dims
    orb = lax.axis_index("orb")
    planes = slab // ways
    sources = 2 * ways
    block = functions * atoms
    band = sources * atoms
    padded = f_ref.shape[0]
    per = LANES // pairs
    places, height = pieces_of(functions, pairs)
    spans, size = spans_of(functions, pairs, band)
    per_domain = atoms * ways
    contract = (((1,), (1,)), ((), ()))
    last = (source_ref.shape[0] - 2 * height) // block
    for h in range(planes):
        for s in range(functions):
            place = (pl.ds((s * sources + c) * atoms, atoms), pl.ds(h * points, points))
            if h < last:
                f_ref[place] = source_ref[h * block + s * atoms : h * block + (s + 1) * atoms, :]
            else:
                f_ref[place] = jnp.zeros((atoms, points), BF16)
    row_id = lax.broadcasted_iota(jnp.int32, size, 0)
    lane_id = lax.broadcasted_iota(jnp.int32, (1, size[1]), 1)
    function_id = jnp.zeros((1, size[1]), jnp.int32)
    for t in range(1, size[1] // pairs):
        function_id = function_id + (lane_id >= t * pairs).astype(jnp.int32)
    atom_id = lax.broadcasted_iota(jnp.int32, (atoms, LANES), 0)
    pair_high = source_ref[last * block : last * block + height, :].astype(F32)
    pair_low = source_ref[last * block + height : last * block + 2 * height, :].astype(F32)
    row_lane = lax.broadcasted_iota(jnp.int32, (1, LANES), 1)
    wide = []
    for name in range(3):
        row, column = places[name]
        piece = pair_high[row : row + 1, :]
        piece = jnp.where(
            (row_lane >= column * pairs) & (row_lane < (column + 1) * pairs), piece, 0.0
        )
        line = piece
        for i in range(1, per):
            line = line + pltpu.roll(piece, i * pairs, 1)
        wide.append(line)
    owner, live, code = wide[0].astype(jnp.int32), wide[1], wide[2].astype(jnp.int32)
    domain = (code >= per_domain).astype(jnp.int32) + (code >= 2 * per_domain).astype(jnp.int32)
    inside = code - domain * per_domain
    orb_of = jnp.zeros(code.shape, jnp.int32)
    for i in range(1, ways):
        orb_of = orb_of + (inside >= i * atoms).astype(jnp.int32)
    local = inside - orb_of * atoms
    slot = orb - orb_of
    slot = jnp.where(slot < 0, slot + ways, slot)
    if c < ways:
        slot = slot + jnp.where(domain == 0, ways, 0)
        valid = domain <= 1
    else:
        slot = slot + jnp.where(domain == 1, ways, 0)
        valid = domain >= 1
    inner = jnp.where(valid, slot * atoms + local, -padded * LANES)
    inner = jnp.concatenate([inner] * (size[1] // LANES), axis=1)
    target = inner + function_id * band
    table_ref[c] = jnp.where(row_id == target, 1.0, 0.0).astype(BF16)
    own = jnp.where(atom_id == owner, live, 0.0)
    own_ref[c] = own
    for first, count, lanes in spans:
        parts = []
        for pair_rows in (pair_high, pair_low):
            for s in range(functions):
                parts.append(
                    jnp.concatenate(
                        [
                            lined(pair_rows, places[g * per, s], pairs) * own
                            for g in range(first // per, first // per + lanes // LANES)
                        ],
                        axis=1,
                    )
                )
        left = jnp.concatenate(parts, axis=0).astype(BF16)
        cols = count * band
        part = lax.dot_general(
            left, table_ref[c, :cols, :lanes], contract, preferred_element_type=F32
        )
        part = part[:block] + part[block:]
        high = part.astype(BF16)
        low = (part - high.astype(F32)).astype(BF16)
        for s in range(functions):
            place = pl.ds((s * sources + c) * atoms, atoms)
            d_ref[place, first * band : first * band + cols] = high[s * atoms : (s + 1) * atoms]
            d_ref[place, padded + first * band : padded + first * band + cols] = low[
                s * atoms : (s + 1) * atoms
            ]


def first_kernel(dims, source_ref, f_ref, d_ref, table_ref, own_ref):
    rows, padded = d_ref.shape[0], f_ref.shape[0]
    if padded > rows:
        f_ref[rows:, :] = jnp.zeros((padded - rows, f_ref.shape[1]), BF16)
    tail = rows // LANES * LANES
    if padded > tail:
        d_ref[:, tail:padded] = jnp.zeros((rows, padded - tail), BF16)
        d_ref[:, padded + tail :] = jnp.zeros((rows, padded - tail), BF16)
    fill_source(dims, 0, source_ref, f_ref, d_ref, table_ref, own_ref)


def next_kernel(dims, c, source_ref, *rest):
    fill_source(dims, c, source_ref, *rest[4:])


def main_kernel(dims, c, v_ref, source_ref, *rest):
    atoms, functions, _, points, slab, ways, _, pairs, _ = dims
    planes = slab // ways
    sources = 2 * ways
    rest = rest[4:]
    own_outs, low_outs = rest[:ways], rest[ways : 2 * ways]
    f_ref, d_ref, table_ref, own_ref, w_ref = rest[2 * ways :]
    block = functions * atoms
    band = sources * atoms
    rows = functions * band
    per = LANES // pairs
    groups = -(-functions // per)
    spans, _ = spans_of(functions, pairs, band)
    orb = lax.axis_index("orb")
    contract = (((1,), (1,)), ((), ()))
    fill_source(dims, c, source_ref, f_ref, d_ref, table_ref, own_ref)
    f_all = f_ref[...]
    aux = jnp.dot(d_ref[...], jnp.concatenate([f_all, f_all], axis=0), preferred_element_type=F32)
    density = jnp.sum(aux * f_ref[:rows, :].astype(F32), axis=0, keepdims=True)
    v_ext = jnp.concatenate([v_ref[pl.ds(h * ways + orb, 1), :] for h in range(planes)], axis=1)
    potential = v_ext + density / jnp.sqrt(1.0 + density * density)
    w_ref[...] = (f_ref[:rows, :].astype(F32) * potential).astype(BF16)
    blocks = lax.dot_general(w_ref[...], f_ref[:rows, :], contract, preferred_element_type=F32)
    used = groups * functions
    head = round_up(used, 8)
    for out in (*own_outs, *low_outs):
        out[used:, :] = jnp.zeros((out.shape[0] - used, LANES), F32)
    for c in range(sources):
        own = own_ref[c]
        mine = jnp.concatenate(
            [blocks[(s * sources + c) * atoms : (s * sources + c + 1) * atoms] for s in range(functions)],
            axis=0,
        )
        high = mine.astype(BF16)
        low = (mine - high.astype(F32)).astype(BF16)
        both = jnp.concatenate([high, low], axis=0)
        for first, count, lanes in spans:
            cols = count * band
            spread = jnp.dot(
                both[:, first * band : first * band + cols],
                table_ref[c, :cols, :lanes],
                preferred_element_type=F32,
            )
            spread = spread[:block] + spread[block:]
            owned = jnp.concatenate([own] * (lanes // LANES), axis=1)
            picked = jnp.concatenate(
                [
                    jnp.sum(spread[s * atoms : (s + 1) * atoms] * owned, axis=0, keepdims=True)
                    for s in range(functions)
                ],
                axis=0,
            )
            out = own_outs[c] if c < ways else low_outs[c - ways]
            for i in range(lanes // LANES):
                g = first // per + i
                out[g * functions : (g + 1) * functions, :] = picked[:, i * LANES : (i + 1) * LANES]
        if c < ways:
            for h in range(planes):
                own_outs[c][head + h : head + h + 1, :points] = density[
                    :, h * points : (h + 1) * points
                ]


def final_kernel(dims, mine_ref, other_ref, *rest):
    _, functions, _, points, slab, ways, _, pairs, _ = dims
    planes = slab // ways
    message_refs = rest[:ways]
    density_out, blocks_out, density_ref, blocks_ref, pad_ref, sems = rest[ways:]
    orb = lax.axis_index("orb")
    per = LANES // pairs
    groups = -(-functions // per)
    head = round_up(groups * functions, 8)
    for k in range(ways):
        residue = lax.rem(orb + k, ways)
        for h in range(planes):
            density_ref[pl.ds(h * ways + residue, 1), :] = message_refs[k][
                head + h : head + h + 1, :points
            ]
    first = pltpu.make_async_copy(density_ref, density_out, sems.at[0])
    first.start()
    total = mine_ref[...] + other_ref[...]
    for t in range(functions):
        g, i = t // per, t % per
        piece = total[g * functions : (g + 1) * functions]
        if i:
            piece = pltpu.roll(piece, LANES - i * pairs, 1)
        pad_ref[t] = piece
    for t in range(functions):
        for s in range(functions):
            blocks_ref[s, t : t + 1, :] = pad_ref[t, s : s + 1, :pairs]
    second = pltpu.make_async_copy(blocks_ref, blocks_out, sems.at[1])
    second.start()
    first.wait()
    second.wait()


def on_device(support, anchor, kernel, pair_owner, pair_partner, pair_live, v_ext):
    atoms, functions, depth, points = support.shape
    pairs = kernel.shape[0]
    slab = v_ext.shape[0]
    ways = lax.axis_size("orb")
    space = lax.axis_size("space")
    planes = slab // ways
    reach = min((depth - 2) // ways + 1, planes)
    dims = (atoms, functions, depth, points, slab, ways, reach, pairs, space)
    block = functions * atoms
    band = 2 * ways * atoms
    per = LANES // pairs
    groups = -(-functions // per)
    height = pieces_of(functions, pairs)[1]
    vmem = pl.BlockSpec(memory_space=pltpu.VMEM)
    hbm = pl.BlockSpec(memory_space=pltpu.HBM)

    packed = pl.pallas_call(
        functools.partial(pack_kernel, dims),
        out_shape=[jax.ShapeDtypeStruct((planes * block + 2 * height, points), BF16)] * ways
        + [jax.ShapeDtypeStruct((reach * block + 2 * height, points), BF16)] * ways,
        in_specs=[hbm] * 6,
        out_specs=[vmem] * (2 * ways),
        scratch_shapes=[
            pltpu.VMEM((functions + 1, 16, LANES), F32),
            pltpu.VMEM((height, LANES), F32),
            pltpu.SMEM((atoms,), jnp.int32),
            pltpu.VMEM((depth, block, points), BF16),
            pltpu.VMEM((functions, functions, pairs), F32),
            pltpu.VMEM((1, pairs), jnp.int32),
            pltpu.VMEM((1, pairs), jnp.int32),
            pltpu.VMEM((1, pairs), jnp.int32),
            pltpu.SemaphoreType.DMA((functions,)),
            pltpu.SemaphoreType.DMA((6,)),
        ],
        compiler_params=pltpu.CompilerParams(vmem_limit_bytes=8 << 20),
        name="pack",
    )(
        fixed(anchor),
        fixed(support.transpose(1, 2, 0, 3)),
        fixed(kernel.transpose(1, 2, 0)),
        fixed(pair_owner.reshape(1, pairs)),
        fixed(pair_partner.reshape(1, pairs)),
        fixed(pair_live.reshape(1, pairs)),
    )
    own, onward = packed[:ways], packed[ways:]
    upper, peers = [], []
    for k in range(ways):
        upper.append(moved_by(onward[k], ("space", "orb"), (1, k)))
    for k in range(1, ways):
        peers.append(moved_by(own[k], ("orb",), (k,)))
    sources = [own[0]] + peers + upper

    rows = functions * band
    padded = round_up(rows, LANES)
    size = spans_of(functions, pairs, band)[1]
    head = round_up(groups * functions, 8)
    order = [0] + [ways] + list(range(1, ways)) + [ways + k for k in range(1, ways)]
    kept = [
        pltpu.VMEM((padded, planes * points), BF16),
        pltpu.VMEM((rows, 2 * padded), BF16),
        pltpu.VMEM((2 * ways, *size), BF16),
        pltpu.VMEM((2 * ways, atoms, LANES), F32),
    ]
    held = pl.pallas_call(
        functools.partial(first_kernel, dims),
        out_shape=kept,
        in_specs=[vmem],
        out_specs=[vmem] * 4,
        compiler_params=pltpu.CompilerParams(vmem_limit_bytes=8 << 20),
        name="first",
    )(sources[0])
    for c in order[1:-1]:
        held = pl.pallas_call(
            functools.partial(next_kernel, dims, c),
            out_shape=kept,
            in_specs=[vmem] + [vmem] * 4,
            out_specs=[vmem] * 4,
            input_output_aliases={1 + i: i for i in range(4)},
            compiler_params=pltpu.CompilerParams(vmem_limit_bytes=8 << 20),
        )(sources[c], *held)
    parts = pl.pallas_call(
        functools.partial(main_kernel, dims, order[-1]),
        out_shape=[jax.ShapeDtypeStruct((head + round_up(planes, 8), LANES), F32)] * ways
        + [jax.ShapeDtypeStruct((head, LANES), F32)] * ways
        + kept,
        in_specs=[vmem] * 6,
        out_specs=[vmem] * (2 * ways + 4),
        scratch_shapes=[pltpu.VMEM((rows, planes * points), BF16)],
        input_output_aliases={2 + i: 2 * ways + i for i in range(4)},
        compiler_params=pltpu.CompilerParams(vmem_limit_bytes=20 << 20),
        name="main",
    )(v_ext, sources[order[-1]], *held)
    parts = parts[: 2 * ways]

    own_parts, low_parts = parts[:ways], parts[ways:]
    messages, arrived = [own_parts[0]], []
    for k in range(ways):
        arrived.append(moved_by(low_parts[k], ("space", "orb"), (-1, -k)))
    for k in range(1, ways):
        messages.append(moved_by(own_parts[k], ("orb",), (-k,)))
    mine = arrived[0]
    for part in arrived[1:]:
        mine = mine + part
    for message in messages:
        mine = mine + message[:head]
    shares = lax.axis_size("grid")
    other = moved_by(mine, ("grid",), (1,))
    for k in range(2, shares):
        other = other + moved_by(mine, ("grid",), (k,))
    density, blocks = pl.pallas_call(
        functools.partial(final_kernel, dims),
        out_shape=[
            jax.ShapeDtypeStruct((slab, points), F32),
            jax.ShapeDtypeStruct((functions, functions, pairs), F32),
        ],
        in_specs=[vmem] * (2 + ways),
        out_specs=[hbm] * 2,
        scratch_shapes=[
            pltpu.VMEM((slab, points), F32),
            pltpu.VMEM((functions, functions, pairs), F32),
            pltpu.VMEM((functions, functions, LANES), F32),
            pltpu.SemaphoreType.DMA((2,)),
        ],
        compiler_params=pltpu.CompilerParams(vmem_limit_bytes=4 << 20),
        name="final",
    )(mine, other, *messages)
    return (density, blocks.transpose(2, 0, 1))


def solution(mesh):
    placed = (
        P(("shift", "space", "orb"), None, None, "grid"),
        P(("shift", "space", "orb")),
        P(("shift", "space", "orb"), None, None),
        P(("shift", "space", "orb")),
        P(("shift", "space", "orb")),
        P(("shift", "space", "orb")),
        P(("shift", "space"), "grid"),
    )
    step = jax.shard_map(
        on_device,
        mesh=mesh,
        in_specs=placed,
        out_specs=(P(("shift", "space"), "grid"), P(("shift", "space", "orb"), None, None)),
        check_vma=False,
    )
    ways = mesh.shape["orb"]
    last = source_ref.shape[0] - 1
    for h in range(planes):
        for s in range(functions):
            place = (pl.ds((s * sources + c) * atoms, atoms), pl.ds(h * points, points))
            if h < last:
                f_ref[place] = source_ref[h * block + s * atoms : h * block + (s + 1) * atoms, :]
            else:
                f_ref[place] = jnp.zeros((atoms, points), BF16)
    row_id = lax.broadcasted_iota(jnp.int32, size, 0)
    lane_id = lax.broadcasted_iota(jnp.int32, (1, size[1]), 1)
    function_id = jnp.zeros((1, size[1]), jnp.int32)
    for t in range(1, size[1] // pairs):
        function_id = function_id + (lane_id >= t * pairs).astype(jnp.int32)
    atom_id = lax.broadcasted_iota(jnp.int32, (atoms, LANES), 0)
    base = groups * functions
    pair_high = source_ref[last, 0:height, :].astype(F32)
    pair_low = source_ref[last, height : 2 * height, :].astype(F32)
    owner = pair_high[base : base + 1, :].astype(jnp.int32)
    live = pair_high[base + 1 : base + 2, :]
    code = pair_high[base + 2 : base + 3, :].astype(jnp.int32)
    domain = (code >= per_domain).astype(jnp.int32) + (code >= 2 * per_domain).astype(jnp.int32)
    inside = code - domain * per_domain
    orb_of = jnp.zeros(code.shape, jnp.int32)
    for i in range(1, ways):
        orb_of = orb_of + (inside >= i * atoms).astype(jnp.int32)
    local = inside - orb_of * atoms
    slot = orb - orb_of
    slot = jnp.where(slot < 0, slot + ways, slot)
    if c < ways:
        slot = slot + jnp.where(domain == 0, ways, 0)
        valid = domain <= 1
    else:
        slot = slot + jnp.where(domain == 1, ways, 0)
        valid = domain >= 1
    inner = jnp.where(valid, slot * atoms + local, -padded * LANES)
    inner = jnp.concatenate([inner] * (size[1] // LANES), axis=1)
    target = inner + function_id * band
    table_ref[c] = jnp.where(row_id == target, 1.0, 0.0).astype(BF16)
    own = jnp.where(atom_id == owner, live, 0.0)
    own_ref[c] = own
    for first, count, lanes in spans:
        parts = []
        for pair_rows in (pair_high, pair_low):
            for s in range(functions):
                parts.append(
                    jnp.concatenate(
                        [
                            lined(pair_rows, places[g * per, s], pairs) * own
                            for g in range(first // per, first // per + lanes // LANES)
                        ],
                        axis=1,
                    )
                )
        left = jnp.concatenate(parts, axis=0).astype(BF16)
        cols = count * band
        part = lax.dot_general(
            left, table_ref[c, :cols, :lanes], contract, preferred_element_type=F32
        )
        part = part[:block] + part[block:]
        high = part.astype(BF16)
        low = (part - high.astype(F32)).astype(BF16)
        for s in range(functions):
            place = pl.ds((s * sources + c) * atoms, atoms)
            d_ref[place, first * band : first * band + cols] = high[s * atoms : (s + 1) * atoms]
            d_ref[place, padded + first * band : padded + first * band + cols] = low[
                s * atoms : (s + 1) * atoms
            ]


def first_kernel(dims, source_ref, f_ref, d_ref, table_ref, own_ref):
    rows, padded = d_ref.shape[0], f_ref.shape[0]
    if padded > rows:
        f_ref[rows:, :] = jnp.zeros((padded - rows, f_ref.shape[1]), BF16)
    tail = rows // LANES * LANES
    if padded > tail:
        d_ref[:, tail:padded] = jnp.zeros((rows, padded - tail), BF16)
        d_ref[:, padded + tail :] = jnp.zeros((rows, padded - tail), BF16)
    fill_source(dims, 0, source_ref, f_ref, d_ref, table_ref, own_ref)


def next_kernel(dims, c, source_ref, *rest):
    fill_source(dims, c, source_ref, *rest[4:])


def main_kernel(dims, c, v_ref, source_ref, *rest):
    atoms, functions, _, points, slab, ways, _, pairs, _ = dims
    planes = slab // ways
    sources = 2 * ways
    rest = rest[4:]
    own_outs, low_outs = rest[:ways], rest[ways : 2 * ways]
    f_ref, d_ref, table_ref, own_ref, w_ref = rest[2 * ways :]
    block = functions * atoms
    band = sources * atoms
    rows = functions * band
    per = LANES // pairs
    groups = -(-functions // per)
    spans, _ = spans_of(functions, pairs, band)
    orb = lax.axis_index("orb")
    contract = (((1,), (1,)), ((), ()))
    fill_source(dims, c, source_ref, f_ref, d_ref, table_ref, own_ref)
    f_all = f_ref[...]
    aux = jnp.dot(d_ref[...], jnp.concatenate([f_all, f_all], axis=0), preferred_element_type=F32)
    density = jnp.sum(aux * f_ref[:rows, :].astype(F32), axis=0, keepdims=True)
    v_ext = jnp.concatenate([v_ref[pl.ds(h * ways + orb, 1), :] for h in range(planes)], axis=1)
    potential = v_ext + density / jnp.sqrt(1.0 + density * density)
    w_ref[...] = (f_ref[:rows, :].astype(F32) * potential).astype(BF16)
    blocks = lax.dot_general(w_ref[...], f_ref[:rows, :], contract, preferred_element_type=F32)
    used = groups * functions
    head = round_up(used, 8)
    for out in (*own_outs, *low_outs):
        out[used:, :] = jnp.zeros((out.shape[0] - used, LANES), F32)
    for c in range(sources):
        own = own_ref[c]
        mine = jnp.concatenate(
            [blocks[(s * sources + c) * atoms : (s * sources + c + 1) * atoms] for s in range(functions)],
            axis=0,
        )
        high = mine.astype(BF16)
        low = (mine - high.astype(F32)).astype(BF16)
        both = jnp.concatenate([high, low], axis=0)
        for first, count, lanes in spans:
            cols = count * band
            spread = jnp.dot(
                both[:, first * band : first * band + cols],
                table_ref[c, :cols, :lanes],
                preferred_element_type=F32,
            )
            spread = spread[:block] + spread[block:]
            owned = jnp.concatenate([own] * (lanes // LANES), axis=1)
            picked = jnp.concatenate(
                [
                    jnp.sum(spread[s * atoms : (s + 1) * atoms] * owned, axis=0, keepdims=True)
                    for s in range(functions)
                ],
                axis=0,
            )
            out = own_outs[c] if c < ways else low_outs[c - ways]
            for i in range(lanes // LANES):
                g = first // per + i
                out[g * functions : (g + 1) * functions, :] = picked[:, i * LANES : (i + 1) * LANES]
        if c < ways:
            for h in range(planes):
                own_outs[c][head + h : head + h + 1, :points] = density[
                    :, h * points : (h + 1) * points
                ]


def final_kernel(dims, mine_ref, other_ref, *rest):
    _, functions, _, points, slab, ways, _, pairs, _ = dims
    planes = slab // ways
    message_refs = rest[:ways]
    density_out, blocks_out, density_ref, blocks_ref, pad_ref, sems = rest[ways:]
    orb = lax.axis_index("orb")
    per = LANES // pairs
    groups = -(-functions // per)
    head = round_up(groups * functions, 8)
    for k in range(ways):
        residue = lax.rem(orb + k, ways)
        for h in range(planes):
            density_ref[pl.ds(h * ways + residue, 1), :] = message_refs[k][
                head + h : head + h + 1, :points
            ]
    first = pltpu.make_async_copy(density_ref, density_out, sems.at[0])
    first.start()
    total = mine_ref[...] + other_ref[...]
    for t in range(functions):
        g, i = t // per, t % per
        piece = total[g * functions : (g + 1) * functions]
        if i:
            piece = pltpu.roll(piece, LANES - i * pairs, 1)
        pad_ref[t] = piece
    for t in range(functions):
        for s in range(functions):
            blocks_ref[s, t : t + 1, :] = pad_ref[t, s : s + 1, :pairs]
    second = pltpu.make_async_copy(blocks_ref, blocks_out, sems.at[1])
    second.start()
    first.wait()
    second.wait()


def on_device(support, anchor, kernel, pair_owner, pair_partner, pair_live, v_ext):
    atoms, functions, depth, points = support.shape
    pairs = kernel.shape[0]
    slab = v_ext.shape[0]
    ways = lax.axis_size("orb")
    space = lax.axis_size("space")
    planes = slab // ways
    reach = min((depth - 2) // ways + 1, planes)
    dims = (atoms, functions, depth, points, slab, ways, reach, pairs, space)
    block = functions * atoms
    band = 2 * ways * atoms
    per = LANES // pairs
    groups = -(-functions // per)
    height = pieces_of(functions, pairs)[1]
    vmem = pl.BlockSpec(memory_space=pltpu.VMEM)
    hbm = pl.BlockSpec(memory_space=pltpu.HBM)

    packed = pl.pallas_call(
        functools.partial(pack_kernel, dims),
        out_shape=[jax.ShapeDtypeStruct((planes * block + 2 * height, points), BF16)] * ways
        + [jax.ShapeDtypeStruct((reach * block + 2 * height, points), BF16)] * ways,
        in_specs=[hbm] * 6,
        out_specs=[vmem] * (2 * ways),
        scratch_shapes=[
            pltpu.VMEM((functions + 1, 16, LANES), F32),
            pltpu.VMEM((height, LANES), F32),
            pltpu.SMEM((atoms,), jnp.int32),
            pltpu.VMEM((depth, block, points), BF16),
            pltpu.VMEM((functions, functions, pairs), F32),
            pltpu.VMEM((1, pairs), jnp.int32),
            pltpu.VMEM((1, pairs), jnp.int32),
            pltpu.VMEM((1, pairs), jnp.int32),
            pltpu.SemaphoreType.DMA((functions,)),
            pltpu.SemaphoreType.DMA((6,)),
        ],
        compiler_params=pltpu.CompilerParams(vmem_limit_bytes=8 << 20),
        name="pack",
    )(
        fixed(anchor),
        fixed(support.transpose(1, 2, 0, 3)),
        fixed(kernel.transpose(1, 2, 0)),
        fixed(pair_owner.reshape(1, pairs)),
        fixed(pair_partner.reshape(1, pairs)),
        fixed(pair_live.reshape(1, pairs)),
    )
    own, onward = packed[:ways], packed[ways:]
    upper, peers = [], []
    for k in range(ways):
        upper.append(moved_by(onward[k], ("space", "orb"), (1, k)))
    for k in range(1, ways):
        peers.append(moved_by(own[k], ("orb",), (k,)))
    sources = [own[0]] + peers + upper

    rows = functions * band
    padded = round_up(rows, LANES)
    size = spans_of(functions, pairs, band)[1]
    head = round_up(groups * functions, 8)
    order = [0] + [ways] + list(range(1, ways)) + [ways + k for k in range(1, ways)]
    kept = [
        pltpu.VMEM((padded, planes * points), BF16),
        pltpu.VMEM((rows, 2 * padded), BF16),
        pltpu.VMEM((2 * ways, *size), BF16),
        pltpu.VMEM((2 * ways, atoms, LANES), F32),
    ]
    held = pl.pallas_call(
        functools.partial(first_kernel, dims),
        out_shape=kept,
        in_specs=[vmem],
        out_specs=[vmem] * 4,
        compiler_params=pltpu.CompilerParams(vmem_limit_bytes=8 << 20),
        name="first",
    )(sources[0])
    for c in order[1:-1]:
        held = pl.pallas_call(
            functools.partial(next_kernel, dims, c),
            out_shape=kept,
            in_specs=[vmem] + [vmem] * 4,
            out_specs=[vmem] * 4,
            input_output_aliases={1 + i: i for i in range(4)},
            compiler_params=pltpu.CompilerParams(vmem_limit_bytes=8 << 20),
        )(sources[c], *held)
    parts = pl.pallas_call(
        functools.partial(main_kernel, dims, order[-1]),
        out_shape=[jax.ShapeDtypeStruct((head + round_up(planes, 8), LANES), F32)] * ways
        + [jax.ShapeDtypeStruct((head, LANES), F32)] * ways
        + kept,
        in_specs=[vmem] * 6,
        out_specs=[vmem] * (2 * ways + 4),
        scratch_shapes=[pltpu.VMEM((rows, planes * points), BF16)],
        input_output_aliases={2 + i: 2 * ways + i for i in range(4)},
        compiler_params=pltpu.CompilerParams(vmem_limit_bytes=20 << 20),
        name="main",
    )(v_ext, sources[order[-1]], *held)
    parts = parts[: 2 * ways]

    own_parts, low_parts = parts[:ways], parts[ways:]
    messages, arrived = [own_parts[0]], []
    for k in range(ways):
        arrived.append(moved_by(low_parts[k], ("space", "orb"), (-1, -k)))
    for k in range(1, ways):
        messages.append(moved_by(own_parts[k], ("orb",), (-k,)))
    mine = arrived[0]
    for part in arrived[1:]:
        mine = mine + part
    for message in messages:
        mine = mine + message[:head]
    shares = lax.axis_size("grid")
    other = moved_by(mine, ("grid",), (1,))
    for k in range(2, shares):
        other = other + moved_by(mine, ("grid",), (k,))
    density, blocks = pl.pallas_call(
        functools.partial(final_kernel, dims),
        out_shape=[
            jax.ShapeDtypeStruct((slab, points), F32),
            jax.ShapeDtypeStruct((functions, functions, pairs), F32),
        ],
        in_specs=[vmem] * (2 + ways),
        out_specs=[hbm] * 2,
        scratch_shapes=[
            pltpu.VMEM((slab, points), F32),
            pltpu.VMEM((functions, functions, pairs), F32),
            pltpu.VMEM((functions, functions, LANES), F32),
            pltpu.SemaphoreType.DMA((2,)),
        ],
        compiler_params=pltpu.CompilerParams(vmem_limit_bytes=4 << 20),
        name="final",
    )(mine, other, *messages)
    return (density, blocks.transpose(2, 0, 1))


def solution(mesh):
    placed = (
        P(("shift", "space", "orb"), None, None, "grid"),
        P(("shift", "space", "orb")),
        P(("shift", "space", "orb"), None, None),
        P(("shift", "space", "orb")),
        P(("shift", "space", "orb")),
        P(("shift", "space", "orb")),
        P(("shift", "space"), "grid"),
    )
    return jax.shard_map(
        on_device,
        mesh=mesh,
        in_specs=placed,
        out_specs=(P(("shift", "space"), "grid"), P(("shift", "space", "orb"), None, None)),
        check_vma=False,
    )
```

time: 27.1 us -> 26.6 us (0.982)
  waiting for transfers between devices: 12.6 us -> 11.2 us
  Pallas kernels: 3.72 us -> 4.56 us
    ppermute x7, waiting for transfers between devices: 12.6 us -> 11.2 us  [moved_by(): return lax.ppermute(value, axes if len(axes) > 1 else axes[0], pairs)]
    pallas_call x1 -> x4, Pallas kernels: 1.62 us -> 2.53 us  [the longest x1 1.51 us: on_device(): pl.pallas_call(functools.partial(main_kernel, dims, order[-1]), out_shape...]
  transfers between devices with their start and end apart: 7 -> 7, of which waited for: 5 -> 5; matrix products, arithmetic and copies ran while one was open for 0% -> 0% of each run, Pallas kernels for 0% -> 4%
where the time goes in v4:
time: 26.6 us; the launch traced here: 26.5 us
  waiting for transfers between devices  11.2 us (42%)
  starting transfers between devices  9.95 us (37%)
  Pallas kernels  4.56 us (17%)
  between operations  0.7 us (3%)
    ppermute x7, waiting for transfers between devices, moved_by(): return lax.ppermute(value, axes if len(axes) > 1 else axes[0], pairs)  11.2 us
    ppermute x7, starting transfers between devices, moved_by(): return lax.ppermute(value, axes if len(axes) > 1 else axes[0], pairs)  9.95 us
    pallas_call x1, Pallas kernels, on_device(): pl.pallas_call(functools.partial(main_kernel, dims, order[-1]), out_shape...  1.51 us
    pallas_call x1, Pallas kernels, on_device(): pl.pallas_call(functools.partial(pack_kernel, dims), out_shape=[jax.Shape...  1.3 us
    pallas_call x1, Pallas kernels, on_device(): pl.pallas_call(functools.partial(final_kernel, dims), out_shape=[jax.Shap...  0.73 us
    pallas_call x2, Pallas kernels, on_device(): pl.pallas_call(functools.partial(next_kernel, dims, c), out_shape=kept, i...  0.68 us
  transfers between devices with their start and end apart: 7, of which 5 were waited for; matrix products, arithmetic and copies ran while one was open for 0% of the time, Pallas kernels for 4%

profile of v4, /device:TPU:0, one launch (start us, length us, event | category | flops | bytes accessed | tf_op | source)
XLA Modules:
  0.0 26.5 jit_solution(14648639998929847625)
XLA Ops:
  0.6 1.3 %pack.1 = (bf16[624,128]{1,0:T(8,128)(2,1)S(1)}, bf16[624,128]{1,0:T(8,128)(2,1)S(1)}, bf16[552,128]{1,0:T(8,128)(2,1)S(1)}, bf16[552,128]{1,0:T(8,128)(2,1)S(1)}) custom-call(s32[8]{0:T(128)} %rest_0_.1, bf16[9,15,8,128]{3,2,1,0:T(8,128)(2,1)} %bitcast.6, f32[9,9,32]{2,1,0:T(8,128)} %bitcast.7, s32[1,32]{1,0:T(1,128)} %bitcast.8, s32[1,32]{1,0:T(1,128)} %bitcast.9, ...), custom_call_target="tpu_custom_call" | custom-call | tf_op jit(solution)/shard_map/pack/pallas_call | solution.py:746
  1.9 3.0 %collective-permute-start.1 = (bf16[624,128]{1,0:T(8,128)(2,1)S(1)}, bf16[624,128]{1,0:T(8,128)(2,1)S(1)}, u32[]{:S(2)}, u32[]{:S(2)}) collective-permute-start(bf16[624,128]{1,0:T(8,128)(2,1)S(1)} %get-tuple-element.25), channel_id=1, source_target_pairs={{0,2},{2,0},{1,3},{3,1},{4,6},{6,4},{5,7},{7,5},{8,10},{10,8},{9,1... | collective-permute-start | bytes 479240 | tf_op jit(solution)/shard_map/ppermute | solution.py:31
  5.0 1.6 %collective-permute-start.2 = (bf16[552,128]{1,0:T(8,128)(2,1)S(1)}, bf16[552,128]{1,0:T(8,128)(2,1)S(1)}, u32[]{:S(2)}, u32[]{:S(2)}) collective-permute-start(bf16[552,128]{1,0:T(8,128)(2,1)S(1)} %get-tuple-element.26), channel_id=1, source_target_pairs={{0,4},{2,6},{4,8},{6,10},{8,12},{10,14},{12,0},{14,2},{1,5},{3,7},... | collective-permute-start | bytes 423944 | tf_op jit(solution)/shard_map/ppermute | solution.py:31
  6.5 1.5 %collective-permute-start = (bf16[552,128]{1,0:T(8,128)(2,1)S(1)}, bf16[552,128]{1,0:T(8,128)(2,1)S(1)}, u32[]{:S(2)}, u32[]{:S(2)}) collective-permute-start(bf16[552,128]{1,0:T(8,128)(2,1)S(1)} %get-tuple-element.24), channel_id=1, source_target_pairs={{0,6},{2,4},{4,10},{6,8},{8,14},{10,12},{12,2},{14,0},{1,7},{3,5},... | collective-permute-start | bytes 423944 | tf_op jit(solution)/shard_map/ppermute | solution.py:31
  8.1 0.3 %first.1 = (bf16[384,1024]{1,0:T(8,128)(2,1)S(1)}, bf16[288,768]{1,0:T(8,128)(2,1)S(1)}, bf16[4,256,256]{2,1,0:T(8,128)(2,1)S(1)}, f32[4,8,128]{2,1,0:T(8,128)S(1)}) custom-call(bf16[624,128]{1,0:T(8,128)(2,1)S(1)} %get-tuple-element.27.source_ref), custom_call_target="tpu_custom_call" | custom-call | tf_op jit(solution)/shard_map/first/pallas_call | solution.py:793
  8.4 4.9 %collective-permute-done.2.source_ref = bf16[552,128]{1,0:T(8,128)(2,1)S(1)} collective-permute-done((bf16[552,128]{1,0:T(8,128)(2,1)S(1)}, bf16[552,128]{1,0:T(8,128)(2,1)S(1)}, u32[]{:S(2)}, u32[]{:S(2)}) %collective-permute-start.2) | collective-permute-done | bytes 141344 | tf_op jit(solution)/shard_map/ppermute | solution.py:31
  13.4 0.3 %shard_map.86 = (bf16[384,1024]{1,0:T(8,128)(2,1)S(1)}, bf16[288,768]{1,0:T(8,128)(2,1)S(1)}, bf16[4,256,256]{2,1,0:T(8,128)(2,1)S(1)}, f32[4,8,128]{2,1,0:T(8,128)S(1)}) custom-call(bf16[552,128]{1,0:T(8,128)(2,1)S(1)} %collective-permute-done.2.source_ref, ...), custom_call_target="tpu_custom_call", output_to_operand_aliasing={{0}: (1, {}), {1}: (2, {}), {2}: (3, {}), {3}: (4, {})} | custom-call | tf_op jit(solution)/shard_map/pallas_call | solution.py:802
  13.7 0.0 collective-permute-done.1.source_ref
  13.7 0.0 copy-start
  13.7 0.3 %shard_map.87 = (bf16[384,1024]{1,0:T(8,128)(2,1)S(1)}, bf16[288,768]{1,0:T(8,128)(2,1)S(1)}, bf16[4,256,256]{2,1,0:T(8,128)(2,1)S(1)}, f32[4,8,128]{2,1,0:T(8,128)S(1)}) custom-call(bf16[624,128]{1,0:T(8,128)(2,1)S(1)} %collective-permute-done.1.source_ref, ...), custom_call_target="tpu_custom_call", output_to_operand_aliasing={{0}: (1, {}), {1}: (2, {}), {2}: (3, {}), {3}: (4, {})} | custom-call | tf_op jit(solution)/shard_map/pallas_call | solution.py:802
  14.1 0.9 %collective-permute-done.source_ref = bf16[552,128]{1,0:T(8,128)(2,1)S(1)} collective-permute-done((bf16[552,128]{1,0:T(8,128)(2,1)S(1)}, bf16[552,128]{1,0:T(8,128)(2,1)S(1)}, u32[]{:S(2)}, u32[]{:S(2)}) %collective-permute-start) | collective-permute-done | bytes 141344 | tf_op jit(solution)/shard_map/ppermute | solution.py:31
  15.0 0.0 copy-done
  15.0 1.5 %main.1 = (f32[40,128]{1,0:T(8,128)S(1)}, f32[40,128]{1,0:T(8,128)S(1)}, f32[32,128]{1,0:T(8,128)S(1)}, f32[32,128]{1,0:T(8,128)S(1)}, bf16[384,1024]{1,0:T(8,12...) custom-call(f32[16,128]{1,0:T(8,128)S(1)} %copy-done, ...), custom_call_target="tpu_custom_call", output_to_operand_aliasing={{4}: (2, {}), {5}: (3, {}), {6}: (4, {}), {7}: (5, {})} | custom-call | tf_op jit(solution)/shard_map/main/pallas_call | solution.py:810
  16.5 1.6 %collective-permute-start.5 = (f32[40,128]{1,0:T(8,128)S(1)}, f32[40,128]{1,0:T(8,128)S(1)}, u32[]{:S(2)}, u32[]{:S(2)}) collective-permute-start(f32[40,128]{1,0:T(8,128)S(1)} %get-tuple-element.43), channel_id=1, source_target_pairs={{0,2},{2,0},{1,3},{3,1},{4,6},{6,4},{5,7},{7,5},{8,10},{10,8},{9,1... | collective-permute-start | bytes 61448 | tf_op jit(solution)/shard_map/ppermute | solution.py:31
  18.1 1.7 %collective-permute-start.3 = (f32[32,128]{1,0:T(8,128)S(1)}, f32[32,128]{1,0:T(8,128)S(1)}, u32[]{:S(2)}, u32[]{:S(2)}) collective-permute-start(f32[32,128]{1,0:T(8,128)S(1)} %get-tuple-element.40), channel_id=1, source_target_pairs={{0,12},{2,14},{4,0},{6,2},{8,4},{10,6},{12,8},{14,10},{1,13},{3,15... | collective-permute-start | bytes 49160 | tf_op jit(solution)/shard_map/ppermute | solution.py:31
  19.8 0.4 %collective-permute-start.4 = (f32[32,128]{1,0:T(8,128)S(1)}, f32[32,128]{1,0:T(8,128)S(1)}, u32[]{:S(2)}, u32[]{:S(2)}) collective-permute-start(f32[32,128]{1,0:T(8,128)S(1)} %get-tuple-element.41), channel_id=1, source_target_pairs={{0,14},{2,12},{4,2},{6,0},{8,6},{10,4},{12,10},{14,8},{1,15},{3,13... | collective-permute-start | bytes 49160 | tf_op jit(solution)/shard_map/ppermute | solution.py:31
  20.2 1.6 %collective-permute-done.3 = f32[32,128]{1,0:T(8,128)S(1)} collective-permute-done((f32[32,128]{1,0:T(8,128)S(1)}, f32[32,128]{1,0:T(8,128)S(1)}, u32[]{:S(2)}, u32[]{:S(2)}) %collective-permute-start.3) | collective-permute-done | bytes 16416 | tf_op jit(solution)/shard_map/ppermute | solution.py:31
  21.8 2.6 %collective-permute-done.4 = f32[32,128]{1,0:T(8,128)S(1)} collective-permute-done((f32[32,128]{1,0:T(8,128)S(1)}, f32[32,128]{1,0:T(8,128)S(1)}, u32[]{:S(2)}, u32[]{:S(2)}) %collective-permute-start.4) | collective-permute-done | bytes 16416 | tf_op jit(solution)/shard_map/ppermute | solution.py:31
  24.5 0.0 collective-permute-done.5.rest_1_
  24.5 0.1 collective-permute-start.6
  24.6 1.2 %collective-permute-done.6.other_ref = f32[32,128]{1,0:T(8,128)S(1)} collective-permute-done((f32[32,128]{1,0:T(8,128)S(1)}, f32[32,128]{1,0:T(8,128)S(1)}, u32[]{:S(2)}, u32[]{:S(2)}) %collective-permute-start.6) | collective-permute-done | bytes 16416 | tf_op jit(solution)/shard_map/ppermute | solution.py:31
  25.7 0.7 %final.1 = (f32[16,128]{1,0:T(8,128)}, f32[9,9,32]{2,1,0:T(8,128)}) custom-call(f32[32,128]{1,0:T(8,128)S(1)} %slice_add_fusion.mine_ref, f32[32,128]{1,0:T(8,128)S(1)} %collective-permute-done.6.other_ref, f32[40,128]{1,0:T(8,128)S(1)} %get-tuple-element.42.rest_0_, f32[40,128]{1,0:T(8,128)S(1)} %collective-permute-done.5.rest_1_), custom_call_target="tpu_custom_call" | custom-call | tf_op jit(solution)/shard_map/final/pallas_call | solution.py:839
  (1 shorter events, 0.0 us)
Async XLA Ops:
  1.9 11.8 %collective-permute-start.1 = (bf16[624,128]{1,0:T(8,128)(2,1)S(1)}, bf16[624,128]{1,0:T(8,128)(2,1)S(1)}, u32[]{:S(2)}, u32[]{:S(2)}) collective-permute-start(bf16[624,128]{1,0:T(8,128)(2,1)S(1)} %get-tuple-element.25), channel_id=1, source_target_pairs={{0,2},{2,0},{1,3},{3,1},{4,6},{6,4},{5,7},{7,5},{8,10},{10,8},{9,1... | collective-permute-start | bytes 479240 | tf_op jit(solution)/shard_map/ppermute | solution.py:31
  5.0 8.4 %collective-permute-start.2 = (bf16[552,128]{1,0:T(8,128)(2,1)S(1)}, bf16[552,128]{1,0:T(8,128)(2,1)S(1)}, u32[]{:S(2)}, u32[]{:S(2)}) collective-permute-start(bf16[552,128]{1,0:T(8,128)(2,1)S(1)} %get-tuple-element.26), channel_id=1, source_target_pairs={{0,4},{2,6},{4,8},{6,10},{8,12},{10,14},{12,0},{14,2},{1,5},{3,7},... | collective-permute-start | bytes 423944 | tf_op jit(solution)/shard_map/ppermute | solution.py:31
  6.5 8.5 %collective-permute-start = (bf16[552,128]{1,0:T(8,128)(2,1)S(1)}, bf16[552,128]{1,0:T(8,128)(2,1)S(1)}, u32[]{:S(2)}, u32[]{:S(2)}) collective-permute-start(bf16[552,128]{1,0:T(8,128)(2,1)S(1)} %get-tuple-element.24), channel_id=1, source_target_pairs={{0,6},{2,4},{4,10},{6,8},{8,14},{10,12},{12,2},{14,0},{1,7},{3,5},... | collective-permute-start | bytes 423944 | tf_op jit(solution)/shard_map/ppermute | solution.py:31
  13.7 1.3 %copy-start = (f32[16,128]{1,0:T(8,128)S(1)}, f32[16,128]{1,0:T(8,128)}, u32[]{:S(2)}) copy-start(f32[16,128]{1,0:T(8,128)} %v_ref.1) | copy-start | bytes 24580
  16.5 7.9 %collective-permute-start.5 = (f32[40,128]{1,0:T(8,128)S(1)}, f32[40,128]{1,0:T(8,128)S(1)}, u32[]{:S(2)}, u32[]{:S(2)}) collective-permute-start(f32[40,128]{1,0:T(8,128)S(1)} %get-tuple-element.43), channel_id=1, source_target_pairs={{0,2},{2,0},{1,3},{3,1},{4,6},{6,4},{5,7},{7,5},{8,10},{10,8},{9,1... | collective-permute-start | bytes 61448 | tf_op jit(solution)/shard_map/ppermute | solution.py:31
  18.1 3.7 %collective-permute-start.3 = (f32[32,128]{1,0:T(8,128)S(1)}, f32[32,128]{1,0:T(8,128)S(1)}, u32[]{:S(2)}, u32[]{:S(2)}) collective-permute-start(f32[32,128]{1,0:T(8,128)S(1)} %get-tuple-element.40), channel_id=1, source_target_pairs={{0,12},{2,14},{4,0},{6,2},{8,4},{10,6},{12,8},{14,10},{1,13},{3,15... | collective-permute-start | bytes 49160 | tf_op jit(solution)/shard_map/ppermute | solution.py:31
  19.8 4.6 %collective-permute-start.4 = (f32[32,128]{1,0:T(8,128)S(1)}, f32[32,128]{1,0:T(8,128)S(1)}, u32[]{:S(2)}, u32[]{:S(2)}) collective-permute-start(f32[32,128]{1,0:T(8,128)S(1)} %get-tuple-element.41), channel_id=1, source_target_pairs={{0,14},{2,12},{4,2},{6,0},{8,6},{10,4},{12,10},{14,8},{1,15},{3,13... | collective-permute-start | bytes 49160 | tf_op jit(solution)/shard_map/ppermute | solution.py:31
  24.5 1.2 %collective-permute-start.6 = (f32[32,128]{1,0:T(8,128)S(1)}, f32[32,128]{1,0:T(8,128)S(1)}, u32[]{:S(2)}, u32[]{:S(2)}) collective-permute-start(f32[32,128]{1,0:T(8,128)S(1)} %slice_add_fusion.mine_ref), channel_id=1, source_target_pairs={{0,1},{1,0},{2,3},{3,2},{4,5},{5,4},{6,7},{7,6},{8,9},{9,8},{10,11... | collective-permute-start | bytes 49160 | tf_op jit(solution)/shard_map/ppermute | solution.py:31

commit v5 on v4

v5 whole, which is shorter than its diff:
```python
import functools

import jax
import jax.numpy as jnp
from jax import lax
from jax.experimental import pallas as pl
from jax.experimental.pallas import tpu as pltpu
from jax.sharding import PartitionSpec as P


LANES = 128
F32 = jnp.float32
BF16 = jnp.bfloat16


def moved_by(value, axes, steps):
    sizes = [lax.axis_size(axis) for axis in axes]
    pairs = []
    total = 1
    for size in sizes:
        total *= size
    for source in range(total):
        rest, place = source, []
        for size in reversed(sizes):
            place.insert(0, rest % size)
            rest //= size
        target = 0
        for size, here, step in zip(sizes, place, steps):
            target = target * size + (here + step) % size
        pairs.append((source, target))
    return lax.ppermute(value, axes if len(axes) > 1 else axes[0], pairs)


def round_up(count, unit):
    return (count + unit - 1) // unit * unit


def fixed(value):
    return pltpu.with_memory_space_constraint(value, pltpu.HBM)


def pieces_of(functions, pairs):
    per = LANES // pairs
    full = functions // per * per
    places = {}
    for t in range(full):
        for s in range(functions):
            places[t, s] = (t // per * functions + s, t % per)
    count = full * functions
    for t in range(full, functions):
        for s in range(functions):
            places[t, s] = (count // per, count % per)
            count += 1
    for name in range(3):
        places[name] = (count // per, count % per)
        count += 1
    return places, round_up(-(-count // per), 8)


def plane_masks(atoms, points, slab, ways, repeat, anchor_ref, residues):
    rows = atoms * repeat
    row = lax.broadcasted_iota(jnp.int32, (rows, points), 0)
    offset = jnp.zeros((rows, points), jnp.int32)
    for a in range(atoms):
        here = row == a
        for i in range(1, repeat):
            here = here | (row == a + i * atoms)
        offset = jnp.where(here, lax.rem(anchor_ref[a], slab), offset)
    planes = slab // ways
    found = []
    for residue in residues:
        start = offset - residue
        shift = jnp.zeros((rows, points), jnp.int32)
        for low in range(planes):
            shift = shift + (start > low * ways).astype(jnp.int32)
        phase = (shift * ways - start).astype(F32).astype(BF16)
        bits, size = [], 1
        while size <= planes:
            if size % planes:
                bit = ((shift & size) != 0).astype(F32).astype(BF16)
                bits.append((size, bit > 0.5))
            size *= 2
        level = shift.astype(F32).astype(BF16)
        found.append(
            (
                [phase == float(e) for e in range(ways - 1)],
                bits,
                [level <= float(h) for h in range(planes)],
            )
        )
    return found


def early_of(planes):
    return max(1, planes * 3 // 8)


def pack_kernel(dims, *rest):
    atoms, functions, depth, points, slab, ways, reach, pairs, space = dims
    given, rest = rest[:6], rest[6:]
    own_refs, next_refs, tail_ref = rest[:ways], rest[ways : 2 * ways], rest[2 * ways]
    k_pad, row_pad, *held, x_sem, sems = rest[2 * ways + 1 :]
    early = early_of(slab // ways)
    anchor_ref, x_ref, k_ref, owner_ref, partner_ref, live_ref = held
    block = functions * atoms
    copies = [
        pltpu.make_async_copy(given[i], held[i], sems.at[i]) for i in range(6) if i != 1
    ]
    x_copies = [
        pltpu.make_async_copy(
            given[1].at[s], x_ref.at[:, pl.ds(s * atoms, atoms), :], x_sem.at[s]
        )
        for s in range(functions)
    ]
    copies[0].start()
    for copy in x_copies:
        copy.start()
    for copy in copies[1:]:
        copy.start()
    k_pad[...] = jnp.zeros_like(k_pad)
    row_pad[...] = jnp.zeros_like(row_pad)
    planes = slab // ways
    orb, domain = lax.axis_index("orb"), lax.axis_index("space")
    copies[0].wait()
    residues = [lax.rem(orb + k, ways) for k in range(ways)]
    first = 0
    masks = {}
    while first < functions:
        repeat = min(2, functions - first)
        if repeat not in masks:
            masks[repeat] = plane_masks(atoms, points, slab, ways, repeat, anchor_ref, residues)
        for s in range(first, first + repeat):
            x_copies[s].wait()
        rows = atoms * repeat
        zero = jnp.zeros((rows, points), BF16)
        tiles = [x_ref[j, first * atoms : first * atoms + rows, :] for j in range(depth)]
        tiles = tiles + [zero] * (planes * ways - depth)
        for k in range(ways):
            phases, bits, levels = masks[repeat][k]
            line = []
            for m in range(planes):
                pick = tiles[m * ways + ways - 1]
                for e in reversed(range(ways - 1)):
                    pick = jnp.where(phases[e], tiles[m * ways + e], pick)
                line.append(pick)
            for size, mask in bits:
                line = [jnp.where(mask, line[(h - size) % planes], line[h]) for h in range(planes)]
            for h in range(planes):
                place = h * block + first * atoms
                own_refs[k][place : place + rows, :] = jnp.where(levels[h], line[h], zero)
                if h < reach:
                    out, base = next_refs[k], place
                    if k == ways - 1 and h >= early:
                        out, base = tail_ref, place - early * block
                    out[base : base + rows, :] = jnp.where(levels[h], zero, line[h])
        first += repeat
    for copy in copies[1:]:
        copy.wait()
    places, height = pieces_of(functions, pairs)
    k_pad[0:functions, :functions, :pairs] = k_ref[...]
    per_domain = atoms * ways
    owner = owner_ref[...] - (domain * ways + orb) * atoms
    partner = partner_ref[...]
    home = jnp.floor((partner.astype(F32) + 0.5) * (1.0 / per_domain)).astype(jnp.int32)
    relative = home - domain + 1
    relative = jnp.where(relative < 0, relative + space, relative)
    relative = jnp.where(relative >= space, relative - space, relative)
    code = relative * per_domain + partner - home * per_domain
    k_pad[functions, 0:1, :pairs] = owner.astype(F32)
    k_pad[functions, 1:2, :pairs] = live_ref[...].astype(F32)
    k_pad[functions, 2:3, :pairs] = code.astype(F32)
    lines = {}
    for name, (row, column) in places.items():
        if isinstance(name, tuple):
            piece = k_pad[name[1], name[0] : name[0] + 1, :]
        else:
            piece = k_pad[functions, name : name + 1, :]
        piece = pltpu.roll(piece, column * pairs, 1) if column else piece
        lines[row] = lines[row] + piece if row in lines else piece
    for row, line in lines.items():
        row_pad[row : row + 1, :] = line
    info = row_pad[...]
    high = info.astype(BF16)
    low = (info - high.astype(F32)).astype(BF16)
    for ref in (*own_refs, *next_refs):
        last = ref.shape[0] - 2 * height
        ref[last : last + height, :] = high
        ref[last + height :, :] = low


def spans_of(functions, pairs, band):
    most = 256 // max(band, pairs)
    spans, first = [], 0
    while first < functions:
        count = min(most, functions - first)
        spans.append((first, count, round_up(count * pairs, LANES)))
        first += count
    return spans, (most * band, round_up(most * pairs, LANES))


def lined(rows, place, pairs):
    row, column = place
    line = rows[row : row + 1, :]
    return pltpu.roll(line, LANES - column * pairs, 1) if column else line


def fill_source(dims, c, source_ref, f_ref, d_ref, table_ref, own_ref):
    atoms, functions, _, points, slab, ways, _, pairs, _ = dims
    orb = lax.axis_index("orb")
    planes = slab // ways
    sources = 2 * ways
    block = functions * atoms
    band = sources * atoms
    padded = f_ref.shape[0]
    per = LANES // pairs
    places, height = pieces_of(functions, pairs)
    spans, size = spans_of(functions, pairs, band)
    per_domain = atoms * ways
    contract = (((1,), (1,)), ((), ()))
    last = (source_ref.shape[0] - 2 * height) // block
    for h in range(early_of(planes) if c == 2 * ways - 1 else planes):
        for s in range(functions):
            place = (pl.ds((s * sources + c) * atoms, atoms), pl.ds(h * points, points))
            if h < last:
                f_ref[place] = source_ref[h * block + s * atoms : h * block + (s + 1) * atoms, :]
            else:
                f_ref[place] = jnp.zeros((atoms, points), BF16)
    row_id = lax.broadcasted_iota(jnp.int32, size, 0)
    lane_id = lax.broadcasted_iota(jnp.int32, (1, size[1]), 1)
    function_id = jnp.zeros((1, size[1]), jnp.int32)
    for t in range(1, size[1] // pairs):
        function_id = function_id + (lane_id >= t * pairs).astype(jnp.int32)
    atom_id = lax.broadcasted_iota(jnp.int32, (atoms, LANES), 0)
    pair_high = source_ref[last * block : last * block + height, :].astype(F32)
    pair_low = source_ref[last * block + height : last * block + 2 * height, :].astype(F32)
    row_lane = lax.broadcasted_iota(jnp.int32, (1, LANES), 1)
    wide = []
    for name in range(3):
        row, column = places[name]
        piece = pair_high[row : row + 1, :]
        piece = jnp.where(
            (row_lane >= column * pairs) & (row_lane < (column + 1) * pairs), piece, 0.0
        )
        line = piece
        for i in range(1, per):
            line = line + pltpu.roll(piece, i * pairs, 1)
        wide.append(line)
    owner, live, code = wide[0].astype(jnp.int32), wide[1], wide[2].astype(jnp.int32)
    domain = (code >= per_domain).astype(jnp.int32) + (code >= 2 * per_domain).astype(jnp.int32)
    inside = code - domain * per_domain
    orb_of = jnp.zeros(code.shape, jnp.int32)
    for i in range(1, ways):
        orb_of = orb_of + (inside >= i * atoms).astype(jnp.int32)
    local = inside - orb_of * atoms
    slot = orb - orb_of
    slot = jnp.where(slot < 0, slot + ways, slot)
    if c < ways:
        slot = slot + jnp.where(domain == 0, ways, 0)
        valid = domain <= 1
    else:
        slot = slot + jnp.where(domain == 1, ways, 0)
        valid = domain >= 1
    inner = jnp.where(valid, slot * atoms + local, -padded * LANES)
    inner = jnp.concatenate([inner] * (size[1] // LANES), axis=1)
    target = inner + function_id * band
    table_ref[c] = jnp.where(row_id == target, 1.0, 0.0).astype(BF16)
    own = jnp.where(atom_id == owner, live, 0.0)
    own_ref[c] = own
    for first, count, lanes in spans:
        parts = []
        for pair_rows in (pair_high, pair_low):
            for s in range(functions):
                parts.append(
                    jnp.concatenate(
                        [
                            lined(pair_rows, places[g * per, s], pairs) * own
                            for g in range(first // per, first // per + lanes // LANES)
                        ],
                        axis=1,
                    )
                )
        left = jnp.concatenate(parts, axis=0).astype(BF16)
        cols = count * band
        whole = functions * band // 256 * 256
        if first * band < whole:
            at, next_at = first * band, whole + first * band
        else:
            at = whole + first * band
            next_at = at + functions * band - whole
        part = lax.dot_general(
            left, table_ref[c, :cols, :lanes], contract, preferred_element_type=F32
        )
        part = part[:block] + part[block:]
        high = part.astype(BF16)
        low = (part - high.astype(F32)).astype(BF16)
        for s in range(functions):
            place = pl.ds((s * sources + c) * atoms, atoms)
            d_ref[place, at : at + cols] = high[s * atoms : (s + 1) * atoms]
            d_ref[place, next_at : next_at + cols] = low[s * atoms : (s + 1) * atoms]


def first_kernel(dims, source_ref, f_ref, d_ref, table_ref, own_ref):
    rows, width = d_ref.shape
    if width > 2 * rows:
        edge = 2 * rows // LANES * LANES
        d_ref[:, edge:] = jnp.zeros((rows, width - edge), BF16)
    fill_source(dims, 0, source_ref, f_ref, d_ref, table_ref, own_ref)


def next_kernel(dims, c, source_ref, *rest):
    fill_source(dims, c, source_ref, *rest[4:])


def main_kernel(dims, c, v_ref, tail_ref, d_ref, table_ref, own_ref, *rest):
    atoms, functions, _, points, slab, ways, reach, pairs, _ = dims
    planes = slab // ways
    sources = 2 * ways
    rest = rest[1:]
    own_outs, low_outs = rest[:ways], rest[ways : 2 * ways]
    f_ref, w_ref = rest[2 * ways :]
    block = functions * atoms
    band = sources * atoms
    rows = functions * band
    per = LANES // pairs
    groups = -(-functions // per)
    spans, _ = spans_of(functions, pairs, band)
    orb = lax.axis_index("orb")
    contract = (((1,), (1,)), ((), ()))
    early = early_of(planes)
    for h in range(early, planes):
        for s in range(functions):
            place = (pl.ds((s * sources + c) * atoms, atoms), pl.ds(h * points, points))
            if h < reach:
                at = (h - early) * block + s * atoms
                f_ref[place] = tail_ref[at : at + atoms, :]
            else:
                f_ref[place] = jnp.zeros((atoms, points), BF16)
    whole = rows // 256 * 256
    body, rest_rows = f_ref[:whole, :], f_ref[whole:rows, :]
    stacked = [body, body, rest_rows, rest_rows]
    if d_ref.shape[1] > 2 * rows:
        stacked.append(jnp.zeros((d_ref.shape[1] - 2 * rows, planes * points), BF16))
    aux = jnp.dot(d_ref[...], jnp.concatenate(stacked, axis=0), preferred_element_type=F32)
    density = jnp.sum(aux * f_ref[:rows, :].astype(F32), axis=0, keepdims=True)
    v_ext = jnp.concatenate([v_ref[pl.ds(h * ways + orb, 1), :] for h in range(planes)], axis=1)
    potential = v_ext + density / jnp.sqrt(1.0 + density * density)
    w_ref[...] = (f_ref[:rows, :].astype(F32) * potential).astype(BF16)
    blocks = lax.dot_general(w_ref[...], f_ref[:rows, :], contract, preferred_element_type=F32)
    used = groups * functions
    head = round_up(used, 8)
    for out in (*own_outs, *low_outs):
        out[used:, :] = jnp.zeros((out.shape[0] - used, LANES), F32)
    for c in range(sources):
        own = own_ref[c]
        mine = jnp.concatenate(
            [blocks[(s * sources + c) * atoms : (s * sources + c + 1) * atoms] for s in range(functions)],
            axis=0,
        )
        high = mine.astype(BF16)
        low = (mine - high.astype(F32)).astype(BF16)
        both = jnp.concatenate([high, low], axis=0)
        for first, count, lanes in spans:
            cols = count * band
            spread = jnp.dot(
                both[:, first * band : first * band + cols],
                table_ref[c, :cols, :lanes],
                preferred_element_type=F32,
            )
            spread = spread[:block] + spread[block:]
            owned = jnp.concatenate([own] * (lanes // LANES), axis=1)
            picked = jnp.concatenate(
                [
                    jnp.sum(spread[s * atoms : (s + 1) * atoms] * owned, axis=0, keepdims=True)
                    for s in range(functions)
                ],
                axis=0,
            )
            out = own_outs[c] if c < ways else low_outs[c - ways]
            for i in range(lanes // LANES):
                g = first // per + i
                out[g * functions : (g + 1) * functions, :] = picked[:, i * LANES : (i + 1) * LANES]
        if c < ways:
            for h in range(planes):
                own_outs[c][head + h : head + h + 1, :points] = density[
                    :, h * points : (h + 1) * points
                ]


def final_kernel(dims, mine_ref, other_ref, *rest):
    _, functions, _, points, slab, ways, _, pairs, _ = dims
    planes = slab // ways
    message_refs = rest[:ways]
    density_out, blocks_out, density_ref, blocks_ref, pad_ref, sems = rest[ways:]
    orb = lax.axis_index("orb")
    per = LANES // pairs
    groups = -(-functions // per)
    head = round_up(groups * functions, 8)
    for k in range(ways):
        residue = lax.rem(orb + k, ways)
        for h in range(planes):
            density_ref[pl.ds(h * ways + residue, 1), :] = message_refs[k][
                head + h : head + h + 1, :points
            ]
    first = pltpu.make_async_copy(density_ref, density_out, sems.at[0])
    first.start()
    total = mine_ref[...] + other_ref[...]
    for t in range(functions):
        g, i = t // per, t % per
        piece = total[g * functions : (g + 1) * functions]
        if i:
            piece = pltpu.roll(piece, LANES - i * pairs, 1)
        pad_ref[t] = piece
    for t in range(functions):
        for s in range(functions):
            blocks_ref[s, t : t + 1, :] = pad_ref[t, s : s + 1, :pairs]
    second = pltpu.make_async_copy(blocks_ref, blocks_out, sems.at[1])
    second.start()
    first.wait()
    second.wait()


def on_device(support, anchor, kernel, pair_owner, pair_partner, pair_live, v_ext):
    atoms, functions, depth, points = support.shape
    pairs = kernel.shape[0]
    slab = v_ext.shape[0]
    ways = lax.axis_size("orb")
    space = lax.axis_size("space")
    planes = slab // ways
    reach = min((depth - 2) // ways + 1, planes)
    early = early_of(planes)
    dims = (atoms, functions, depth, points, slab, ways, reach, pairs, space)
    block = functions * atoms
    band = 2 * ways * atoms
    per = LANES // pairs
    groups = -(-functions // per)
    height = pieces_of(functions, pairs)[1]
    vmem = pl.BlockSpec(memory_space=pltpu.VMEM)
    hbm = pl.BlockSpec(memory_space=pltpu.HBM)

    packed = pl.pallas_call(
        functools.partial(pack_kernel, dims),
        out_shape=[jax.ShapeDtypeStruct((planes * block + 2 * height, points), BF16)] * ways
        + [jax.ShapeDtypeStruct((reach * block + 2 * height, points), BF16)] * (ways - 1)
        + [
            jax.ShapeDtypeStruct((early * block + 2 * height, points), BF16),
            jax.ShapeDtypeStruct(((reach - early) * block, points), BF16),
        ],
        in_specs=[hbm] * 6,
        out_specs=[vmem] * (2 * ways + 1),
        scratch_shapes=[
            pltpu.VMEM((functions + 1, 16, LANES), F32),
            pltpu.VMEM((height, LANES), F32),
            pltpu.SMEM((atoms,), jnp.int32),
            pltpu.VMEM((depth, block, points), BF16),
            pltpu.VMEM((functions, functions, pairs), F32),
            pltpu.VMEM((1, pairs), jnp.int32),
            pltpu.VMEM((1, pairs), jnp.int32),
            pltpu.VMEM((1, pairs), jnp.int32),
            pltpu.SemaphoreType.DMA((functions,)),
            pltpu.SemaphoreType.DMA((6,)),
        ],
        compiler_params=pltpu.CompilerParams(vmem_limit_bytes=8 << 20),
        name="pack",
    )(
        fixed(anchor),
        fixed(support.transpose(1, 2, 0, 3)),
        fixed(kernel.transpose(1, 2, 0)),
        fixed(pair_owner.reshape(1, pairs)),
        fixed(pair_partner.reshape(1, pairs)),
        fixed(pair_live.reshape(1, pairs)),
    )
    own, onward, tail = packed[:ways], packed[ways : 2 * ways], packed[2 * ways]
    upper, peers = [], []
    for k in range(ways):
        upper.append(moved_by(onward[k], ("space", "orb"), (1, k)))
    for k in range(1, ways):
        peers.append(moved_by(own[k], ("orb",), (k,)))
    tail = moved_by(tail, ("space", "orb"), (1, ways - 1))
    sources = [own[0]] + peers + upper

    rows = functions * band
    size = spans_of(functions, pairs, band)[1]
    head = round_up(groups * functions, 8)
    order = [0] + [ways] + list(range(1, ways)) + [ways + k for k in range(1, ways)]
    kept = [
        pltpu.VMEM((rows, planes * points), BF16),
        pltpu.VMEM((rows, round_up(2 * rows, LANES)), BF16),
        pltpu.VMEM((2 * ways, *size), BF16),
        pltpu.VMEM((2 * ways, atoms, LANES), F32),
    ]
    held = pl.pallas_call(
        functools.partial(first_kernel, dims),
        out_shape=kept,
        in_specs=[vmem],
        out_specs=[vmem] * 4,
        compiler_params=pltpu.CompilerParams(vmem_limit_bytes=8 << 20),
        name="first",
    )(sources[0])
    for c in order[1:]:
        held = pl.pallas_call(
            functools.partial(next_kernel, dims, c),
            out_shape=kept,
            in_specs=[vmem] + [vmem] * 4,
            out_specs=[vmem] * 4,
            input_output_aliases={1 + i: i for i in range(4)},
            compiler_params=pltpu.CompilerParams(vmem_limit_bytes=8 << 20),
        )(sources[c], *held)
    f_all, d_all, tables, owns = held
    parts = pl.pallas_call(
        functools.partial(main_kernel, dims, order[-1]),
        out_shape=[jax.ShapeDtypeStruct((head + round_up(planes, 8), LANES), F32)] * ways
        + [jax.ShapeDtypeStruct((head, LANES), F32)] * ways
        + kept[:1],
        in_specs=[vmem] * 6,
        out_specs=[vmem] * (2 * ways + 1),
        scratch_shapes=[pltpu.VMEM((rows, planes * points), BF16)],
        input_output_aliases={5: 2 * ways},
        compiler_params=pltpu.CompilerParams(vmem_limit_bytes=20 << 20),
        name="main",
    )(v_ext, tail, d_all, tables, owns, f_all)
    parts = parts[: 2 * ways]

    own_parts, low_parts = parts[:ways], parts[ways:]
    messages, arrived = [own_parts[0]], []
    for k in range(ways):
        arrived.append(moved_by(low_parts[k], ("space", "orb"), (-1, -k)))
    for k in range(1, ways):
        messages.append(moved_by(own_parts[k], ("orb",), (-k,)))
    mine = arrived[0]
    for part in arrived[1:]:
        mine = mine + part
    for message in messages:
        mine = mine + message[:head]
    shares = lax.axis_size("grid")
    other = moved_by(mine, ("grid",), (1,))
    for k in range(2, shares):
        other = other + moved_by(mine, ("grid",), (k,))
    density, blocks = pl.pallas_call(
        functools.partial(final_kernel, dims),
        out_shape=[
            jax.ShapeDtypeStruct((slab, points), F32),
            jax.ShapeDtypeStruct((functions, functions, pairs), F32),
        ],
        in_specs=[vmem] * (2 + ways),
        out_specs=[hbm] * 2,
        scratch_shapes=[
            pltpu.VMEM((slab, points), F32),
            pltpu.VMEM((functions, functions, pairs), F32),
            pltpu.VMEM((functions, functions, LANES), F32),
            pltpu.SemaphoreType.DMA((2,)),
        ],
        compiler_params=pltpu.CompilerParams(vmem_limit_bytes=4 << 20),
        name="final",
    )(mine, other, *messages)
    return (density, blocks.transpose(2, 0, 1))


def solution(mesh):
    placed = (
        P(("shift", "space", "orb"), None, None, "grid"),
        P(("shift", "space", "orb")),
        P(("shift", "space", "orb"), None, None),
        P(("shift", "space", "orb")),
        P(("shift", "space", "orb")),
        P(("shift", "space", "orb")),
        P(("shift", "space"), "grid"),
    )
    return jax.shard_map(
        on_device,
        mesh=mesh,
        in_specs=placed,
        out_specs=(P(("shift", "space"), "grid"), P(("shift", "space", "orb"), None, None)),
        check_vma=False,
    )
```

time: 26.6 us -> 27.1 us (1.019)
  starting transfers between devices: 9.95 us -> 12.4 us
  waiting for transfers between devices: 11.2 us -> 8.81 us
  local copies, waits for them, and re-layouts: 0.01 us -> 0.35 us
    ppermute x7 -> x8, waiting for transfers between devices: 11.2 us -> 8.81 us  [moved_by(): return lax.ppermute(value, axes if len(axes) > 1 else axes[0], pairs)]
    ppermute x7 -> x8, starting transfers between devices: 9.95 us -> 12.4 us  [moved_by(): return lax.ppermute(value, axes if len(axes) > 1 else axes[0], pairs)]
    pallas_call x2 -> x3, Pallas kernels: 0.68 us -> 1.03 us  [on_device(): pl.pallas_call(functools.partial(next_kernel, dims, c), out_shape=kept, i...]
    unnamed x2, local copies, waits for them, and re-layouts: 0.01 us -> 0.35 us
    pallas_call x1, Pallas kernels: 1.51 us -> 1.22 us  [on_device(): pl.pallas_call(functools.partial(main_kernel, dims, order[-1]), out_shape...]
  transfers between devices with their start and end apart: 7 -> 8, of which waited for: 5 -> 5; matrix products, arithmetic and copies ran while one was open for 0% -> 0% of each run, Pallas kernels for 4% -> 5%
where the time goes in v5:
time: 27.1 us; the launch traced here: 26.9 us
  starting transfers between devices  12.4 us (46%)
  waiting for transfers between devices  8.81 us (33%)
  Pallas kernels  4.63 us (17%)
  between operations  0.69 us (3%)
  local copies, waits for them, and re-layouts  0.35 us (1%)
    ppermute x8, starting transfers between devices, moved_by(): return lax.ppermute(value, axes if len(axes) > 1 else axes[0], pairs)  12.4 us
    ppermute x8, waiting for transfers between devices, moved_by(): return lax.ppermute(value, axes if len(axes) > 1 else axes[0], pairs)  8.81 us
    pallas_call x1, Pallas kernels, on_device(): pl.pallas_call(functools.partial(pack_kernel, dims), out_shape=[jax.Shape...  1.3 us
    pallas_call x1, Pallas kernels, on_device(): pl.pallas_call(functools.partial(main_kernel, dims, order[-1]), out_shape...  1.22 us
    pallas_call x3, Pallas kernels, on_device(): pl.pallas_call(functools.partial(next_kernel, dims, c), out_shape=kept, i...  1.03 us
    pallas_call x1, Pallas kernels, on_device(): pl.pallas_call(functools.partial(final_kernel, dims), out_shape=[jax.Shap...  0.73 us
  transfers between devices with their start and end apart: 8, of which 5 were waited for; matrix products, arithmetic and copies ran while one was open for 0% of the time, Pallas kernels for 5%

profile of v5, /device:TPU:0, one launch (start us, length us, event | category | flops | bytes accessed | tf_op | source)
XLA Modules:
  0.0 26.9 jit_solution(11869546104304081586)
XLA Ops:
  0.6 1.3 %pack.1 = (bf16[624,128]{1,0:T(8,128)(2,1)S(1)}, bf16[624,128]{1,0:T(8,128)(2,1)S(1)}, bf16[552,128]{1,0:T(8,128)(2,1)S(1)}, bf16[264,128]{1,0:T(8,128)(2,1)S(1)}, bf16[288,128]{1,0:T(8,128)(2,1)S(1)}) custom-call(s32[8]{0:T(128)} %rest_0_.1, bf16[9,15,8,128]{3,2,1,0:T(8,128)(2,1)} %bitcast.6, f32[9,9,32]{2,1,0:T(8,128)} %bitcast.7, s32[1,32]{1,0:T(1,128)} %bitcast.8, ...), custom_call_target="tpu_custom_call" | custom-call | tf_op jit(solution)/shard_map/pack/pallas_call | solution.py:440
  1.9 3.0 %collective-permute-start.2 = (bf16[624,128]{1,0:T(8,128)(2,1)S(1)}, bf16[624,128]{1,0:T(8,128)(2,1)S(1)}, u32[]{:S(2)}, u32[]{:S(2)}) collective-permute-start(bf16[624,128]{1,0:T(8,128)(2,1)S(1)} %get-tuple-element.31), channel_id=1, source_target_pairs={{0,2},{2,0},{1,3},{3,1},{4,6},{6,4},{5,7},{7,5},{8,10},{10,8},{9,1... | collective-permute-start | bytes 479240 | tf_op jit(solution)/shard_map/ppermute | solution.py:31
  5.0 1.6 %collective-permute-start.3 = (bf16[552,128]{1,0:T(8,128)(2,1)S(1)}, bf16[552,128]{1,0:T(8,128)(2,1)S(1)}, u32[]{:S(2)}, u32[]{:S(2)}) collective-permute-start(bf16[552,128]{1,0:T(8,128)(2,1)S(1)} %get-tuple-element.32), channel_id=1, source_target_pairs={{0,4},{2,6},{4,8},{6,10},{8,12},{10,14},{12,0},{14,2},{1,5},{3,7},... | collective-permute-start | bytes 423944 | tf_op jit(solution)/shard_map/ppermute | solution.py:31
  6.5 1.5 %collective-permute-start = (bf16[288,128]{1,0:T(8,128)(2,1)S(1)}, bf16[288,128]{1,0:T(8,128)(2,1)S(1)}, u32[]{:S(2)}, u32[]{:S(2)}) collective-permute-start(bf16[288,128]{1,0:T(8,128)(2,1)S(1)} %get-tuple-element.29), channel_id=1, source_target_pairs={{0,6},{2,4},{4,10},{6,8},{8,14},{10,12},{12,2},{14,0},{1,7},{3,5},... | collective-permute-start | bytes 221192 | tf_op jit(solution)/shard_map/ppermute | solution.py:31
  8.1 2.5 %collective-permute-start.1 = (bf16[264,128]{1,0:T(8,128)(2,1)S(1)}, bf16[264,128]{1,0:T(8,128)(2,1)S(1)}, u32[]{:S(2)}, u32[]{:S(2)}) collective-permute-start(bf16[264,128]{1,0:T(8,128)(2,1)S(1)} %get-tuple-element.30), channel_id=1, source_target_pairs={{0,6},{2,4},{4,10},{6,8},{8,14},{10,12},{12,2},{14,0},{1,7},{3,5},... | collective-permute-start | bytes 202760 | tf_op jit(solution)/shard_map/ppermute | solution.py:31
  10.6 0.3 %first.1 = (bf16[288,1024]{1,0:T(8,128)(2,1)S(1)}, bf16[288,640]{1,0:T(8,128)(2,1)S(1)}, bf16[4,256,256]{2,1,0:T(8,128)(2,1)S(1)}, f32[4,8,128]{2,1,0:T(8,128)S(1)}) custom-call(bf16[624,128]{1,0:T(8,128)(2,1)S(1)} %get-tuple-element.33.source_ref), custom_call_target="tpu_custom_call" | custom-call | tf_op jit(solution)/shard_map/first/pallas_call | solution.py:491
  10.9 2.2 %collective-permute-done.3.source_ref = bf16[552,128]{1,0:T(8,128)(2,1)S(1)} collective-permute-done((bf16[552,128]{1,0:T(8,128)(2,1)S(1)}, bf16[552,128]{1,0:T(8,128)(2,1)S(1)}, u32[]{:S(2)}, u32[]{:S(2)}) %collective-permute-start.3) | collective-permute-done | bytes 141344 | tf_op jit(solution)/shard_map/ppermute | solution.py:31
  13.2 0.3 %shard_map.86 = (bf16[288,1024]{1,0:T(8,128)(2,1)S(1)}, bf16[288,640]{1,0:T(8,128)(2,1)S(1)}, bf16[4,256,256]{2,1,0:T(8,128)(2,1)S(1)}, f32[4,8,128]{2,1,0:T(8,128)S(1)}) custom-call(bf16[552,128]{1,0:T(8,128)(2,1)S(1)} %collective-permute-done.3.source_ref, ...), custom_call_target="tpu_custom_call", output_to_operand_aliasing={{0}: (1, {}), {1}: (2, {}), {2}: (3, {}), {3}: (4, {})} | custom-call | tf_op jit(solution)/shard_map/pallas_call | solution.py:500
  13.5 0.0 collective-permute-done.2.source_ref
  13.5 0.4 %shard_map.87 = (bf16[288,1024]{1,0:T(8,128)(2,1)S(1)}, bf16[288,640]{1,0:T(8,128)(2,1)S(1)}, bf16[4,256,256]{2,1,0:T(8,128)(2,1)S(1)}, f32[4,8,128]{2,1,0:T(8,128)S(1)}) custom-call(bf16[624,128]{1,0:T(8,128)(2,1)S(1)} %collective-permute-done.2.source_ref, ...), custom_call_target="tpu_custom_call", output_to_operand_aliasing={{0}: (1, {}), {1}: (2, {}), {2}: (3, {}), {3}: (4, {})} | custom-call | tf_op jit(solution)/shard_map/pallas_call | solution.py:500
  13.9 1.2 %collective-permute-done.1.source_ref = bf16[264,128]{1,0:T(8,128)(2,1)S(1)} collective-permute-done((bf16[264,128]{1,0:T(8,128)(2,1)S(1)}, bf16[264,128]{1,0:T(8,128)(2,1)S(1)}, u32[]{:S(2)}, u32[]{:S(2)}) %collective-permute-start.1) | collective-permute-done | bytes 67616 | tf_op jit(solution)/shard_map/ppermute | solution.py:31
  15.1 0.0 copy-start
  15.1 0.3 %shard_map.88 = (bf16[288,1024]{1,0:T(8,128)(2,1)S(1)}, bf16[288,640]{1,0:T(8,128)(2,1)S(1)}, bf16[4,256,256]{2,1,0:T(8,128)(2,1)S(1)}, f32[4,8,128]{2,1,0:T(8,128)S(1)}) custom-call(bf16[264,128]{1,0:T(8,128)(2,1)S(1)} %collective-permute-done.1.source_ref, ...), custom_call_target="tpu_custom_call", output_to_operand_aliasing={{0}: (1, {}), {1}: (2, {}), {2}: (3, {}), {3}: (4, {})} | custom-call | tf_op jit(solution)/shard_map/pallas_call | solution.py:500
  15.4 0.0 collective-permute-done.tail_ref
  15.4 0.3 %copy-done = f32[16,128]{1,0:T(8,128)S(1)} copy-done((f32[16,128]{1,0:T(8,128)S(1)}, f32[16,128]{1,0:T(8,128)}, u32[]{:S(2)}) %copy-start) | copy-done | bytes 8216
  15.8 1.2 %main.1 = (f32[40,128]{1,0:T(8,128)S(1)}, f32[40,128]{1,0:T(8,128)S(1)}, f32[32,128]{1,0:T(8,128)S(1)}, f32[32,128]{1,0:T(8,128)S(1)}, bf16[288,1024]{1,0:T(8,128)(2,1)S(1)}) custom-call(f32[16,128]{1,0:T(8,128)S(1)} %copy-done, bf16[288,128]{1,0:T(8,128)(2,1)S(1)} %collective-permute-done.tail_ref, ...), custom_call_target="tpu_custom_call", output_to_operand_aliasing={{4}: (5, {})} | custom-call | tf_op jit(solution)/shard_map/main/pallas_call | solution.py:509
  17.0 1.6 %collective-permute-start.6 = (f32[40,128]{1,0:T(8,128)S(1)}, f32[40,128]{1,0:T(8,128)S(1)}, u32[]{:S(2)}, u32[]{:S(2)}) collective-permute-start(f32[40,128]{1,0:T(8,128)S(1)} %get-tuple-element.53), channel_id=1, source_target_pairs={{0,2},{2,0},{1,3},{3,1},{4,6},{6,4},{5,7},{7,5},{8,10},{10,8},{9,1... | collective-permute-start | bytes 61448 | tf_op jit(solution)/shard_map/ppermute | solution.py:31
  18.6 1.7 %collective-permute-start.4 = (f32[32,128]{1,0:T(8,128)S(1)}, f32[32,128]{1,0:T(8,128)S(1)}, u32[]{:S(2)}, u32[]{:S(2)}) collective-permute-start(f32[32,128]{1,0:T(8,128)S(1)} %get-tuple-element.50), channel_id=1, source_target_pairs={{0,12},{2,14},{4,0},{6,2},{8,4},{10,6},{12,8},{14,10},{1,13},{3,15... | collective-permute-start | bytes 49160 | tf_op jit(solution)/shard_map/ppermute | solution.py:31
  20.2 0.4 %collective-permute-start.5 = (f32[32,128]{1,0:T(8,128)S(1)}, f32[32,128]{1,0:T(8,128)S(1)}, u32[]{:S(2)}, u32[]{:S(2)}) collective-permute-start(f32[32,128]{1,0:T(8,128)S(1)} %get-tuple-element.51), channel_id=1, source_target_pairs={{0,14},{2,12},{4,2},{6,0},{8,6},{10,4},{12,10},{14,8},{1,15},{3,13... | collective-permute-start | bytes 49160 | tf_op jit(solution)/shard_map/ppermute | solution.py:31
  20.6 1.6 %collective-permute-done.4 = f32[32,128]{1,0:T(8,128)S(1)} collective-permute-done((f32[32,128]{1,0:T(8,128)S(1)}, f32[32,128]{1,0:T(8,128)S(1)}, u32[]{:S(2)}, u32[]{:S(2)}) %collective-permute-start.4) | collective-permute-done | bytes 16416 | tf_op jit(solution)/shard_map/ppermute | solution.py:31
  22.3 2.6 %collective-permute-done.5 = f32[32,128]{1,0:T(8,128)S(1)} collective-permute-done((f32[32,128]{1,0:T(8,128)S(1)}, f32[32,128]{1,0:T(8,128)S(1)}, u32[]{:S(2)}, u32[]{:S(2)}) %collective-permute-start.5) | collective-permute-done | bytes 16416 | tf_op jit(solution)/shard_map/ppermute | solution.py:31
  24.9 0.0 collective-permute-done.6.rest_1_
  24.9 0.1 collective-permute-start.7
  25.0 1.2 %collective-permute-done.7.other_ref = f32[32,128]{1,0:T(8,128)S(1)} collective-permute-done((f32[32,128]{1,0:T(8,128)S(1)}, f32[32,128]{1,0:T(8,128)S(1)}, u32[]{:S(2)}, u32[]{:S(2)}) %collective-permute-start.7) | collective-permute-done | bytes 16416 | tf_op jit(solution)/shard_map/ppermute | solution.py:31
  26.1 0.7 %final.1 = (f32[16,128]{1,0:T(8,128)}, f32[9,9,32]{2,1,0:T(8,128)}) custom-call(f32[32,128]{1,0:T(8,128)S(1)} %slice_add_fusion.mine_ref, f32[32,128]{1,0:T(8,128)S(1)} %collective-permute-done.7.other_ref, f32[40,128]{1,0:T(8,128)S(1)} %get-tuple-element.52.rest_0_, f32[40,128]{1,0:T(8,128)S(1)} %collective-permute-done.6.rest_1_), custom_call_target="tpu_custom_call" | custom-call | tf_op jit(solution)/shard_map/final/pallas_call | solution.py:538
  (1 shorter events, 0.0 us)
Async XLA Ops:
  1.9 11.6 %collective-permute-start.2 = (bf16[624,128]{1,0:T(8,128)(2,1)S(1)}, bf16[624,128]{1,0:T(8,128)(2,1)S(1)}, u32[]{:S(2)}, u32[]{:S(2)}) collective-permute-start(bf16[624,128]{1,0:T(8,128)(2,1)S(1)} %get-tuple-element.31), channel_id=1, source_target_pairs={{0,2},{2,0},{1,3},{3,1},{4,6},{6,4},{5,7},{7,5},{8,10},{10,8},{9,1... | collective-permute-start | bytes 479240 | tf_op jit(solution)/shard_map/ppermute | solution.py:31
  5.0 8.2 %collective-permute-start.3 = (bf16[552,128]{1,0:T(8,128)(2,1)S(1)}, bf16[552,128]{1,0:T(8,128)(2,1)S(1)}, u32[]{:S(2)}, u32[]{:S(2)}) collective-permute-start(bf16[552,128]{1,0:T(8,128)(2,1)S(1)} %get-tuple-element.32), channel_id=1, source_target_pairs={{0,4},{2,6},{4,8},{6,10},{8,12},{10,14},{12,0},{14,2},{1,5},{3,7},... | collective-permute-start | bytes 423944 | tf_op jit(solution)/shard_map/ppermute | solution.py:31
  6.5 8.9 %collective-permute-start = (bf16[288,128]{1,0:T(8,128)(2,1)S(1)}, bf16[288,128]{1,0:T(8,128)(2,1)S(1)}, u32[]{:S(2)}, u32[]{:S(2)}) collective-permute-start(bf16[288,128]{1,0:T(8,128)(2,1)S(1)} %get-tuple-element.29), channel_id=1, source_target_pairs={{0,6},{2,4},{4,10},{6,8},{8,14},{10,12},{12,2},{14,0},{1,7},{3,5},... | collective-permute-start | bytes 221192 | tf_op jit(solution)/shard_map/ppermute | solution.py:31
  8.1 7.0 %collective-permute-start.1 = (bf16[264,128]{1,0:T(8,128)(2,1)S(1)}, bf16[264,128]{1,0:T(8,128)(2,1)S(1)}, u32[]{:S(2)}, u32[]{:S(2)}) collective-permute-start(bf16[264,128]{1,0:T(8,128)(2,1)S(1)} %get-tuple-element.30), channel_id=1, source_target_pairs={{0,6},{2,4},{4,10},{6,8},{8,14},{10,12},{12,2},{14,0},{1,7},{3,5},... | collective-permute-start | bytes 202760 | tf_op jit(solution)/shard_map/ppermute | solution.py:31
  15.1 0.7 %copy-start = (f32[16,128]{1,0:T(8,128)S(1)}, f32[16,128]{1,0:T(8,128)}, u32[]{:S(2)}) copy-start(f32[16,128]{1,0:T(8,128)} %v_ref.1) | copy-start | bytes 24580
  17.0 7.9 %collective-permute-start.6 = (f32[40,128]{1,0:T(8,128)S(1)}, f32[40,128]{1,0:T(8,128)S(1)}, u32[]{:S(2)}, u32[]{:S(2)}) collective-permute-start(f32[40,128]{1,0:T(8,128)S(1)} %get-tuple-element.53), channel_id=1, source_target_pairs={{0,2},{2,0},{1,3},{3,1},{4,6},{6,4},{5,7},{7,5},{8,10},{10,8},{9,1... | collective-permute-start | bytes 61448 | tf_op jit(solution)/shard_map/ppermute | solution.py:31
  18.6 3.7 %collective-permute-start.4 = (f32[32,128]{1,0:T(8,128)S(1)}, f32[32,128]{1,0:T(8,128)S(1)}, u32[]{:S(2)}, u32[]{:S(2)}) collective-permute-start(f32[32,128]{1,0:T(8,128)S(1)} %get-tuple-element.50), channel_id=1, source_target_pairs={{0,12},{2,14},{4,0},{6,2},{8,4},{10,6},{12,8},{14,10},{1,13},{3,15... | collective-permute-start | bytes 49160 | tf_op jit(solution)/shard_map/ppermute | solution.py:31
  20.2 4.6 %collective-permute-start.5 = (f32[32,128]{1,0:T(8,128)S(1)}, f32[32,128]{1,0:T(8,128)S(1)}, u32[]{:S(2)}, u32[]{:S(2)}) collective-permute-start(f32[32,128]{1,0:T(8,128)S(1)} %get-tuple-element.51), channel_id=1, source_target_pairs={{0,14},{2,12},{4,2},{6,0},{8,6},{10,4},{12,10},{14,8},{1,15},{3,13... | collective-permute-start | bytes 49160 | tf_op jit(solution)/shard_map/ppermute | solution.py:31
  24.9 1.2 %collective-permute-start.7 = (f32[32,128]{1,0:T(8,128)S(1)}, f32[32,128]{1,0:T(8,128)S(1)}, u32[]{:S(2)}, u32[]{:S(2)}) collective-permute-start(f32[32,128]{1,0:T(8,128)S(1)} %slice_add_fusion.mine_ref), channel_id=1, source_target_pairs={{0,1},{1,0},{2,3},{3,2},{4,5},{5,4},{6,7},{7,6},{8,9},{9,8},{10,11... | collective-permute-start | bytes 49160 | tf_op jit(solution)/shard_map/ppermute | solution.py:31

commit v6 on v5

--- a/solution.py
+++ b/solution.py
@@ -92,7 +92,7 @@
 
 
 def early_of(planes):
-    return max(1, planes * 3 // 8)
+    return max(1, planes * 2 // 8)
 
 
 def pack_kernel(dims, *rest):
@@ -123,14 +123,20 @@
     orb, domain = lax.axis_index("orb"), lax.axis_index("space")
     copies[0].wait()
     residues = [lax.rem(orb + k, ways) for k in range(ways)]
-    first = 0
+    first, waiting = 0, x_copies + copies[1:]
     masks = {}
     while first < functions:
         repeat = min(2, functions - first)
         if repeat not in masks:
             masks[repeat] = plane_masks(atoms, points, slab, ways, repeat, anchor_ref, residues)
-        for s in range(first, first + repeat):
-            x_copies[s].wait()
+        if first + 4 >= functions:
+            for copy in waiting:
+                copy.wait()
+            waiting = []
+        else:
+            for s in range(first, first + repeat):
+                x_copies[s].wait()
+            waiting = waiting[repeat:]
         rows = atoms * repeat
         zero = jnp.zeros((rows, points), BF16)
         tiles = [x_ref[j, first * atoms : first * atoms + rows, :] for j in range(depth)]
@@ -154,8 +160,6 @@
                         out, base = tail_ref, place - early * block
                     out[base : base + rows, :] = jnp.where(levels[h], zero, line[h])
         first += repeat
-    for copy in copies[1:]:
-        copy.wait()
     places, height = pieces_of(functions, pairs)
     k_pad[0:functions, :functions, :pairs] = k_ref[...]
     per_domain = atoms * ways

time: 27.1 us -> 27 us (level)
  no operation moved by 1% of the time
where the time goes in v6:
time: 27 us; the launch traced here: 26.8 us
  starting transfers between devices  12.5 us (46%)
  waiting for transfers between devices  8.75 us (32%)
  Pallas kernels  4.58 us (17%)
  between operations  0.69 us (3%)
  local copies, waits for them, and re-layouts  0.35 us (1%)
    ppermute x8, starting transfers between devices, moved_by(): return lax.ppermute(value, axes if len(axes) > 1 else axes[0], pairs)  12.5 us
    ppermute x8, waiting for transfers between devices, moved_by(): return lax.ppermute(value, axes if len(axes) > 1 else axes[0], pairs)  8.75 us
    pallas_call x1, Pallas kernels, on_device(): pl.pallas_call(functools.partial(pack_kernel, dims), out_shape=[jax.Shape...  1.24 us
    pallas_call x1, Pallas kernels, on_device(): pl.pallas_call(functools.partial(main_kernel, dims, order[-1]), out_shape...  1.23 us
    pallas_call x3, Pallas kernels, on_device(): pl.pallas_call(functools.partial(next_kernel, dims, c), out_shape=kept, i...  1.03 us
    pallas_call x1, Pallas kernels, on_device(): pl.pallas_call(functools.partial(final_kernel, dims), out_shape=[jax.Shap...  0.73 us
  transfers between devices with their start and end apart: 8, of which 5 were waited for; matrix products, arithmetic and copies ran while one was open for 0% of the time, Pallas kernels for 5%

profile of v6, /device:TPU:0, one launch (start us, length us, event | category | flops | bytes accessed | tf_op | source)
XLA Modules:
  0.0 26.8 jit_solution(661697039966736470)
XLA Ops:
  0.6 1.2 %pack.1 = (bf16[624,128]{1,0:T(8,128)(2,1)S(1)}, bf16[624,128]{1,0:T(8,128)(2,1)S(1)}, bf16[552,128]{1,0:T(8,128)(2,1)S(1)}, bf16[192,128]{1,0:T(8,128)(2,1)S(1)}, bf16[360,128]{1,0:T(8,128)(2,1)S(1)}) custom-call(s32[8]{0:T(128)} %rest_0_.1, bf16[9,15,8,128]{3,2,1,0:T(8,128)(2,1)} %bitcast.6, f32[9,9,32]{2,1,0:T(8,128)} %bitcast.7, s32[1,32]{1,0:T(1,128)} %bitcast.8, ...), custom_call_target="tpu_custom_call" | custom-call | tf_op jit(solution)/shard_map/pack/pallas_call | solution.py:444
  1.9 3.0 %collective-permute-start.2 = (bf16[624,128]{1,0:T(8,128)(2,1)S(1)}, bf16[624,128]{1,0:T(8,128)(2,1)S(1)}, u32[]{:S(2)}, u32[]{:S(2)}) collective-permute-start(bf16[624,128]{1,0:T(8,128)(2,1)S(1)} %get-tuple-element.31), channel_id=1, source_target_pairs={{0,2},{2,0},{1,3},{3,1},{4,6},{6,4},{5,7},{7,5},{8,10},{10,8},{9,1... | collective-permute-start | bytes 479240 | tf_op jit(solution)/shard_map/ppermute | solution.py:31
  4.9 1.6 %collective-permute-start.3 = (bf16[552,128]{1,0:T(8,128)(2,1)S(1)}, bf16[552,128]{1,0:T(8,128)(2,1)S(1)}, u32[]{:S(2)}, u32[]{:S(2)}) collective-permute-start(bf16[552,128]{1,0:T(8,128)(2,1)S(1)} %get-tuple-element.32), channel_id=1, source_target_pairs={{0,4},{2,6},{4,8},{6,10},{8,12},{10,14},{12,0},{14,2},{1,5},{3,7},... | collective-permute-start | bytes 423944 | tf_op jit(solution)/shard_map/ppermute | solution.py:31
  6.5 1.5 %collective-permute-start = (bf16[360,128]{1,0:T(8,128)(2,1)S(1)}, bf16[360,128]{1,0:T(8,128)(2,1)S(1)}, u32[]{:S(2)}, u32[]{:S(2)}) collective-permute-start(bf16[360,128]{1,0:T(8,128)(2,1)S(1)} %get-tuple-element.29), channel_id=1, source_target_pairs={{0,6},{2,4},{4,10},{6,8},{8,14},{10,12},{12,2},{14,0},{1,7},{3,5},... | collective-permute-start | bytes 276488 | tf_op jit(solution)/shard_map/ppermute | solution.py:31
  8.0 2.5 %collective-permute-start.1 = (bf16[192,128]{1,0:T(8,128)(2,1)S(1)}, bf16[192,128]{1,0:T(8,128)(2,1)S(1)}, u32[]{:S(2)}, u32[]{:S(2)}) collective-permute-start(bf16[192,128]{1,0:T(8,128)(2,1)S(1)} %get-tuple-element.30), channel_id=1, source_target_pairs={{0,6},{2,4},{4,10},{6,8},{8,14},{10,12},{12,2},{14,0},{1,7},{3,5},... | collective-permute-start | bytes 147464 | tf_op jit(solution)/shard_map/ppermute | solution.py:31
  10.5 0.3 %first.1 = (bf16[288,1024]{1,0:T(8,128)(2,1)S(1)}, bf16[288,640]{1,0:T(8,128)(2,1)S(1)}, bf16[4,256,256]{2,1,0:T(8,128)(2,1)S(1)}, f32[4,8,128]{2,1,0:T(8,128)S(1)}) custom-call(bf16[624,128]{1,0:T(8,128)(2,1)S(1)} %get-tuple-element.33.source_ref), custom_call_target="tpu_custom_call" | custom-call | tf_op jit(solution)/shard_map/first/pallas_call | solution.py:495
  10.9 2.4 %collective-permute-done.3.source_ref = bf16[552,128]{1,0:T(8,128)(2,1)S(1)} collective-permute-done((bf16[552,128]{1,0:T(8,128)(2,1)S(1)}, bf16[552,128]{1,0:T(8,128)(2,1)S(1)}, u32[]{:S(2)}, u32[]{:S(2)}) %collective-permute-start.3) | collective-permute-done | bytes 141344 | tf_op jit(solution)/shard_map/ppermute | solution.py:31
  13.3 0.3 %shard_map.86 = (bf16[288,1024]{1,0:T(8,128)(2,1)S(1)}, bf16[288,640]{1,0:T(8,128)(2,1)S(1)}, bf16[4,256,256]{2,1,0:T(8,128)(2,1)S(1)}, f32[4,8,128]{2,1,0:T(8,128)S(1)}) custom-call(bf16[552,128]{1,0:T(8,128)(2,1)S(1)} %collective-permute-done.3.source_ref, ...), custom_call_target="tpu_custom_call", output_to_operand_aliasing={{0}: (1, {}), {1}: (2, {}), {2}: (3, {}), {3}: (4, {})} | custom-call | tf_op jit(solution)/shard_map/pallas_call | solution.py:504
  13.6 0.0 collective-permute-done.2.source_ref
  13.7 0.4 %shard_map.87 = (bf16[288,1024]{1,0:T(8,128)(2,1)S(1)}, bf16[288,640]{1,0:T(8,128)(2,1)S(1)}, bf16[4,256,256]{2,1,0:T(8,128)(2,1)S(1)}, f32[4,8,128]{2,1,0:T(8,128)S(1)}) custom-call(bf16[624,128]{1,0:T(8,128)(2,1)S(1)} %collective-permute-done.2.source_ref, ...), custom_call_target="tpu_custom_call", output_to_operand_aliasing={{0}: (1, {}), {1}: (2, {}), {2}: (3, {}), {3}: (4, {})} | custom-call | tf_op jit(solution)/shard_map/pallas_call | solution.py:504
  14.0 0.9 %collective-permute-done.1.source_ref = bf16[192,128]{1,0:T(8,128)(2,1)S(1)} collective-permute-done((bf16[192,128]{1,0:T(8,128)(2,1)S(1)}, bf16[192,128]{1,0:T(8,128)(2,1)S(1)}, u32[]{:S(2)}, u32[]{:S(2)}) %collective-permute-start.1) | collective-permute-done | bytes 49184 | tf_op jit(solution)/shard_map/ppermute | solution.py:31
  14.9 0.0 copy-start
  15.0 0.3 %shard_map.88 = (bf16[288,1024]{1,0:T(8,128)(2,1)S(1)}, bf16[288,640]{1,0:T(8,128)(2,1)S(1)}, bf16[4,256,256]{2,1,0:T(8,128)(2,1)S(1)}, f32[4,8,128]{2,1,0:T(8,128)S(1)}) custom-call(bf16[192,128]{1,0:T(8,128)(2,1)S(1)} %collective-permute-done.1.source_ref, ...), custom_call_target="tpu_custom_call", output_to_operand_aliasing={{0}: (1, {}), {1}: (2, {}), {2}: (3, {}), {3}: (4, {})} | custom-call | tf_op jit(solution)/shard_map/pallas_call | solution.py:504
  15.3 0.0 collective-permute-done.tail_ref
  15.3 0.3 %copy-done = f32[16,128]{1,0:T(8,128)S(1)} copy-done((f32[16,128]{1,0:T(8,128)S(1)}, f32[16,128]{1,0:T(8,128)}, u32[]{:S(2)}) %copy-start) | copy-done | bytes 8216
  15.6 1.2 %main.1 = (f32[40,128]{1,0:T(8,128)S(1)}, f32[40,128]{1,0:T(8,128)S(1)}, f32[32,128]{1,0:T(8,128)S(1)}, f32[32,128]{1,0:T(8,128)S(1)}, bf16[288,1024]{1,0:T(8,128)(2,1)S(1)}) custom-call(f32[16,128]{1,0:T(8,128)S(1)} %copy-done, bf16[360,128]{1,0:T(8,128)(2,1)S(1)} %collective-permute-done.tail_ref, ...), custom_call_target="tpu_custom_call", output_to_operand_aliasing={{4}: (5, {})} | custom-call | tf_op jit(solution)/shard_map/main/pallas_call | solution.py:513
  16.9 1.6 %collective-permute-start.6 = (f32[40,128]{1,0:T(8,128)S(1)}, f32[40,128]{1,0:T(8,128)S(1)}, u32[]{:S(2)}, u32[]{:S(2)}) collective-permute-start(f32[40,128]{1,0:T(8,128)S(1)} %get-tuple-element.53), channel_id=1, source_target_pairs={{0,2},{2,0},{1,3},{3,1},{4,6},{6,4},{5,7},{7,5},{8,10},{10,8},{9,1... | collective-permute-start | bytes 61448 | tf_op jit(solution)/shard_map/ppermute | solution.py:31
  18.4 1.7 %collective-permute-start.4 = (f32[32,128]{1,0:T(8,128)S(1)}, f32[32,128]{1,0:T(8,128)S(1)}, u32[]{:S(2)}, u32[]{:S(2)}) collective-permute-start(f32[32,128]{1,0:T(8,128)S(1)} %get-tuple-element.50), channel_id=1, source_target_pairs={{0,12},{2,14},{4,0},{6,2},{8,4},{10,6},{12,8},{14,10},{1,13},{3,15... | collective-permute-start | bytes 49160 | tf_op jit(solution)/shard_map/ppermute | solution.py:31
  20.2 0.4 %collective-permute-start.5 = (f32[32,128]{1,0:T(8,128)S(1)}, f32[32,128]{1,0:T(8,128)S(1)}, u32[]{:S(2)}, u32[]{:S(2)}) collective-permute-start(f32[32,128]{1,0:T(8,128)S(1)} %get-tuple-element.51), channel_id=1, source_target_pairs={{0,14},{2,12},{4,2},{6,0},{8,6},{10,4},{12,10},{14,8},{1,15},{3,13... | collective-permute-start | bytes 49160 | tf_op jit(solution)/shard_map/ppermute | solution.py:31
  20.6 1.6 %collective-permute-done.4 = f32[32,128]{1,0:T(8,128)S(1)} collective-permute-done((f32[32,128]{1,0:T(8,128)S(1)}, f32[32,128]{1,0:T(8,128)S(1)}, u32[]{:S(2)}, u32[]{:S(2)}) %collective-permute-start.4) | collective-permute-done | bytes 16416 | tf_op jit(solution)/shard_map/ppermute | solution.py:31
  22.2 2.6 %collective-permute-done.5 = f32[32,128]{1,0:T(8,128)S(1)} collective-permute-done((f32[32,128]{1,0:T(8,128)S(1)}, f32[32,128]{1,0:T(8,128)S(1)}, u32[]{:S(2)}, u32[]{:S(2)}) %collective-permute-start.5) | collective-permute-done | bytes 16416 | tf_op jit(solution)/shard_map/ppermute | solution.py:31
  24.8 0.0 collective-permute-done.6.rest_1_
  24.8 0.1 collective-permute-start.7
  24.9 1.2 %collective-permute-done.7.other_ref = f32[32,128]{1,0:T(8,128)S(1)} collective-permute-done((f32[32,128]{1,0:T(8,128)S(1)}, f32[32,128]{1,0:T(8,128)S(1)}, u32[]{:S(2)}, u32[]{:S(2)}) %collective-permute-start.7) | collective-permute-done | bytes 16416 | tf_op jit(solution)/shard_map/ppermute | solution.py:31
  26.1 0.7 %final.1 = (f32[16,128]{1,0:T(8,128)}, f32[9,9,32]{2,1,0:T(8,128)}) custom-call(f32[32,128]{1,0:T(8,128)S(1)} %slice_add_fusion.mine_ref, f32[32,128]{1,0:T(8,128)S(1)} %collective-permute-done.7.other_ref, f32[40,128]{1,0:T(8,128)S(1)} %get-tuple-element.52.rest_0_, f32[40,128]{1,0:T(8,128)S(1)} %collective-permute-done.6.rest_1_), custom_call_target="tpu_custom_call" | custom-call | tf_op jit(solution)/shard_map/final/pallas_call | solution.py:542
  (1 shorter events, 0.0 us)
Async XLA Ops:
  1.9 11.8 %collective-permute-start.2 = (bf16[624,128]{1,0:T(8,128)(2,1)S(1)}, bf16[624,128]{1,0:T(8,128)(2,1)S(1)}, u32[]{:S(2)}, u32[]{:S(2)}) collective-permute-start(bf16[624,128]{1,0:T(8,128)(2,1)S(1)} %get-tuple-element.31), channel_id=1, source_target_pairs={{0,2},{2,0},{1,3},{3,1},{4,6},{6,4},{5,7},{7,5},{8,10},{10,8},{9,1... | collective-permute-start | bytes 479240 | tf_op jit(solution)/shard_map/ppermute | solution.py:31
  4.9 8.4 %collective-permute-start.3 = (bf16[552,128]{1,0:T(8,128)(2,1)S(1)}, bf16[552,128]{1,0:T(8,128)(2,1)S(1)}, u32[]{:S(2)}, u32[]{:S(2)}) collective-permute-start(bf16[552,128]{1,0:T(8,128)(2,1)S(1)} %get-tuple-element.32), channel_id=1, source_target_pairs={{0,4},{2,6},{4,8},{6,10},{8,12},{10,14},{12,0},{14,2},{1,5},{3,7},... | collective-permute-start | bytes 423944 | tf_op jit(solution)/shard_map/ppermute | solution.py:31
  6.5 8.8 %collective-permute-start = (bf16[360,128]{1,0:T(8,128)(2,1)S(1)}, bf16[360,128]{1,0:T(8,128)(2,1)S(1)}, u32[]{:S(2)}, u32[]{:S(2)}) collective-permute-start(bf16[360,128]{1,0:T(8,128)(2,1)S(1)} %get-tuple-element.29), channel_id=1, source_target_pairs={{0,6},{2,4},{4,10},{6,8},{8,14},{10,12},{12,2},{14,0},{1,7},{3,5},... | collective-permute-start | bytes 276488 | tf_op jit(solution)/shard_map/ppermute | solution.py:31
  8.0 6.9 %collective-permute-start.1 = (bf16[192,128]{1,0:T(8,128)(2,1)S(1)}, bf16[192,128]{1,0:T(8,128)(2,1)S(1)}, u32[]{:S(2)}, u32[]{:S(2)}) collective-permute-start(bf16[192,128]{1,0:T(8,128)(2,1)S(1)} %get-tuple-element.30), channel_id=1, source_target_pairs={{0,6},{2,4},{4,10},{6,8},{8,14},{10,12},{12,2},{14,0},{1,7},{3,5},... | collective-permute-start | bytes 147464 | tf_op jit(solution)/shard_map/ppermute | solution.py:31
  14.9 0.7 %copy-start = (f32[16,128]{1,0:T(8,128)S(1)}, f32[16,128]{1,0:T(8,128)}, u32[]{:S(2)}) copy-start(f32[16,128]{1,0:T(8,128)} %v_ref.1) | copy-start | bytes 24580
  16.9 7.9 %collective-permute-start.6 = (f32[40,128]{1,0:T(8,128)S(1)}, f32[40,128]{1,0:T(8,128)S(1)}, u32[]{:S(2)}, u32[]{:S(2)}) collective-permute-start(f32[40,128]{1,0:T(8,128)S(1)} %get-tuple-element.53), channel_id=1, source_target_pairs={{0,2},{2,0},{1,3},{3,1},{4,6},{6,4},{5,7},{7,5},{8,10},{10,8},{9,1... | collective-permute-start | bytes 61448 | tf_op jit(solution)/shard_map/ppermute | solution.py:31
  18.4 3.7 %collective-permute-start.4 = (f32[32,128]{1,0:T(8,128)S(1)}, f32[32,128]{1,0:T(8,128)S(1)}, u32[]{:S(2)}, u32[]{:S(2)}) collective-permute-start(f32[32,128]{1,0:T(8,128)S(1)} %get-tuple-element.50), channel_id=1, source_target_pairs={{0,12},{2,14},{4,0},{6,2},{8,4},{10,6},{12,8},{14,10},{1,13},{3,15... | collective-permute-start | bytes 49160 | tf_op jit(solution)/shard_map/ppermute | solution.py:31
  20.2 4.6 %collective-permute-start.5 = (f32[32,128]{1,0:T(8,128)S(1)}, f32[32,128]{1,0:T(8,128)S(1)}, u32[]{:S(2)}, u32[]{:S(2)}) collective-permute-start(f32[32,128]{1,0:T(8,128)S(1)} %get-tuple-element.51), channel_id=1, source_target_pairs={{0,14},{2,12},{4,2},{6,0},{8,6},{10,4},{12,10},{14,8},{1,15},{3,13... | collective-permute-start | bytes 49160 | tf_op jit(solution)/shard_map/ppermute | solution.py:31
  24.8 1.2 %collective-permute-start.7 = (f32[32,128]{1,0:T(8,128)S(1)}, f32[32,128]{1,0:T(8,128)S(1)}, u32[]{:S(2)}, u32[]{:S(2)}) collective-permute-start(f32[32,128]{1,0:T(8,128)S(1)} %slice_add_fusion.mine_ref), channel_id=1, source_target_pairs={{0,1},{1,0},{2,3},{3,2},{4,5},{5,4},{6,7},{7,6},{8,9},{9,8},{10,11... | collective-permute-start | bytes 49160 | tf_op jit(solution)/shard_map/ppermute | solution.py:31
